TPU v7x, 32 devices: a whole 2x2x4 slice. The times are simulated.
32 devices in a mesh: dp: 4 (over y, x), ctx: 8 (over z, core).
Axes of the slice: x: 2, y: 2, z: 4, core: 2. Of those that a mesh axis runs over, the one named last changes fastest.
Arguments:
- tokens: bfloat16 [8, 512, 2560], P('dp', 'ctx'), may hold values from -6 to 6
- lengths: int32 [8], P('dp'), may hold values from 128 to 512, as said below
- cotangent: bfloat16 [8, 512, 2560], P('dp', 'ctx'), may hold values from -6 to 6
- input_gain: bfloat16 [2560], P(('dp', 'ctx')), may hold values from 0.5 to 1.5
- query_gain: bfloat16 [768], P(('dp', 'ctx')), may hold values from 0.5 to 1.5
- latent_gain: bfloat16 [256], P(('dp', 'ctx')), may hold values from 0.5 to 1.5
- post_gain: bfloat16 [2560], P(('dp', 'ctx')), may hold values from 0.5 to 1.5
- query_down: bfloat16 [2560, 768], P(('dp', 'ctx')), may hold values from -0.125 to 0.125
- query_up: bfloat16 [768, 3840], P(('dp', 'ctx')), may hold values from -0.21875 to 0.21875
- latent_down: bfloat16 [2560, 288], P(('dp', 'ctx')), may hold values from -0.125 to 0.125
- latent_up: bfloat16 [256, 5120], P(('dp', 'ctx')), may hold values from -0.375 to 0.375
- out_proj: bfloat16 [2560, 2560], P(('dp', 'ctx')), may hold values from -6 to 6
- gate_proj: bfloat16 [2560, 6400], P(('dp', 'ctx')), may hold values from -0.125 to 0.125
- up_proj: bfloat16 [2560, 6400], P(('dp', 'ctx')), may hold values from -0.125 to 0.125
- down_proj: bfloat16 [6400, 2560], P(('dp', 'ctx')), may hold values from -0.75 to 0.75
Outputs:
- layer_out: bfloat16 [8, 512, 2560], P('dp', 'ctx')
- input_grad: float32 [8, 512, 2560], P('dp', 'ctx')
- grad_input_gain: float32 [2560], P(('dp', 'ctx'))
- grad_query_gain: float32 [768], P(('dp', 'ctx'))
- grad_latent_gain: float32 [256], P(('dp', 'ctx'))
- grad_post_gain: float32 [2560], P(('dp', 'ctx'))
- grad_query_down: float32 [2560, 768], P(('dp', 'ctx'))
- grad_query_up: float32 [768, 3840], P(('dp', 'ctx'))
- grad_latent_down: float32 [2560, 288], P(('dp', 'ctx'))
- grad_latent_up: float32 [256, 5120], P(('dp', 'ctx'))
- grad_out_proj: float32 [2560, 2560], P(('dp', 'ctx'))
- grad_gate_proj: float32 [2560, 6400], P(('dp', 'ctx'))
- grad_up_proj: float32 [2560, 6400], P(('dp', 'ctx'))
- grad_down_proj: float32 [6400, 2560], P(('dp', 'ctx'))
Inputs may be any that keep to these rules, and one draw needn't show every extreme that they name: `lengths`: positions at or past a slot's length are padding; some slot has all 512 positions valid.
All inputs are finite; a program needn't handle non-finite values.
Results may differ from a plain program's by a relative error of at most 0.018.
Values may be sent and summed in bfloat16 or wider, within the bound.
A program may use at most 640 MiB of HBM per device.

v0:
```python
import jax
import jax.numpy as jnp
from jax import lax
from jax.sharding import PartitionSpec as P

D = 2560
HEADS = 40
QRANK = 768
KVRANK = 256
NOPE = 64
ROPE = 32
VDIM = 64


epsilon = 1e-05
branch_scale = 1.4 / 62**0.5
neg_large = -1e30
bfloat = jnp.bfloat16
single = jnp.float32
highest = lax.Precision.HIGHEST


def normalize(values):
    factor = lax.rsqrt(jnp.mean(values * values, axis=-1, keepdims=True) + epsilon)
    return (values * factor, factor)


def norm_back(grad_scaled, normed, factor):
    return factor * (grad_scaled - normed * jnp.mean(grad_scaled * normed, axis=-1, keepdims=True))


def rotate(values, cosine, sine):
    half_width = values.shape[-1] // 2
    leading = values[..., :half_width]
    trailing = values[..., half_width:]
    return jnp.concatenate(
        [leading * cosine - trailing * sine, trailing * cosine + leading * sine], axis=-1
    )


def unrotate(grads, cosine, sine):
    half_width = grads.shape[-1] // 2
    leading = grads[..., :half_width]
    trailing = grads[..., half_width:]
    return jnp.concatenate(
        [leading * cosine + trailing * sine, trailing * cosine - leading * sine], axis=-1
    )


def dot_plain(left, right):
    return jnp.dot(left, right, preferred_element_type=single)


def dot_rows(left, right):
    return lax.dot_general(left, right, (((1,), (1,)), ((), ())), preferred_element_type=single)


def dot_cols(left, right):
    return lax.dot_general(left, right, (((0,), (0,)), ((), ())), preferred_element_type=single)


def exact_rows(left, right):
    return lax.dot_general(
        left, right, (((1,), (1,)), ((), ())), precision=highest, preferred_element_type=single
    )


def exact_cols(left, right):
    return lax.dot_general(
        left, right, (((0,), (0,)), ((), ())), precision=highest, preferred_element_type=single
    )


def key_blocks(all_kv, all_rope):
    key_total = all_kv.shape[0]
    block_size = min(512, key_total)
    block_count = key_total // block_size
    kv_blocks = all_kv.reshape(block_count, block_size, HEADS, NOPE + VDIM)
    rope_blocks = all_rope.reshape(block_count, block_size, ROPE)
    offsets = jnp.arange(block_count, dtype=jnp.int32) * block_size
    return ((kv_blocks, rope_blocks, offsets), block_size)


def block_scores(query, kv_block, rope_block, offset, query_pos, length, block_size):
    score_scale = 1.0 / (NOPE + ROPE) ** 0.5
    key_pos = offset + jnp.arange(block_size, dtype=jnp.int32)
    logits = jnp.einsum(
        "qhd,khd->hqk", query[:, :, :NOPE], kv_block[:, :, :NOPE], preferred_element_type=single
    )
    logits = logits + jnp.einsum(
        "qhd,kd->hqk", query[:, :, NOPE:], rope_block, preferred_element_type=single
    )
    allowed = (key_pos[None, :] <= query_pos[:, None]) & (key_pos[None, :] < length)
    return (logits * score_scale, allowed[None, :, :])


def attend(query, all_kv, all_rope, query_pos, length):
    items, block_size = key_blocks(all_kv, all_rope)
    span_len = query.shape[0]
    head_count = query.shape[1]

    def stat_step(state, item):
        run_max, run_sum = state
        logits, allowed = block_scores(
            query, item[0], item[1], item[2], query_pos, length, block_size
        )
        masked = jnp.where(allowed, logits, neg_large)
        new_max = jnp.maximum(run_max, jnp.max(masked, axis=-1))
        exponent = jnp.where(allowed, jnp.exp(masked - new_max[:, :, None]), 0.0)
        return ((new_max, run_sum * jnp.exp(run_max - new_max) + jnp.sum(exponent, axis=-1)), None)

    initial = (
        jnp.full((head_count, span_len), neg_large, single),
        jnp.zeros((head_count, span_len), single),
    )
    (run_max, run_sum), unused = lax.scan(stat_step, initial, items)
    log_total = run_max + jnp.log(run_sum)

    def out_step(running, item):
        logits, allowed = block_scores(
            query, item[0], item[1], item[2], query_pos, length, block_size
        )
        probs = jnp.where(allowed, jnp.exp(logits - log_total[:, :, None]), 0.0).astype(bfloat)
        return (
            running
            + jnp.einsum(
                "hqk,khd->qhd", probs, item[0][:, :, NOPE:], preferred_element_type=single
            ),
            None,
        )

    attn_raw, unused = lax.scan(out_step, jnp.zeros((span_len, head_count, VDIM), single), items)
    return (attn_raw, log_total)


def attend_back(query, all_kv, all_rope, query_pos, length, log_total, grad_attn, delta):
    items, block_size = key_blocks(all_kv, all_rope)
    score_scale = 1.0 / (NOPE + ROPE) ** 0.5
    key_total = all_kv.shape[0]

    def grad_step(grad_query, item):
        kv_block, rope_block, offset = item
        logits, allowed = block_scores(
            query, kv_block, rope_block, offset, query_pos, length, block_size
        )
        probs = jnp.where(allowed, jnp.exp(logits - log_total[:, :, None]), 0.0)
        grad_value = jnp.einsum(
            "hqk,qhd->khd", probs.astype(bfloat), grad_attn, preferred_element_type=single
        )
        grad_probs = jnp.einsum(
            "qhd,khd->hqk", grad_attn, kv_block[:, :, NOPE:], preferred_element_type=single
        )
        grad_scores = (probs * (grad_probs - delta[:, :, None])).astype(bfloat)
        grad_query = grad_query + jnp.concatenate(
            [
                jnp.einsum(
                    "hqk,khd->qhd",
                    grad_scores,
                    kv_block[:, :, :NOPE],
                    preferred_element_type=single,
                ),
                jnp.einsum("hqk,kd->qhd", grad_scores, rope_block, preferred_element_type=single),
            ],
            axis=-1,
        )
        grad_key = (
            jnp.einsum(
                "hqk,qhd->khd", grad_scores, query[:, :, :NOPE], preferred_element_type=single
            )
            * score_scale
        )
        grad_rope = (
            jnp.einsum(
                "hqk,qhd->kd", grad_scores, query[:, :, NOPE:], preferred_element_type=single
            )
            * score_scale
        )
        return (grad_query, (jnp.concatenate([grad_key, grad_value], axis=-1), grad_rope))

    initial = jnp.zeros((query.shape[0], query.shape[1], NOPE + ROPE), single)
    grad_query, (grad_kv, grad_rope) = lax.scan(grad_step, initial, items)
    return (
        grad_query * score_scale,
        grad_kv.reshape(key_total, HEADS * (NOPE + VDIM)),
        grad_rope.reshape(key_total, ROPE),
    )


def weight_sums(records):
    joined = tuple((jnp.concatenate(list(group), axis=0) for group in zip(*records)))
    (
        normed_in,
        grad_query_latent,
        grad_latent_all,
        grad_attn_branch,
        attn,
        normed_mid,
        grad_gate,
        grad_up,
        hidden,
        grad_branch,
    ) = joined
    part_query_down, part_latent_down, part_out_proj = (
        lax.psum_scatter(
            dot_cols(normed_in, grad_query_latent), ("dp", "ctx"), scatter_dimension=0, tiled=True
        ),
        lax.psum_scatter(
            dot_cols(normed_in, grad_latent_all), ("dp", "ctx"), scatter_dimension=0, tiled=True
        ),
        lax.psum_scatter(
            dot_cols(grad_attn_branch, attn), ("dp", "ctx"), scatter_dimension=0, tiled=True
        ),
    )
    part_gate, part_up = (
        lax.psum_scatter(
            dot_cols(normed_mid, grad_gate), ("dp", "ctx"), scatter_dimension=0, tiled=True
        ),
        lax.psum_scatter(
            dot_cols(normed_mid, grad_up), ("dp", "ctx"), scatter_dimension=0, tiled=True
        ),
    )
    part_down = lax.psum_scatter(
        dot_cols(hidden, grad_branch), ("dp", "ctx"), scatter_dimension=0, tiled=True
    )
    return (part_query_down, part_latent_down, part_out_proj, part_gate, part_up, part_down)


def on_device(
    tokens,
    lengths,
    cotangent,
    input_gain,
    query_gain,
    latent_gain,
    post_gain,
    query_down,
    query_up,
    latent_down,
    latent_up,
    out_proj,
    gate_proj,
    up_proj,
    down_proj,
):
    batch_count = tokens.shape[0]
    span_len = tokens.shape[1]
    query_pos = lax.axis_index("ctx") * span_len + jnp.arange(span_len, dtype=jnp.int32)
    freqs = 10000.0 ** (-(2.0 * jnp.arange(ROPE // 2, dtype=single)) / ROPE)
    angles = query_pos.astype(single)[:, None] * freqs[None, :]
    cosine = jnp.cos(angles)
    sine = jnp.sin(angles)
    (
        full_input_gain,
        full_query_gain,
        full_latent_gain,
        full_query_down,
        full_query_up,
        full_latent_down,
        full_latent_up,
        full_out_proj,
    ) = (
        lax.all_gather(input_gain, ("dp", "ctx"), axis=0, tiled=True),
        lax.all_gather(query_gain, ("dp", "ctx"), axis=0, tiled=True),
        lax.all_gather(latent_gain, ("dp", "ctx"), axis=0, tiled=True),
        lax.all_gather(query_down, ("dp", "ctx"), axis=0, tiled=True),
        lax.all_gather(query_up, ("dp", "ctx"), axis=0, tiled=True),
        lax.all_gather(latent_down, ("dp", "ctx"), axis=0, tiled=True),
        lax.all_gather(latent_up, ("dp", "ctx"), axis=0, tiled=True),
        lax.all_gather(out_proj, ("dp", "ctx"), axis=0, tiled=True),
    )
    full_post_gain, full_gate, full_up, full_down = (
        lax.all_gather(post_gain, ("dp", "ctx"), axis=0, tiled=True),
        lax.all_gather(gate_proj, ("dp", "ctx"), axis=0, tiled=True),
        lax.all_gather(up_proj, ("dp", "ctx"), axis=0, tiled=True),
        lax.all_gather(down_proj, ("dp", "ctx"), axis=0, tiled=True),
    )
    post_scale = full_post_gain.astype(single)
    latent_up_single = full_latent_up.astype(single)
    sum_input_gain = jnp.zeros((D,), single)
    sum_query_gain = jnp.zeros((QRANK,), single)
    sum_latent_gain = jnp.zeros((KVRANK,), single)
    sum_post_gain = jnp.zeros((D,), single)
    sum_query_up = jnp.zeros((QRANK, HEADS * (NOPE + ROPE)), single)
    sum_latent_up = jnp.zeros((KVRANK, HEADS * (NOPE + VDIM)), single)
    big_totals = None
    records = []
    layer_out = []
    input_grad = []
    for batch_index in range(batch_count):
        inputs = tokens[batch_index].astype(single)
        length = lengths[batch_index]
        normed_first, factor_first = normalize(inputs)
        normed_in = (normed_first * full_input_gain.astype(single)).astype(bfloat)
        query_latent = dot_plain(normed_in, full_query_down)
        normed_query, factor_query = normalize(query_latent)
        query_normed = (normed_query * full_query_gain.astype(single)).astype(bfloat)
        query_full = dot_plain(query_normed, full_query_up).reshape(span_len, HEADS, NOPE + ROPE)
        query_rot = rotate(query_full[:, :, NOPE:], cosine[:, None, :], sine[:, None, :])
        query = jnp.concatenate([query_full[:, :, :NOPE], query_rot], axis=-1).astype(bfloat)
        latent_all = dot_plain(normed_in, full_latent_down)
        normed_latent, factor_latent = normalize(latent_all[:, :KVRANK])
        latent_normed = (normed_latent * full_latent_gain.astype(single)).astype(bfloat)
        key_rope = rotate(latent_all[:, KVRANK:], cosine, sine).astype(bfloat)
        all_latent, all_rope = (
            lax.all_gather(latent_normed, "ctx", axis=0, tiled=True),
            lax.all_gather(key_rope, "ctx", axis=0, tiled=True),
        )
        all_kv = dot_plain(all_latent, full_latent_up).astype(bfloat)
        attn_raw, log_total = attend(query, all_kv, all_rope, query_pos, length)
        attn = attn_raw.astype(bfloat).reshape(span_len, HEADS * VDIM)
        middle = inputs + branch_scale * dot_rows(attn, full_out_proj)
        normed_post, factor_post = normalize(middle)
        normed_mid = (normed_post * post_scale).astype(bfloat)
        gate_act = dot_plain(normed_mid, full_gate)
        up_act = dot_plain(normed_mid, full_up)
        hidden = (jax.nn.silu(gate_act) * up_act).astype(bfloat)
        branch_out = dot_plain(hidden, full_down)
        layer_out.append((middle + branch_scale * branch_out).astype(bfloat))
        grad_out = cotangent[batch_index].astype(single)
        grad_branch = (branch_scale * grad_out).astype(bfloat)
        grad_hidden = dot_rows(grad_branch, full_down)
        sigma = jax.nn.sigmoid(gate_act)
        grad_gate = (grad_hidden * up_act * (sigma * (1.0 + gate_act * (1.0 - sigma)))).astype(
            bfloat
        )
        grad_up = (grad_hidden * (gate_act * sigma)).astype(bfloat)
        grad_normed_mid = dot_rows(grad_gate, full_gate) + dot_rows(grad_up, full_up)
        sum_post_gain = sum_post_gain + jnp.sum(grad_normed_mid * normed_post, axis=0)
        grad_middle = grad_out + norm_back(grad_normed_mid * post_scale, normed_post, factor_post)
        grad_attn_branch = (branch_scale * grad_middle).astype(bfloat)
        grad_attn = (
            dot_plain(grad_attn_branch, full_out_proj).astype(bfloat).reshape(span_len, HEADS, VDIM)
        )
        delta = jnp.sum(grad_attn.astype(single) * attn_raw, axis=-1).T
        grad_query, grad_kv_all, grad_rope_all = attend_back(
            query, all_kv, all_rope, query_pos, length, log_total, grad_attn, delta
        )
        latent_part = exact_rows(grad_kv_all, latent_up_single)
        sum_latent_up = sum_latent_up + exact_cols(all_latent.astype(single), grad_kv_all)
        grad_latent_normed, grad_rope_own = (
            lax.psum_scatter(
                latent_part.astype(jnp.bfloat16), "ctx", scatter_dimension=0, tiled=True
            ).astype(jnp.float32),
            lax.psum_scatter(
                grad_rope_all.astype(jnp.bfloat16), "ctx", scatter_dimension=0, tiled=True
            ).astype(jnp.float32),
        )
        sum_latent_gain = sum_latent_gain + jnp.sum(grad_latent_normed * normed_latent, axis=0)
        grad_latent = norm_back(
            grad_latent_normed * full_latent_gain.astype(single), normed_latent, factor_latent
        )
        grad_latent_all = jnp.concatenate(
            [grad_latent, unrotate(grad_rope_own, cosine, sine)], axis=-1
        ).astype(bfloat)
        grad_query_low = grad_query.astype(bfloat).astype(single)
        grad_query_full = jnp.concatenate(
            [
                grad_query_low[:, :, :NOPE],
                unrotate(grad_query_low[:, :, NOPE:], cosine[:, None, :], sine[:, None, :]),
            ],
            axis=-1,
        )
        grad_query_full = grad_query_full.astype(bfloat).reshape(span_len, HEADS * (NOPE + ROPE))
        grad_query_normed = dot_rows(grad_query_full, full_query_up)
        sum_query_gain = sum_query_gain + jnp.sum(grad_query_normed * normed_query, axis=0)
        grad_query_latent = norm_back(
            grad_query_normed * full_query_gain.astype(single), normed_query, factor_query
        ).astype(bfloat)
        grad_normed_in = dot_rows(grad_query_latent, full_query_down) + dot_rows(
            grad_latent_all, full_latent_down
        )
        sum_input_gain = sum_input_gain + jnp.sum(grad_normed_in * normed_first, axis=0)
        input_grad.append(
            grad_middle
            + norm_back(grad_normed_in * full_input_gain.astype(single), normed_first, factor_first)
        )
        sum_query_up = sum_query_up + dot_cols(query_normed, grad_query_full)
        record = (
            normed_in,
            grad_query_latent,
            grad_latent_all,
            grad_attn_branch,
            attn,
            normed_mid,
            grad_gate,
            grad_up,
            hidden,
            grad_branch,
        )
        records.append(record)
    big_totals = weight_sums(records)
    (
        grad_input_gain,
        grad_query_gain,
        grad_latent_gain,
        grad_post_gain,
        grad_query_up,
        grad_latent_up,
    ) = (
        lax.psum_scatter(sum_input_gain, ("dp", "ctx"), scatter_dimension=0, tiled=True),
        lax.psum_scatter(sum_query_gain, ("dp", "ctx"), scatter_dimension=0, tiled=True),
        lax.psum_scatter(sum_latent_gain, ("dp", "ctx"), scatter_dimension=0, tiled=True),
        lax.psum_scatter(sum_post_gain, ("dp", "ctx"), scatter_dimension=0, tiled=True),
        lax.psum_scatter(sum_query_up, ("dp", "ctx"), scatter_dimension=0, tiled=True),
        lax.psum_scatter(sum_latent_up, ("dp", "ctx"), scatter_dimension=0, tiled=True),
    )
    (
        grad_query_down,
        grad_latent_down,
        grad_out_proj,
        grad_gate_proj,
        grad_up_proj,
        grad_down_proj,
    ) = big_totals
    return (
        jnp.stack(layer_out),
        jnp.stack(input_grad),
        grad_input_gain,
        grad_query_gain,
        grad_latent_gain,
        grad_post_gain,
        grad_query_down,
        grad_query_up,
        grad_latent_down,
        grad_latent_up,
        grad_out_proj,
        grad_gate_proj,
        grad_up_proj,
        grad_down_proj,
    )


def solution(mesh):
    in_specs = (
        P("dp", "ctx", None),
        P("dp"),
        P("dp", "ctx", None),
        P(("dp", "ctx")),
        P(("dp", "ctx")),
        P(("dp", "ctx")),
        P(("dp", "ctx")),
        P(("dp", "ctx"), None),
        P(("dp", "ctx"), None),
        P(("dp", "ctx"), None),
        P(("dp", "ctx"), None),
        P(("dp", "ctx"), None),
        P(("dp", "ctx"), None),
        P(("dp", "ctx"), None),
        P(("dp", "ctx"), None),
    )
    out_specs = (
        P("dp", "ctx", None),
        P("dp", "ctx", None),
        P(("dp", "ctx")),
        P(("dp", "ctx")),
        P(("dp", "ctx")),
        P(("dp", "ctx")),
        P(("dp", "ctx"), None),
        P(("dp", "ctx"), None),
        P(("dp", "ctx"), None),
        P(("dp", "ctx"), None),
        P(("dp", "ctx"), None),
        P(("dp", "ctx"), None),
        P(("dp", "ctx"), None),
        P(("dp", "ctx"), None),
    )
    return jax.shard_map(
        on_device, mesh=mesh, in_specs=in_specs, out_specs=out_specs, check_vma=False
    )
```

profile of v0, /device:TPU:9, one launch (start us, length us, event | category | flops | bytes accessed | tf_op | source)
XLA Modules:
  0.0 4130.9 jit_solution(14989081254797091914)
XLA Ops:
  13.8 40.1 all-reduce.10
  158.5 33.6 all-gather.15.cloned.1.call-done
  196.4 65.8 %all-gather.17.cloned.1.call-done = bf16[768,3840]{1,0:T(8,128)(2,1)} async-done(((bf16[24,3840]{1,0:T(8,128)(2,1)}), bf16[768,3840]{1,0:T(8,128)(2,1)}) %all-gather.17.cloned.1.call-update) | async-done | bytes 5898256 | tf_op jit(solution)/shard_map/all_gather | solution.py:266
  295.9 65.3 %all-gather.19.cloned.1.call-done = bf16[2560,2560]{1,0:T(8,128)(2,1)} async-done(((bf16[80,2560]{1,0:T(8,128)(2,1)}), bf16[2560,2560]{1,0:T(8,128)(2,1)}) %all-gather.19.cloned.1.call-update) | async-done | bytes 13107216 | tf_op jit(solution)/shard_map/all_gather | solution.py:269
  376.3 175.7 %all-gather.21.cloned.1.call-done = bf16[2560,6400]{1,0:T(8,128)(2,1)} async-done(((bf16[80,6400]{1,0:T(8,128)(2,1)}), bf16[2560,6400]{1,0:T(8,128)(2,1)}) %all-gather.21.cloned.1.call-update) | async-done | bytes 32768016 | tf_op jit(solution)/shard_map/all_gather | solution.py:273
  566.5 177.6 %all-gather.23.cloned.1.call-done = bf16[2560,6400]{1,0:T(8,128)(2,1)} async-done(((bf16[80,6400]{1,0:T(8,128)(2,1)}), bf16[2560,6400]{1,0:T(8,128)(2,1)}) %all-gather.23.cloned.1.call-update) | async-done | bytes 32768016 | tf_op jit(solution)/shard_map/all_gather | solution.py:274
  758.7 177.6 %all-gather.25.cloned.1.call-done = bf16[6400,2560]{1,0:T(8,128)(2,1)} async-done(((bf16[200,2560]{1,0:T(8,128)(2,1)}), bf16[6400,2560]{1,0:T(8,128)(2,1)}) %all-gather.25.cloned.1.call-update) | async-done | bytes 32768016 | tf_op jit(solution)/shard_map/all_gather | solution.py:275
  936.3 17.9 multiply_convert_fusion.4
  969.9 16.0 multiply_reduce_fusion.3
  1014.1 17.7 multiply_convert_fusion.2
  1047.5 16.0 multiply_reduce_fusion.2
  1163.4 25.9 reduce-scatter.20.cloned.1.call-done
  1190.6 29.9 reduce-scatter.22.cloned.1.call-done
  1235.9 17.7 convolution_add_fusion.1
  1298.3 23.0 fusion.32
  1322.7 22.8 fusion.28
  1354.9 23.8 fusion.36
  1408.2 45.9 %all-reduce.9 = (f32[2560]{0:T(1024)S(1)}, f32[768]{0:T(1024)S(1)}, f32[256]{0:T(256)S(1)}, f32[2560]{0:T(1024)S(1)}) all-reduce(f32[2560]{0:T(1024)S(1)} %add.335, f32[768]{0:T(1024)S(1)} %add.336, f32[256]{0:T(256)S(1)} %add.337, f32[2560]{0:T(1024)S(1)} %add.338), channel_id=6, replica_groups=mesh['dp'=4,'ctx'=8] {'dp','ctx'}, use_global_device_ids=true, to_apply=%region_28.29.clone | all-reduce | flops 6144 | bytes 49152
  1472.9 133.5 %reduce-scatter.24.cloned.1.call-done = f32[80,768]{1,0:T(8,128)} async-done(((f32[2560,768]{1,0:T(8,128)}), f32[80,768]{1,0:T(8,128)}) %reduce-scatter.24.cloned.1.call-update) | async-done | bytes 245776 | tf_op jit(solution)/shard_map/reduce_scatter | solution.py:204
  1606.4 154.8 %reduce-scatter.26.cloned.1.call-done = f32[24,3840]{1,0:T(8,128)} async-done(((f32[768,3840]{1,0:T(8,128)}), f32[24,3840]{1,0:T(8,128)}) %reduce-scatter.26.cloned.1.call-update) | async-done | bytes 368656 | tf_op jit(solution)/shard_map/reduce_scatter | solution.py:404
  1761.1 285.1 %reduce-scatter.32.cloned.1.call-done = f32[80,2560]{1,0:T(8,128)} async-done(((f32[2560,2560]{1,0:T(8,128)}), f32[80,2560]{1,0:T(8,128)}) %reduce-scatter.32.cloned.1.call-update) | async-done | bytes 819216 | tf_op jit(solution)/shard_map/reduce_scatter | solution.py:210
  2046.2 692.4 %reduce-scatter.36.cloned.1.call-done = f32[80,6400]{1,0:T(8,128)} async-done(((f32[2560,6400]{1,0:T(8,128)}), f32[80,6400]{1,0:T(8,128)}) %reduce-scatter.36.cloned.1.call-update) | async-done | bytes 2048016 | tf_op jit(solution)/shard_map/reduce_scatter | solution.py:218
  2738.6 692.6 %reduce-scatter.34.cloned.1.call-done = f32[80,6400]{1,0:T(8,128)} async-done(((f32[2560,6400]{1,0:T(8,128)}), f32[80,6400]{1,0:T(8,128)}) %reduce-scatter.34.cloned.1.call-update) | async-done | bytes 2048016 | tf_op jit(solution)/shard_map/reduce_scatter | solution.py:215
  3431.3 692.4 %reduce-scatter.42.cloned.1.call-done = f32[200,2560]{1,0:T(8,128)} async-done(((f32[6400,2560]{1,0:T(8,128)}), f32[200,2560]{1,0:T(8,128)}) %reduce-scatter.42.cloned.1.call-update) | async-done | bytes 2048016
  (507 shorter events, 471.1 us)
Async XLA Ops:
  7.2 61.0 %all-gather.11.cloned.1.call-start = ((), (), s32[]{:S(2)}) async-start(), calls=%async_computation.12 | async-start | bytes 2027520 | tf_op jit(solution)/shard_map/all_gather | solution.py:267
  8.0 123.5 %all-gather.13.cloned.1.call-start = ((), (), s32[]{:S(2)}) async-start(), calls=%async_computation.13 | async-start | bytes 2703360 | tf_op jit(solution)/shard_map/all_gather | solution.py:268
  8.7 183.4 %all-gather.15.cloned.1.call-start = ((), (), s32[]{:S(2)}) async-start(), calls=%async_computation.14 | async-start | bytes 4055040 | tf_op jit(solution)/shard_map/all_gather | solution.py:265
  9.5 252.7 %all-gather.17.cloned.1.call-start = ((), (), s32[]{:S(2)}) async-start(), calls=%async_computation.15 | async-start | bytes 6082560 | tf_op jit(solution)/shard_map/all_gather | solution.py:266
  10.0 351.2 %all-gather.19.cloned.1.call-start = ((), (), s32[]{:S(2)}) async-start(), calls=%async_computation.16 | async-start | bytes 13516800 | tf_op jit(solution)/shard_map/all_gather | solution.py:269
  10.6 541.4 %all-gather.21.cloned.1.call-start = ((), (), s32[]{:S(2)}) async-start(), calls=%async_computation.17 | async-start | bytes 33792000 | tf_op jit(solution)/shard_map/all_gather | solution.py:273
  11.2 733.0 %all-gather.23.cloned.1.call-start = ((), (), s32[]{:S(2)}) async-start(), calls=%async_computation.18 | async-start | bytes 33792000 | tf_op jit(solution)/shard_map/all_gather | solution.py:274
  11.9 924.4 %all-gather.25.cloned.1.call-start = ((), (), s32[]{:S(2)}) async-start(), calls=%async_computation.19 | async-start | bytes 33792000 | tf_op jit(solution)/shard_map/all_gather | solution.py:275
  12.7 1146.7 %reduce-scatter.40.cloned.1.call-start = ((), (), s32[]{:S(2)}) async-start(), calls=%async_computation.30 | async-start | bytes 147456
  53.9 1009.5 %copy-start.73 = (f32[2560]{0:T(1024)}, f32[2560]{0:T(1024)S(1)}, u32[]{:S(2)}) copy-start(f32[2560]{0:T(1024)S(1)} %convert_element_type.229) | copy-start | bytes 30724
  370.4 693.0 %copy-start.8 = (f32[64,2560]{1,0:T(8,128)}, f32[64,2560]{1,0:T(8,128)S(1)}, u32[]{:S(2)}) copy-start(f32[64,2560]{1,0:T(8,128)S(1)} %get-tuple-element.281) | copy-start | bytes 1966084
  370.5 693.0 %copy-start.111 = (f32[64]{0:T(128)}, f32[64]{0:T(128)S(1)}, u32[]{:S(2)}) copy-start(f32[64]{0:T(128)S(1)} %add_rsqrt_fusion.4) | copy-start | bytes 772
  376.2 687.3 %copy-start.10 = (f32[64,2560]{1,0:T(8,128)}, f32[64,2560]{1,0:T(8,128)S(1)}, u32[]{:S(2)}) copy-start(f32[64,2560]{1,0:T(8,128)S(1)} %get-tuple-element.283) | copy-start | bytes 1966084
  1104.0 56.2 %reduce-scatter.38.cloned.1.call-start = ((), (), s32[]{:S(2)}) async-start(), calls=%async_computation.29 | async-start | bytes 147456
  1115.7 73.5 %reduce-scatter.20.cloned.1.call-start = ((), (), s32[]{:S(2)}) async-start(), calls=%async_computation.20 | async-start | bytes 294912 | tf_op jit(solution)/shard_map/reduce_scatter | solution.py:341
  1134.9 85.5 %reduce-scatter.22.cloned.1.call-start = ((), (), s32[]{:S(2)}) async-start(), calls=%async_computation.21 | async-start | bytes 294912 | tf_op jit(solution)/shard_map/reduce_scatter | solution.py:341
  1159.4 300.8 %reduce-scatter.28.cloned.1.call-start = ((), (), s32[]{:S(2)}) async-start(), calls=%async_computation.24 | async-start | bytes 4055040 | tf_op jit(solution)/shard_map/reduce_scatter | solution.py:207
  1226.8 246.1 %reduce-scatter.30.cloned.1.call-start = ((), (), s32[]{:S(2)}) async-start(), calls=%async_computation.25 | async-start | bytes 5406720 | tf_op jit(solution)/shard_map/reduce_scatter | solution.py:405
  1253.7 352.7 %reduce-scatter.24.cloned.1.call-start = ((), (), s32[]{:S(2)}) async-start(), calls=%async_computation.22 | async-start | bytes 8110080 | tf_op jit(solution)/shard_map/reduce_scatter | solution.py:204
  1276.0 485.2 %reduce-scatter.26.cloned.1.call-start = ((), (), s32[]{:S(2)}) async-start(), calls=%async_computation.23 | async-start | bytes 12165120 | tf_op jit(solution)/shard_map/reduce_scatter | solution.py:404
  1284.3 762.0 %reduce-scatter.32.cloned.1.call-start = ((), (), s32[]{:S(2)}) async-start(), calls=%async_computation.26 | async-start | bytes 27033600 | tf_op jit(solution)/shard_map/reduce_scatter | solution.py:210
  1296.7 1441.9 %reduce-scatter.36.cloned.1.call-start = ((), (), s32[]{:S(2)}) async-start(), calls=%async_computation.28 | async-start | bytes 67584000 | tf_op jit(solution)/shard_map/reduce_scatter | solution.py:218
  1321.3 2110.0 %reduce-scatter.34.cloned.1.call-start = ((), (), s32[]{:S(2)}) async-start(), calls=%async_computation.27 | async-start | bytes 67584000 | tf_op jit(solution)/shard_map/reduce_scatter | solution.py:215
  1345.6 2778.1 %reduce-scatter.42.cloned.1.call-start = ((), (), s32[]{:S(2)}) async-start(), calls=%async_computation.31 | async-start | bytes 67584000
  (143 other events, 4717.1 us)
Sparse Core Ops, SparseCore 0:
  11.1 57.1 all-gather.10
  71.1 56.8 all-gather.12
  131.0 61.1 all-gather.14
  195.0 67.1 all-gather.16
  264.9 96.2 all-gather.18
  363.9 188.0 all-gather.20
  554.9 189.2 all-gather.22
  747.0 189.2 all-gather.24
  1104.1 23.1 reduce-scatter.39
  1130.1 28.3 reduce-scatter.37
  1160.7 28.4 reduce-scatter.19
  1192.0 28.4 reduce-scatter.21
  1226.9 106.8 reduce-scatter.27
  1336.5 136.3 reduce-scatter.29
  1479.0 127.3 reduce-scatter.23
  1614.0 147.1 reduce-scatter.25
  1763.9 282.2 reduce-scatter.31
  2049.0 689.5 reduce-scatter.35
  2741.7 689.5 reduce-scatter.33
  3434.1 689.5 reduce-scatter.41
where the time goes:
time: 4140 us; the launch traced here: 4130 us
  waiting for transfers between devices  3430 us (83%)
  matrix products  447 us (11%)
  blocking collectives  144 us (3%)
  local copies, waits for them, and re-layouts  50 us (1%)
    unnamed x23, waiting for transfers between devices  698 us
    reduce_scatter x1, waiting for transfers between devices, weight_sums(): lax.psum_scatter(dot_cols(normed_mid, grad_gate), ('dp', 'ctx'), scatter_...  693 us
    reduce_scatter x1, waiting for transfers between devices, weight_sums(): lax.psum_scatter(dot_cols(normed_mid, grad_up), ('dp', 'ctx'), scatter_di...  692 us
    reduce_scatter x1, waiting for transfers between devices, weight_sums(): lax.psum_scatter(dot_cols(grad_attn_branch, attn), ('dp', 'ctx'), scatter...  285 us
    all_gather x1, waiting for transfers between devices, on_device(): lax.all_gather(up_proj, ('dp', 'ctx'), axis=0, tiled=True)  178 us
    all_gather x1, waiting for transfers between devices, on_device(): lax.all_gather(down_proj, ('dp', 'ctx'), axis=0, tiled=True)  178 us
    all_gather x1, waiting for transfers between devices, on_device(): lax.all_gather(gate_proj, ('dp', 'ctx'), axis=0, tiled=True)  176 us
    reduce_scatter x1, waiting for transfers between devices, on_device(): lax.psum_scatter(sum_query_up, ('dp', 'ctx'), scatter_dimension=0, tiled=...  155 us
  transfers between devices with their start and end apart: 20, of which 16 were waited for; matrix products, arithmetic and copies ran while one was open for 9% of the time, Pallas kernels for 0%

commit v1 on v0

v1 whole, which is shorter than its diff:
```python
import functools

import jax
import jax.numpy as jnp
from jax import lax
from jax.experimental import pallas as pl
from jax.experimental.pallas import tpu as pltpu
from jax.sharding import PartitionSpec as P

D = 2560
FF = 6400
HEADS = 40
QRANK = 768
KVRANK = 256
NOPE = 64
ROPE = 32
VDIM = 64

LANES = 128
LATENT = QRANK + KVRANK + LANES

epsilon = 1e-05
branch_scale = 1.4 / 62**0.5
score_scale = 1.0 / (NOPE + ROPE) ** 0.5
neg_large = -1e30
bfloat = jnp.bfloat16
single = jnp.float32
highest = lax.Precision.HIGHEST


def dot(left, right, left_dim=1, right_dim=0, precision=None):
    return lax.dot_general(
        left,
        right,
        (((left_dim,), (right_dim,)), ((), ())),
        precision=precision,
        preferred_element_type=single,
    )


def normalize(values):
    factor = lax.rsqrt(jnp.mean(values * values, axis=-1, keepdims=True) + epsilon)
    return (values * factor, factor)


def norm_back(grad_scaled, normed, factor):
    return factor * (grad_scaled - normed * jnp.mean(grad_scaled * normed, axis=-1, keepdims=True))


def gather_ctx(values):
    return lax.all_gather(values, "ctx", axis=0, tiled=True)


def scatter_ctx(values):
    return lax.psum_scatter(values, "ctx", scatter_dimension=0, tiled=True)


def exchange_ctx(values):
    return lax.all_to_all(values, "ctx", 0, 0, tiled=True)


def gather_dp(values):
    return lax.all_gather(values, "dp", axis=0, tiled=True)


def scatter_dp(values):
    return lax.psum_scatter(values, "dp", scatter_dimension=0, tiled=True)


def rows_of(ref):
    block = ref[...]
    return block.reshape(block.shape[0] * block.shape[2], block.shape[3])


def store_rows(ref, lanes, values):
    ref[:, :, :, lanes] = values.reshape(ref.shape[0], 1, ref.shape[2], values.shape[-1])


def head_lanes(head):
    return pl.ds(head * LANES, LANES)


def valid_pairs(total, length):
    row = lax.broadcasted_iota(jnp.int32, (total, total), 0)
    col = lax.broadcasted_iota(jnp.int32, (total, total), 1)
    return (col <= row) & (col < length)


def attend_kernel(
    heads, length_ref, latent_ref, query_up_ref, latent_up_ref, table_ref,
    query_ref, kv_ref, attn_ref, total_ref,
):
    latent = rows_of(latent_ref)
    total = latent.shape[0]
    query_normed = latent[:, :QRANK]
    latent_normed = latent[:, QRANK : QRANK + KVRANK]
    rope = latent[:, QRANK + KVRANK :]
    allowed = valid_pairs(total, length_ref[pl.program_id(0)])
    lane = lax.broadcasted_iota(jnp.int32, (total, LANES), 1)
    cosine, sine_low, sine_high = table_ref[0], table_ref[1], table_ref[2]
    totals = jnp.zeros((total, LANES), single)
    held = None
    for head in range(heads):
        full = dot(query_normed, query_up_ref[:, head_lanes(head)])
        query = (
            full * cosine
            + pltpu.roll(full, LANES - ROPE // 2, 1) * sine_low
            + pltpu.roll(full, ROPE // 2, 1) * sine_high
        ).astype(bfloat)
        kv = dot(latent_normed, latent_up_ref[:, head_lanes(head)]).astype(bfloat)
        key = jnp.where(lane < NOPE, kv, rope)
        store_rows(query_ref, head_lanes(head), query)
        store_rows(kv_ref, head_lanes(head), kv)
        scores = dot(query, key, 1, 1) * score_scale
        masked = jnp.where(allowed, scores, neg_large)
        top = jnp.max(masked, axis=-1, keepdims=True)
        exponent = jnp.exp(masked - top)
        weight = jnp.sum(exponent, axis=-1, keepdims=True)
        totals = jnp.where(lane == head, top + jnp.log(weight), totals)
        probs = (exponent * (1.0 / weight)).astype(bfloat)
        out = dot(probs, kv)
        if head % 2 == 0:
            held = pltpu.roll(out, VDIM, 1)
            if head == heads - 1:
                store_rows(attn_ref, pl.ds(head * VDIM, VDIM), held[:, :VDIM].astype(bfloat))
        else:
            pair = jnp.where(lane < VDIM, held, out).astype(bfloat)
            store_rows(attn_ref, pl.ds((head - 1) * VDIM, LANES), pair)
    store_rows(total_ref, pl.ds(0, LANES), totals)


def attend_back_kernel(
    heads, length_ref, query_ref, kv_ref, rope_ref, total_ref, grad_attn_ref, table_ref,
    grad_query_ref, grad_kv_ref, grad_rope_ref,
):
    rope = rows_of(rope_ref)
    total = rope.shape[0]
    totals = rows_of(total_ref)
    allowed = valid_pairs(total, length_ref[pl.program_id(0)])
    lane = lax.broadcasted_iota(jnp.int32, (total, LANES), 1)
    cosine, sine_low, sine_high = table_ref[0], table_ref[1], table_ref[2]
    grad_rope = jnp.zeros((total, LANES), single)
    queries, kvs, grads = rows_of(query_ref), rows_of(kv_ref), rows_of(grad_attn_ref)
    for head in range(heads):
        span = slice(head * LANES, (head + 1) * LANES)
        query, kv, grad_attn = queries[:, span], kvs[:, span], grads[:, span]
        key = jnp.where(lane < NOPE, kv, rope)
        scores = dot(query, key, 1, 1) * score_scale
        probs = jnp.where(allowed, jnp.exp(scores - totals[:, head : head + 1]), 0.0)
        grad_probs = dot(grad_attn, kv, 1, 1)
        delta = jnp.sum(probs * grad_probs, axis=-1, keepdims=True)
        grad_scores = (probs * (grad_probs - delta)).astype(bfloat)
        grad_query = (dot(grad_scores, key) * score_scale).astype(bfloat).astype(single)
        grad_full = (
            grad_query * cosine
            - pltpu.roll(grad_query, LANES - ROPE // 2, 1) * sine_low
            - pltpu.roll(grad_query, ROPE // 2, 1) * sine_high
        )
        store_rows(grad_query_ref, head_lanes(head), grad_full.astype(bfloat))
        grad_key = dot(grad_scores, query, 0, 0) * score_scale
        grad_value = dot(probs.astype(bfloat), grad_attn, 0, 0)
        store_rows(grad_kv_ref, head_lanes(head), jnp.where(lane < NOPE, grad_key, grad_value))
        grad_rope = grad_rope + jnp.where(lane < NOPE, 0.0, grad_key)
    store_rows(grad_rope_ref, pl.ds(0, LANES), grad_rope)


def slot_spec(ctx, span, width, block=0):
    return pl.BlockSpec((ctx, 1, span, width), lambda b: (0, b, 0, block))


def whole_spec(shape):
    return pl.BlockSpec(shape, lambda b: (0,) * len(shape))


def attend(lengths, latent, query_up, latent_up, table, heads):
    ctx, batch, span, _ = latent.shape
    wide = heads * LANES
    shapes = [
        ((ctx, batch, span, wide), bfloat),
        ((ctx, batch, span, wide), bfloat),
        ((ctx, batch, span, heads * VDIM), bfloat),
        ((ctx, batch, span, LANES), single),
    ]
    return pl.pallas_call(
        functools.partial(attend_kernel, heads),
        grid=(batch,),
        out_shape=[jax.ShapeDtypeStruct(*item) for item in shapes],
        in_specs=[
            pl.BlockSpec(memory_space=pltpu.SMEM),
            slot_spec(ctx, span, LATENT),
            whole_spec(query_up.shape),
            whole_spec(latent_up.shape),
            whole_spec(table.shape),
        ],
        out_specs=[slot_spec(ctx, span, item[0][-1]) for item in shapes],
        compiler_params=pltpu.CompilerParams(vmem_limit_bytes=56 << 20),
        name="attend",
    )(lengths, latent, query_up, latent_up, table)


def attend_back(lengths, query, kv, latent, totals, grad_attn, table, heads):
    ctx, batch, span, _ = latent.shape
    wide = heads * LANES
    shapes = [
        ((ctx, batch, span, wide), bfloat),
        ((ctx, batch, span, wide), single),
        ((ctx, batch, span, LANES), single),
    ]
    return pl.pallas_call(
        functools.partial(attend_back_kernel, heads),
        grid=(batch,),
        out_shape=[jax.ShapeDtypeStruct(*item) for item in shapes],
        in_specs=[
            pl.BlockSpec(memory_space=pltpu.SMEM),
            slot_spec(ctx, span, wide),
            slot_spec(ctx, span, wide),
            slot_spec(ctx, span, LANES, (QRANK + KVRANK) // LANES),
            slot_spec(ctx, span, LANES),
            slot_spec(ctx, span, wide),
            whole_spec(table.shape),
        ],
        out_specs=[slot_spec(ctx, span, item[0][-1]) for item in shapes],
        compiler_params=pltpu.CompilerParams(vmem_limit_bytes=56 << 20),
        name="attend_back",
    )(lengths, query, kv, latent, totals, grad_attn, table)


def angles_at(positions):
    freqs = 10000.0 ** (-(2.0 * jnp.arange(ROPE // 2, dtype=single)) / ROPE)
    angles = positions.astype(single)[:, None] * freqs[None, :]
    return (jnp.cos(angles), jnp.sin(angles))


def head_table(total):
    cosine, sine = angles_at(jnp.arange(total, dtype=jnp.int32))
    ones, none = jnp.ones((total, NOPE), single), jnp.zeros((total, NOPE), single)
    tail = jnp.zeros((total, LANES - NOPE - ROPE), single)
    zero = jnp.zeros_like(sine)
    return jnp.stack(
        [
            jnp.concatenate([ones, cosine, cosine, tail], axis=-1),
            jnp.concatenate([none, -sine, zero, tail], axis=-1),
            jnp.concatenate([none, zero, sine, tail], axis=-1),
        ]
    )


def pad_rope(values):
    return jnp.pad(values, ((0, 0), (NOPE, LANES - NOPE - ROPE)))


def on_device(
    dp,
    ctx,
    tokens,
    lengths,
    cotangent,
    input_gain,
    query_gain,
    latent_gain,
    post_gain,
    query_down,
    query_up,
    latent_down,
    latent_up,
    out_proj,
    gate_proj,
    up_proj,
    down_proj,
):
    batch, span, _ = tokens.shape
    own = batch * span
    group = ctx * own
    heads = -(-HEADS // ctx)
    spare = heads * ctx - HEADS
    d_rows, q_rows, l_rows, f_rows = (
        query_down.shape[0], query_up.shape[0], latent_up.shape[0], down_proj.shape[0],
    )
    d_part, f_part = dp * d_rows, dp * f_rows
    place = lax.axis_index("ctx")

    def slices(values):
        return values.reshape(own, dp, ctx, d_rows).transpose(2, 0, 1, 3).reshape(ctx, own, d_part)

    def unslices(values):
        return values.reshape(ctx, own, dp, d_rows).transpose(1, 2, 0, 3).reshape(own, D)

    def columns(values):
        split = values.reshape(d_rows, dp, ctx, f_rows).transpose(2, 0, 1, 3)
        return exchange_ctx(split.reshape(ctx, d_rows, f_part)).reshape(ctx * d_rows, f_part)

    gains = lax.all_gather(
        jnp.concatenate([input_gain, query_gain, latent_gain, post_gain]), ("dp", "ctx"), axis=0
    ).astype(single)
    cuts = (d_rows, d_rows + q_rows, d_rows + q_rows + l_rows)
    gain_in = gains[:, : cuts[0]].reshape(dp, ctx, d_rows)
    gain_in = lax.dynamic_index_in_dim(gain_in, place, 1, keepdims=False).reshape(1, d_part)
    gain_query = gains[:, cuts[0] : cuts[1]].reshape(1, QRANK)
    gain_latent = gains[:, cuts[1] : cuts[2]].reshape(1, KVRANK)
    gain_post = gains[:, cuts[2] :].reshape(1, D)

    down_rows = gather_dp(jnp.concatenate([query_down, latent_down[:, :KVRANK], pad_rope(latent_down[:, KVRANK:])], axis=1))
    up_query = query_up.reshape(q_rows, HEADS, NOPE + ROPE)
    up_query = jnp.pad(up_query, ((0, 0), (0, spare), (0, LANES - NOPE - ROPE)))
    up_latent = jnp.pad(latent_up.reshape(l_rows, HEADS, NOPE + VDIM), ((0, 0), (0, spare), (0, 0)))
    ups = jnp.concatenate([up_query, up_latent], axis=0)
    ups = ups.reshape(q_rows + l_rows, ctx, heads * LANES).transpose(1, 0, 2)
    ups = gather_dp(exchange_ctx(ups)).reshape(dp * ctx, q_rows + l_rows, heads * LANES)
    query_ups = ups[:, :q_rows].reshape(QRANK, heads * LANES)
    latent_ups = ups[:, q_rows:].reshape(KVRANK, heads * LANES)
    out_padded = jnp.pad(out_proj, ((0, 0), (0, spare * VDIM)))
    out_rows = gather_dp(out_padded)
    gate = gather_dp(columns(gate_proj))
    up = gather_dp(columns(up_proj))
    down = gather_dp(down_proj)
    out_heads = out_padded.reshape(d_rows, ctx, heads * VDIM).transpose(1, 0, 2)
    out_heads = gather_dp(exchange_ctx(out_heads).reshape(ctx * d_rows, heads * VDIM))
    out_heads = jnp.pad(out_heads.reshape(D, heads, VDIM), ((0, 0), (0, 0), (NOPE, 0)))
    out_heads = out_heads.reshape(D, heads * LANES)

    flat = tokens.reshape(own, D)
    inputs = flat.astype(single)
    normed_first, factor_first = normalize(inputs)
    factor_all = lax.all_gather(factor_first, "ctx", axis=0, tiled=True)
    token_slices = exchange_ctx(slices(flat)).reshape(group, d_part).astype(single)
    normed_slices = token_slices * factor_all
    normed_in = (normed_slices * gain_in).astype(bfloat)
    latents = scatter_ctx(dot(normed_in, down_rows).astype(bfloat)).astype(single)
    normed_query, factor_query = normalize(latents[:, :QRANK])
    query_normed = (normed_query * gain_query).astype(bfloat)
    normed_latent, factor_latent = normalize(latents[:, QRANK : QRANK + KVRANK])
    latent_normed = (normed_latent * gain_latent).astype(bfloat)
    cosine, sine = angles_at(place * span + jnp.arange(span, dtype=jnp.int32))
    cosine, sine = jnp.tile(cosine, (batch, 1)), jnp.tile(sine, (batch, 1))
    half = QRANK + KVRANK + NOPE + ROPE // 2
    leading, trailing = latents[:, half - ROPE // 2 : half], latents[:, half : half + ROPE // 2]
    key_rope = jnp.concatenate(
        [leading * cosine - trailing * sine, trailing * cosine + leading * sine], axis=-1
    ).astype(bfloat)
    latent_own = jnp.concatenate([query_normed, latent_normed, pad_rope(key_rope)], axis=-1)
    latent_all = gather_ctx(latent_own)

    table = head_table(ctx * span)
    latent_slots = latent_all.reshape(ctx, batch, span, LATENT)
    query, kv, attn, totals = attend(lengths, latent_slots, query_ups, latent_ups, table, heads)
    attn_all = gather_ctx(attn.reshape(1, group, heads * VDIM))
    attn_all = attn_all.transpose(1, 0, 2).reshape(group, ctx * heads * VDIM)
    branch = exchange_ctx(dot(attn_all, out_rows, 1, 1).astype(bfloat).reshape(ctx, own, d_part))
    middle = inputs + branch_scale * unslices(branch).astype(single)
    normed_post, factor_post = normalize(middle)
    normed_mid = gather_ctx((normed_post * gain_post).astype(bfloat))

    grad_out = cotangent.reshape(own, D).astype(single)
    grad_branch = gather_ctx((branch_scale * grad_out).astype(bfloat))
    gate_act = dot(normed_mid, gate)
    up_act = dot(normed_mid, up)
    sigma = jax.nn.sigmoid(gate_act)
    hidden = (gate_act * sigma * up_act).astype(bfloat)
    branch_out = scatter_ctx(dot(hidden, down).astype(bfloat)).astype(single)
    layer_out = (middle + branch_scale * branch_out).astype(bfloat)
    grad_hidden = dot(grad_branch, down, 1, 1)
    grad_gate = (grad_hidden * up_act * (sigma * (1.0 + gate_act * (1.0 - sigma)))).astype(bfloat)
    grad_up = (grad_hidden * (gate_act * sigma)).astype(bfloat)
    grad_normed_mid = dot(grad_gate, gate, 1, 1) + dot(grad_up, up, 1, 1)
    grad_normed_mid = scatter_ctx(grad_normed_mid.astype(bfloat)).astype(single)
    grad_middle = grad_out + norm_back(grad_normed_mid * gain_post, normed_post, factor_post)
    grad_attn_branch = gather_ctx((branch_scale * grad_middle).astype(bfloat))

    grad_attn = dot(grad_attn_branch, out_heads).astype(bfloat)
    grad_query, grad_kv, grad_rope = attend_back(
        lengths, query, kv, latent_slots, totals,
        grad_attn.reshape(ctx, batch, span, heads * LANES), table, heads,
    )
    grad_query = grad_query.reshape(group, heads * LANES)
    grad_kv = grad_kv.reshape(group, heads * LANES)
    grad_latents = jnp.concatenate(
        [
            dot(grad_query, query_ups, 1, 1),
            dot(grad_kv, latent_ups.astype(single), 1, 1, highest),
            grad_rope.reshape(group, LANES),
        ],
        axis=-1,
    )
    grad_latents = scatter_ctx(grad_latents.astype(bfloat)).astype(single)
    grad_query_normed = grad_latents[:, :QRANK]
    grad_latent_normed = grad_latents[:, QRANK : QRANK + KVRANK]
    leading, trailing = (
        grad_latents[:, half - ROPE // 2 : half], grad_latents[:, half : half + ROPE // 2],
    )
    grad_key_rope = jnp.concatenate(
        [leading * cosine + trailing * sine, trailing * cosine - leading * sine], axis=-1
    )
    grad_down = jnp.concatenate(
        [
            norm_back(grad_query_normed * gain_query, normed_query, factor_query),
            norm_back(grad_latent_normed * gain_latent, normed_latent, factor_latent),
            pad_rope(grad_key_rope),
        ],
        axis=-1,
    ).astype(bfloat)
    grad_down = gather_ctx(grad_down)
    grad_normed_in = dot(grad_down, down_rows, 1, 1)
    grad_scaled = exchange_ctx((grad_normed_in * gain_in).astype(bfloat).reshape(ctx, own, d_part))
    input_grad = grad_middle + norm_back(
        unslices(grad_scaled).astype(single), normed_first, factor_first
    )

    grad_down_proj = scatter_dp(dot(hidden, grad_branch, 0, 0).astype(bfloat)).astype(single)

    def owners(values):
        summed = scatter_dp(values.astype(bfloat)).reshape(ctx, d_rows, f_part)
        split = exchange_ctx(summed).reshape(ctx, d_rows, dp, f_rows).transpose(1, 2, 0, 3)
        return split.reshape(d_rows, FF).astype(single)

    grad_gate_proj = owners(dot(normed_mid, grad_gate, 0, 0))
    grad_up_proj = owners(dot(normed_mid, grad_up, 0, 0))
    row = lax.broadcasted_iota(jnp.int32, (D, d_part), 0)
    col = lax.broadcasted_iota(jnp.int32, (D, d_part), 1)
    chosen = (row == (col // d_rows) * (ctx * d_rows) + place * d_rows + col % d_rows).astype(bfloat)
    branch_slices = dot(grad_attn_branch, chosen).astype(bfloat)
    grad_out_proj = dot(branch_slices, attn_all[:, : HEADS * VDIM], 0, 0)
    grad_out_proj = scatter_dp(grad_out_proj.astype(bfloat)).astype(single)
    grad_query_ups = dot(latent_all[:, :QRANK], grad_query, 0, 0)
    grad_latent_ups = dot(
        latent_all[:, QRANK : QRANK + KVRANK].astype(single), grad_kv, 0, 0, highest
    )
    grad_ups = jnp.concatenate(
        [
            grad_query_ups.reshape(dp * ctx, q_rows, heads * LANES),
            grad_latent_ups.reshape(dp * ctx, l_rows, heads * LANES),
        ],
        axis=1,
    )
    grad_ups = exchange_ctx(scatter_dp(grad_ups.astype(bfloat))).transpose(1, 0, 2)
    grad_ups = grad_ups.reshape(q_rows + l_rows, ctx * heads, LANES)[:, :HEADS].astype(single)
    grad_query_up = grad_ups[:q_rows, :, : NOPE + ROPE].reshape(q_rows, HEADS * (NOPE + ROPE))
    grad_latent_up = grad_ups[q_rows:].reshape(l_rows, HEADS * (NOPE + VDIM))

    gain_sums = jnp.concatenate(
        [
            jnp.sum(grad_normed_mid * normed_post, axis=0).reshape(dp * ctx, d_rows),
            jnp.sum(grad_query_normed * normed_query, axis=0).reshape(dp * ctx, q_rows),
            jnp.sum(grad_latent_normed * normed_latent, axis=0).reshape(dp * ctx, l_rows),
        ],
        axis=1,
    )
    gain_sums = lax.psum_scatter(gain_sums, ("dp", "ctx"), scatter_dimension=0, tiled=True)[0]
    grad_rows = dot(normed_in, grad_down, 0, 0)
    last = jnp.sum(grad_normed_in * normed_slices, axis=0)[:, None]
    grad_rows = jnp.concatenate([grad_rows[:, : LATENT - 1], last], axis=1)
    grad_rows = scatter_dp(grad_rows)
    rope_start = QRANK + KVRANK + NOPE
    return (
        layer_out.reshape(batch, span, D),
        input_grad.reshape(batch, span, D),
        grad_rows[:, LATENT - 1],
        gain_sums[d_rows : d_rows + q_rows],
        gain_sums[d_rows + q_rows :],
        gain_sums[:d_rows],
        grad_rows[:, :QRANK],
        grad_query_up,
        jnp.concatenate(
            [grad_rows[:, QRANK : QRANK + KVRANK], grad_rows[:, rope_start : rope_start + ROPE]], axis=1
        ),
        grad_latent_up,
        grad_out_proj,
        grad_gate_proj,
        grad_up_proj,
        grad_down_proj,
    )


def solution(mesh):
    both = ("dp", "ctx")
    tokens, vector, matrix = P("dp", "ctx", None), P(both), P(both, None)
    return jax.shard_map(
        functools.partial(on_device, mesh.shape["dp"], mesh.shape["ctx"]),
        mesh=mesh,
        in_specs=(tokens, P("dp"), tokens) + (vector,) * 4 + (matrix,) * 8,
        out_specs=(tokens, tokens) + (vector,) * 4 + (matrix,) * 8,
        check_vma=False,
    )
```

time: 4140 us -> 1210 us (0.29)
  waiting for transfers between devices: 3430 us -> 550 us
  matrix products: 447 us -> 129 us
  blocking collectives: 144 us -> 284 us
  local copies, waits for them, and re-layouts: 50 us -> 128 us
    reduce_scatter x9 -> x8, waiting for transfers between devices: 2030 us -> 140 us  [the longest x4 76.1 us: scatter_ctx(): return lax.psum_scatter(values, 'ctx', scatter_dimension=0, tiled=True)]
    unnamed x23 -> x24, waiting for transfers between devices: 698 us -> 107 us
    all_gather x8 -> x12, waiting for transfers between devices: 708 us -> 270 us  [the longest x6 172 us: gather_ctx(): return lax.all_gather(values, 'ctx', axis=0, tiled=True)]
    dot_general x60 -> x19, matrix products: 447 us -> 129 us  [dot(): lax.dot_general(left, right, (((left_dim,), (right_dim,)), ((), ())), pre...]
    all_to_all x0 -> x5, blocking collectives: none -> 182 us  [exchange_ctx(): return lax.all_to_all(values, 'ctx', 0, 0, tiled=True)]
  transfers between devices with their start and end apart: 20 -> 27, of which waited for: 16 -> 18; matrix products, arithmetic and copies ran while one was open for 9% -> 19% of each run, Pallas kernels for 0% -> 1%
where the time goes in v1:
time: 1210 us; the launch traced here: 1200 us
  waiting for transfers between devices  550 us (45%)
  blocking collectives  284 us (23%)
  matrix products  129 us (11%)
  local copies, waits for them, and re-layouts  128 us (11%)
  other arithmetic  36.8 us (3%)
  starting transfers between devices  33 us (3%)
  Pallas kernels  26.4 us (2%)
  between operations  17.6 us (1%)
    all_to_all x5, blocking collectives, exchange_ctx(): return lax.all_to_all(values, 'ctx', 0, 0, tiled=True)  182 us
    all_gather x6, waiting for transfers between devices, gather_ctx(): return lax.all_gather(values, 'ctx', axis=0, tiled=True)  172 us
    dot_general x19, matrix products, dot(): lax.dot_general(left, right, (((left_dim,), (right_dim,)), ((), ())), pre...  129 us
    unnamed x24, waiting for transfers between devices  107 us
    all_gather x6, waiting for transfers between devices, gather_dp(): return lax.all_gather(values, 'dp', axis=0, tiled=True)  98 us
    unnamed x2, blocking collectives  79.9 us
    reduce_scatter x4, waiting for transfers between devices, scatter_ctx(): return lax.psum_scatter(values, 'ctx', scatter_dimension=0, tiled=True)  76.1 us
    reduce_scatter x4, waiting for transfers between devices, scatter_dp(): return lax.psum_scatter(values, 'dp', scatter_dimension=0, tiled=True)  64.4 us
  transfers between devices with their start and end apart: 27, of which 18 were waited for; matrix products, arithmetic and copies ran while one was open for 19% of the time, Pallas kernels for 1%

profile of v1, /device:TPU:9, one launch (start us, length us, event | category | flops | bytes accessed | tf_op | source)
XLA Modules:
  0.0 1203.4 jit_solution(15198878497425139187)
XLA Ops:
  18.9 39.3 %all-reduce.5 = bf16[6144]{0:T(1024)(128)(2,1)S(1)} all-reduce(bf16[6144]{0:T(1024)(128)(2,1)S(1)} %dynamic-update-slice), channel_id=2, replica_groups=mesh['dp'=4,'ctx'=8] {'dp','ctx'}, use_global_device_ids=true, to_apply=%add.5 | all-reduce | flops 6144 | bytes 24576
  85.0 20.4 %all_to_all.50 = bf16[8,32,640]{2,1,0:T(8,128)(2,1)} all-to-all(bf16[8,32,640]{2,1,0:T(8,128)(2,1)S(1)} %copy.157), channel_id=1, replica_groups=mesh['dp'=4,'ctx'=8] {'ctx'}, dimensions={0} | all-to-all | bytes 655360 | tf_op jit(solution)/shard_map/all_to_all | solution.py:59
  106.0 17.5 %reduce-scatter.16.cloned.1.call-done = bf16[128,1152]{1,0:T(8,128)(2,1)} async-done(((bf16[1024,1152]{1,0:T(8,128)(2,1)}), bf16[128,1152]{1,0:T(8,128)(2,1)}) %reduce-scatter.16.cloned.1.call-update) | async-done | bytes 294928 | tf_op jit(solution)/shard_map/reduce_scatter | solution.py:55
  137.7 29.7 %all-gather.14.cloned.1.call-done = bf16[1024,1152]{1,0:T(8,128)(2,1)} async-done(((bf16[128,1152]{1,0:T(8,128)(2,1)}), bf16[1024,1152]{1,0:T(8,128)(2,1)}) %all-gather.14.cloned.1.call-update) | async-done | bytes 2359312 | tf_op jit(solution)/shard_map/all_gather | solution.py:51
  167.4 12.9 %attend.1 = (bf16[8,2,64,640]{3,2,1,0:T(8,128)(2,1)}, bf16[8,2,64,640]{3,2,1,0:T(8,128)(2,1)}, bf16[8,2,64,320]{3,2,1,0:T(8,128)(2,1)}, f32[8,2,64,128]{3,2,1,0:T(8,128)}) custom-call(s32[2]{0:T(128)} %length_ref.3, bf16[8,2,64,1152]{3,2,1,0:T(8,128)(2,1)} %bitcast.208, bf16[768,640]{1,0:T(8,128)(2,1)} %bitcast.224, ...), custom_call_target="tpu_custom_call" | custom-call | tf_op jit(solution)/shard_map/attend/pallas_call | solution.py:184
  191.1 50.8 %all_to_all.51 = bf16[8,80,800]{2,1,0:T(8,128)(2,1)} all-to-all(bf16[8,80,800]{2,1,0:T(8,128)(2,1)} %reshape.369), channel_id=1, replica_groups=mesh['dp'=4,'ctx'=8] {'ctx'}, dimensions={0} | all-to-all | bytes 2048000 | tf_op jit(solution)/shard_map/all_to_all | solution.py:59
  242.0 21.3 %all-gather.18.cloned.1.call-done = bf16[8,1024,320]{1,2,0:T(8,128)(2,1)} async-done(((bf16[1,1024,320]{1,2,0:T(8,128)(2,1)}), bf16[8,1024,320]{1,2,0:T(8,128)(2,1)}) %all-gather.18.cloned.1.call-update) | async-done | bytes 5242896 | tf_op jit(solution)/shard_map/all_gather | solution.py:51
  277.9 14.4 %all-to-all-done.2 = bf16[8,128,320]{1,2,0:T(8,128)(2,1)S(1)} async-done(((bf16[8,128,320]{1,2,0:T(8,128)(2,1)}), bf16[8,128,320]{1,2,0:T(8,128)(2,1)S(1)}, u32[]{:S(2)}, u32[]{:S(2)}) %all-to-all-start.2) | async-done | bytes 655392 | tf_op jit(solution)/shard_map/all_to_all | solution.py:59
  313.8 54.6 %all_to_all.52 = bf16[8,80,800]{2,1,0:T(8,128)(2,1)} all-to-all(bf16[8,80,800]{2,1,0:T(8,128)(2,1)} %reshape.372), channel_id=1, replica_groups=mesh['dp'=4,'ctx'=8] {'ctx'}, dimensions={0} | all-to-all | bytes 2048000 | tf_op jit(solution)/shard_map/all_to_all | solution.py:59
  370.5 18.1 %all-gather.22.cloned.1.call-done = bf16[1024,2560]{1,0:T(8,128)(2,1)} async-done(((bf16[128,2560]{1,0:T(8,128)(2,1)}), bf16[1024,2560]{1,0:T(8,128)(2,1)}) %all-gather.22.cloned.1.call-update) | async-done | bytes 5242896 | tf_op jit(solution)/shard_map/all_gather | solution.py:51
  398.7 50.7 %all-gather.26.cloned.1.call-done = bf16[2560,800]{1,0:T(8,128)(2,1)} async-done(((bf16[640,800]{1,0:T(8,128)(2,1)}), bf16[2560,800]{1,0:T(8,128)(2,1)}) %all-gather.26.cloned.1.call-update) | async-done | bytes 4096016 | tf_op jit(solution)/shard_map/all_gather | solution.py:63
  459.3 43.5 %all-gather.28.cloned.1.call-done = bf16[800,2560]{1,0:T(8,128)(2,1)} async-done(((bf16[200,2560]{1,0:T(8,128)(2,1)}), bf16[800,2560]{1,0:T(8,128)(2,1)}) %all-gather.28.cloned.1.call-update) | async-done | bytes 4096016 | tf_op jit(solution)/shard_map/all_gather | solution.py:63
  502.8 56.9 %all-gather.30.cloned.1.call-done = bf16[1024,2560]{1,0:T(8,128)(2,1)} async-done(((bf16[128,2560]{1,0:T(8,128)(2,1)}), bf16[1024,2560]{1,0:T(8,128)(2,1)}) %all-gather.30.cloned.1.call-update) | async-done | bytes 5242896 | tf_op jit(solution)/shard_map/all_gather | solution.py:51
  591.9 24.3 %all_to_all.53 = bf16[8,80,320]{2,1,0:T(8,128)(2,1)} all-to-all(bf16[8,80,320]{2,1,0:T(8,128)(2,1)S(1)} %bitcast.229), channel_id=1, replica_groups=mesh['dp'=4,'ctx'=8] {'ctx'}, dimensions={0} | all-to-all | bytes 819200 | tf_op jit(solution)/shard_map/all_to_all | solution.py:59
  616.3 41.7 %reduce-scatter.20.cloned.1.call-done = bf16[128,2560]{1,0:T(8,128)(2,1)} async-done(((bf16[1024,2560]{1,0:T(8,128)(2,1)}), bf16[128,2560]{1,0:T(8,128)(2,1)}) %reduce-scatter.20.cloned.1.call-update) | async-done | bytes 655376 | tf_op jit(solution)/shard_map/reduce_scatter | solution.py:55
  668.9 45.6 %all-gather.32.cloned.1.call-done = bf16[1024,2560]{1,0:T(8,128)(2,1)} async-done(((bf16[128,2560]{1,0:T(8,128)(2,1)}), bf16[1024,2560]{1,0:T(8,128)(2,1)}) %all-gather.32.cloned.1.call-update) | async-done | bytes 5242896 | tf_op jit(solution)/shard_map/all_gather | solution.py:51
  723.3 13.5 %attend_back.1 = (bf16[8,2,64,640]{3,2,1,0:T(8,128)(2,1)}, f32[8,2,64,640]{3,2,1,0:T(8,128)}, f32[8,2,64,128]{3,2,1,0:T(8,128)}) custom-call(s32[2]{0:T(128)} %length_ref.3, bf16[8,2,64,640]{3,2,1,0:T(8,128)(2,1)} %get-tuple-element.22.query_ref, bf16[8,2,64,640]{3,2,1,0:T(8,128)(2,1)} %get-tuple-element.23.kv_ref, bf16[8,2,64,1152]{3,2,1,0:T(8,128)(2,1)} %bitcast.209, ...), custom_call_target="tpu_custom_call" | custom-call | tf_op jit(solution)/shard_map/attend_back/pallas_call | solution.py:209
  844.8 53.5 %reduce-scatter.30.cloned.1.call-done = bf16[640,800]{1,0:T(8,128)(2,1)} async-done(((bf16[2560,800]{1,0:T(8,128)(2,1)}), bf16[640,800]{1,0:T(8,128)(2,1)}) %reduce-scatter.30.cloned.1.call-update) | async-done | bytes 1024016 | tf_op jit(solution)/shard_map/reduce_scatter | solution.py:67
  898.3 32.1 %all_to_all.54 = bf16[8,80,800]{2,1,0:T(8,128)(2,1)} all-to-all(bf16[8,80,800]{2,1,0:T(8,128)(2,1)} %bitcast.234), channel_id=1, replica_groups=mesh['dp'=4,'ctx'=8] {'ctx'}, dimensions={0} | all-to-all | bytes 2048000 | tf_op jit(solution)/shard_map/all_to_all | solution.py:59
  938.0 47.9 %reduce-scatter.32.cloned.1.call-done = bf16[200,2560]{1,0:T(8,128)(2,1)} async-done(((bf16[800,2560]{1,0:T(8,128)(2,1)}), bf16[200,2560]{1,0:T(8,128)(2,1)}) %reduce-scatter.32.cloned.1.call-update) | async-done | bytes 1024016
  1023.1 40.5 %all-reduce.7 = f32[32,112]{1,0:T(8,128)S(1)} all-reduce(f32[32,112]{1,0:T(8,128)S(1)} %pad_maximum_fusion.5), channel_id=8, replica_groups=mesh['dp'=4,'ctx'=8] {'dp','ctx'}, use_global_device_ids=true, to_apply=%region_17.18.clone | all-reduce | flops 3584 | bytes 28672
  1079.3 18.5 %all-to-all-done.6 = bf16[8,128,320]{1,2,0:T(8,128)(2,1)} async-done(((bf16[8,128,320]{1,2,0:T(8,128)(2,1)}), bf16[8,128,320]{1,2,0:T(8,128)(2,1)}, u32[]{:S(2)}, u32[]{:S(2)}) %all-to-all-start.6) | async-done | bytes 655392 | tf_op jit(solution)/shard_map/all_to_all | solution.py:59
  1111.7 16.9 %reduce-scatter.18.cloned.1.call-done = bf16[128,2560]{1,0:T(8,128)(2,1)} async-done(((bf16[1024,2560]{1,0:T(8,128)(2,1)}), bf16[128,2560]{1,0:T(8,128)(2,1)}) %reduce-scatter.18.cloned.1.call-update) | async-done | bytes 655376 | tf_op jit(solution)/shard_map/reduce_scatter | solution.py:55
  1132.5 57.4 %all-reduce.11.cloned.1.call-done = f32[320,1152]{1,0:T(8,128)} async-done(((f32[320,1152]{1,0:T(8,128)}), f32[320,1152]{1,0:T(8,128)}) %all-reduce.11.cloned.1.call-update) | async-done | bytes 1474576
  (288 shorter events, 363.8 us)
Async XLA Ops:
  12.1 68.1 %all-to-all-start = ((bf16[8,128,320]{1,2,0:T(8,128)(2,1)}), bf16[8,128,320]{1,2,0:T(8,128)(2,1)S(1)}, u32[]{:S(2)}, u32[]{:S(2)}) async-start(bf16[8,128,320]{1,2,0:T(8,128)(2,1)} %bitcast.2), calls=%async_computation | async-start | bytes 1310720 | tf_op jit(solution)/shard_map/all_to_all | solution.py:59
  17.8 105.8 %reduce-scatter.16.cloned.1.call-start = ((), (), s32[]{:S(2)}) async-start(), calls=%async_computation.19 | async-start | bytes 2654208 | tf_op jit(solution)/shard_map/reduce_scatter | solution.py:55
  105.4 61.9 %all-gather.14.cloned.1.call-start = ((), (), s32[]{:S(2)}) async-start(), calls=%async_computation.20 | async-start | bytes 2654208 | tf_op jit(solution)/shard_map/all_gather | solution.py:51
  126.2 115.8 %all-gather.20.cloned.1.call-start = ((), (), s32[]{:S(2)}) async-start(), calls=%async_computation.23 | async-start | bytes 2048000 | tf_op jit(solution)/shard_map/all_gather | solution.py:63
  126.8 136.5 %all-gather.18.cloned.1.call-start = ((), (), s32[]{:S(2)}) async-start(), calls=%async_computation.22 | async-start | bytes 5898240 | tf_op jit(solution)/shard_map/all_gather | solution.py:51
  182.7 187.9 %all-gather.24.cloned.1.call-start = ((), (), s32[]{:S(2)}) async-start(), calls=%async_computation.25 | async-start | bytes 5734400 | tf_op jit(solution)/shard_map/all_gather | solution.py:63
  277.7 111.0 %all-gather.22.cloned.1.call-start = ((), (), s32[]{:S(2)}) async-start(), calls=%async_computation.24 | async-start | bytes 5898240 | tf_op jit(solution)/shard_map/all_gather | solution.py:51
  301.3 148.0 %all-gather.26.cloned.1.call-start = ((), (), s32[]{:S(2)}) async-start(), calls=%async_computation.26 | async-start | bytes 5734400 | tf_op jit(solution)/shard_map/all_gather | solution.py:63
  368.4 134.4 %all-gather.28.cloned.1.call-start = ((), (), s32[]{:S(2)}) async-start(), calls=%async_computation.27 | async-start | bytes 5120000 | tf_op jit(solution)/shard_map/all_gather | solution.py:63
  369.0 190.7 %all-gather.30.cloned.1.call-start = ((), (), s32[]{:S(2)}) async-start(), calls=%async_computation.29 | async-start | bytes 5898240 | tf_op jit(solution)/shard_map/all_gather | solution.py:51
  370.5 287.5 %reduce-scatter.20.cloned.1.call-start = ((), (), s32[]{:S(2)}) async-start(), calls=%async_computation.30 | async-start | bytes 5898240 | tf_op jit(solution)/shard_map/reduce_scatter | solution.py:55
  588.6 73.0 %all-gather.34.cloned.1.call-start = ((), (), s32[]{:S(2)}) async-start(), calls=%async_computation.32 | async-start | bytes 2457600 | tf_op jit(solution)/shard_map/all_gather | solution.py:63
  616.2 98.3 %all-gather.32.cloned.1.call-start = ((), (), s32[]{:S(2)}) async-start(), calls=%async_computation.31 | async-start | bytes 5898240 | tf_op jit(solution)/shard_map/all_gather | solution.py:51
  661.1 151.7 %reduce-scatter.22.cloned.1.call-start = ((), (), s32[]{:S(2)}) async-start(), calls=%async_computation.33 | async-start | bytes 2654208 | tf_op jit(solution)/shard_map/reduce_scatter | solution.py:55
  744.8 94.5 %reduce-scatter.28.cloned.1.call-start = ((), (), s32[]{:S(2)}) async-start(), calls=%async_computation.37 | async-start | bytes 5734400 | tf_op jit(solution)/shard_map/reduce_scatter | solution.py:67
  761.7 136.6 %reduce-scatter.30.cloned.1.call-start = ((), (), s32[]{:S(2)}) async-start(), calls=%async_computation.38 | async-start | bytes 5734400 | tf_op jit(solution)/shard_map/reduce_scatter | solution.py:67
  778.4 152.6 %reduce-scatter.24.cloned.1.call-start = ((), (), s32[]{:S(2)}) async-start(), calls=%async_computation.35 | async-start | bytes 1638400 | tf_op jit(solution)/shard_map/reduce_scatter | solution.py:67
  793.8 192.1 %reduce-scatter.32.cloned.1.call-start = ((), (), s32[]{:S(2)}) async-start(), calls=%async_computation.40 | async-start | bytes 5120000
  803.3 217.6 %reduce-scatter.26.cloned.1.call-start = ((), (), s32[]{:S(2)}) async-start(), calls=%async_computation.36 | async-start | bytes 2048000 | tf_op jit(solution)/shard_map/reduce_scatter | solution.py:67
  812.8 251.0 %all-gather.36.cloned.1.call-start = ((), (), s32[]{:S(2)}) async-start(), calls=%async_computation.34 | async-start | bytes 2654208 | tf_op jit(solution)/shard_map/all_gather | solution.py:51
  819.5 309.2 %reduce-scatter.18.cloned.1.call-start = ((), (), s32[]{:S(2)}) async-start(), calls=%async_computation.28 | async-start | bytes 5898240 | tf_op jit(solution)/shard_map/reduce_scatter | solution.py:55
  839.4 58.9 %all-to-all-start.8 = ((bf16[8,80,800]{2,1,0:T(8,128)(2,1)}), bf16[8,80,800]{2,1,0:T(8,128)(2,1)}, u32[]{:S(2)}, u32[]{:S(2)}) async-start(bf16[8,80,800]{2,1,0:T(8,128)(2,1)} %bitcast.233), calls=%async_computation.14 | async-start | bytes 2293760 | tf_op jit(solution)/shard_map/all_to_all | solution.py:59
  931.0 84.0 %all-to-all-start.7 = ((bf16[8,32,640]{2,1,0:T(8,128)(2,1)}), bf16[8,32,640]{2,1,0:T(8,128)(2,1)S(1)}, u32[]{:S(2)}, u32[]{:S(2)}) async-start(bf16[8,32,640]{2,1,0:T(8,128)(2,1)} %reduce-scatter.24.cloned.1.call-done), calls=%async_computation.12 | async-start | bytes 655360 | tf_op jit(solution)/shard_map/all_to_all | solution.py:59
  1073.0 116.9 %all-reduce.11.cloned.1.call-start = ((), (), s32[]{:S(2)}) async-start(), calls=%async_computation.39 | async-start | bytes 2949120
  (35 other events, 707.9 us)
Sparse Core Ops, SparseCore 0:
  83.5 40.0 reduce-scatter.15
  588.7 69.2 reduce-scatter.19
  745.0 31.7 reduce-scatter.21
  779.7 59.6 reduce-scatter.27
  842.3 55.9 reduce-scatter.29
  901.6 29.2 reduce-scatter.23
  934.1 51.8 reduce-scatter.31
  989.0 31.3 reduce-scatter.25
  1022.0 32.4 all-gather.35
  1056.7 71.8 reduce-scatter.17
  1131.8 58.0 all-reduce.10
Sparse Core Ops, SparseCore 1:
  105.5 28.1 all-gather.15
  135.7 31.6 all-gather.13
  169.1 30.3 all-gather.19
  201.7 61.5 all-gather.17
  265.2 58.8 all-gather.23
  326.2 62.4 all-gather.21
  390.4 58.9 all-gather.25
  451.1 51.7 all-gather.27
  504.9 54.7 all-gather.29
  616.3 35.6 all-gather.33
  661.2 53.3 all-gather.31

commit v2 on v1

v2 whole, which is shorter than its diff:
```python
import functools

import jax
import jax.numpy as jnp
from jax import lax
from jax.experimental import pallas as pl
from jax.experimental.pallas import tpu as pltpu
from jax.sharding import PartitionSpec as P

D = 2560
FF = 6400
HEADS = 40
QRANK = 768
KVRANK = 256
NOPE = 64
ROPE = 32
VDIM = 64

LANES = 128
LATENT = QRANK + KVRANK + LANES

epsilon = 1e-05
branch_scale = 1.4 / 62**0.5
score_scale = 1.0 / (NOPE + ROPE) ** 0.5
neg_large = -1e30
bfloat = jnp.bfloat16
MESH = pl.DeviceIdType.MESH
single = jnp.float32
highest = lax.Precision.HIGHEST


def dot(left, right, left_dim=1, right_dim=0, precision=None):
    return lax.dot_general(
        left,
        right,
        (((left_dim,), (right_dim,)), ((), ())),
        precision=precision,
        preferred_element_type=single,
    )


def normalize(values):
    factor = lax.rsqrt(jnp.mean(values * values, axis=-1, keepdims=True) + epsilon)
    return (values * factor, factor)


def norm_back(grad_scaled, normed, factor):
    return factor * (grad_scaled - normed * jnp.mean(grad_scaled * normed, axis=-1, keepdims=True))


def gather_dp(values):
    return lax.all_gather(values, "dp", axis=0, tiled=True)


def scatter_dp(values):
    return lax.psum_scatter(values, "dp", scatter_dimension=0, tiled=True)


def gather_xla(values):
    return lax.all_gather(values, "ctx", axis=0, tiled=True)


def scatter_xla(values):
    return lax.psum_scatter(values, "ctx", scatter_dimension=0, tiled=True)


def exchange_xla(values):
    return lax.all_to_all(values, "ctx", 0, 0, tiled=True)


class Line:
    def __init__(self, ctx):
        self.pairs = ctx // 2
        self.place = lax.axis_index("ctx")
        self.pair, self.core = self.place // 2, self.place % 2
        self.has_left, self.has_right = self.pair > 0, self.pair < self.pairs - 1
        self.left = {"ctx": jnp.maximum(self.place - 2, 0)}
        self.right = {"ctx": jnp.minimum(self.place + 2, ctx - 1)}
        self.twin = {"ctx": self.place + 1 - 2 * self.core}


def remote(source, target, send, receive, device):
    return pltpu.make_async_remote_copy(
        src_ref=source, dst_ref=target, send_sem=send, recv_sem=receive,
        device_id=device, device_id_type=MESH,
    )


def gather_line(line, own_ref, all_ref, sems):
    send_left, send_right, send_twin, receive, receive_twin, local = sems
    pairs, pair, core = line.pairs, line.pair, line.core

    def to_side(source, slot, sem, device):
        return remote(source, all_ref.at[slot * 2 + core], sem.at[slot], receive.at[slot], device)

    def to_twin(source, slot):
        return remote(source, all_ref.at[slot * 2 + core], send_twin.at[slot], receive_twin.at[slot], line.twin)

    pl.when(line.has_right)(lambda: to_side(own_ref, pair, send_right, line.right).start())
    pl.when(line.has_left)(lambda: to_side(own_ref, pair, send_left, line.left).start())
    to_twin(own_ref, pair).start()
    keep = pltpu.make_async_copy(own_ref, all_ref.at[line.place], local)
    keep.start()
    for step in range(1, pairs):
        def from_left(slot=pair - step):
            block = all_ref.at[slot * 2 + core]
            to_side(block, slot, send_left, line.left).wait_recv()
            pl.when(line.has_right)(lambda: to_side(block, slot, send_right, line.right).start())
            to_twin(block, slot).start()

        def from_right(slot=pair + step):
            block = all_ref.at[slot * 2 + core]
            to_side(block, slot, send_right, line.right).wait_recv()
            pl.when(line.has_left)(lambda: to_side(block, slot, send_left, line.left).start())
            to_twin(block, slot).start()

        pl.when(pair - step >= 0)(from_left)
        pl.when(pair + step < pairs)(from_right)
    keep.wait()
    for slot in range(pairs):
        to_twin(own_ref, slot).wait()
        pl.when((slot <= pair) & line.has_right)(
            lambda slot=slot: to_side(own_ref, slot, send_right, line.right).wait_send())
        pl.when((slot >= pair) & line.has_left)(
            lambda slot=slot: to_side(own_ref, slot, send_left, line.left).wait_send())


def comm_params(collective_id, mebibytes):
    return pltpu.CompilerParams(
        collective_id=collective_id, has_side_effects=True, vmem_limit_bytes=mebibytes << 20
    )


def link_cost(size):
    return pl.CostEstimate(flops=0, transcendentals=0, bytes_accessed=size)


def scatter_line(line, parts_ref, twin_ref, left_ref, right_ref, send_ref, sems):
    send_twin, receive_twin, send_left, send_right, from_left_sem, from_right_sem = sems
    pairs, pair, core = line.pairs, line.pair, line.core

    def to_twin(slot):
        return remote(parts_ref.at[slot * 2 + 1 - core], twin_ref.at[slot], send_twin.at[slot], receive_twin.at[slot], line.twin)

    def to_right(slot):
        return remote(send_ref.at[slot], left_ref.at[slot], send_right.at[slot], from_left_sem.at[slot], line.right)

    def to_left(slot):
        return remote(send_ref.at[slot], right_ref.at[slot], send_left.at[slot], from_right_sem.at[slot], line.left)

    def both_cores(slot):
        return parts_ref[slot * 2 + core].astype(single) + twin_ref[slot].astype(single)

    for step in range(pairs - 1, 0, -1):
        pl.when(pair + step < pairs)(lambda slot=pair + step: to_twin(slot).start())
        pl.when(pair - step >= 0)(lambda slot=pair - step: to_twin(slot).start())
    to_twin(pair).start()
    for step in range(pairs - 1, 0, -1):
        def pass_right(slot=pair + step):
            to_twin(slot).wait_recv()
            send_ref[slot] = both_cores(slot).astype(send_ref.dtype)

            @pl.when(line.has_left)
            def _():
                to_right(slot).wait_recv()
                send_ref[slot] = (both_cores(slot) + left_ref[slot].astype(single)).astype(send_ref.dtype)
            to_right(slot).start()

        def pass_left(slot=pair - step):
            to_twin(slot).wait_recv()
            send_ref[slot] = both_cores(slot).astype(send_ref.dtype)

            @pl.when(line.has_right)
            def _():
                to_left(slot).wait_recv()
                send_ref[slot] = (both_cores(slot) + right_ref[slot].astype(single)).astype(send_ref.dtype)
            to_left(slot).start()

        pl.when(pair + step < pairs)(pass_right)
        pl.when(pair - step >= 0)(pass_left)
    to_twin(pair).wait_recv()


def scatter_total(line, parts_ref, twin_ref, left_ref, right_ref, send_ref, sems, out_ref):
    send_twin, receive_twin, send_left, send_right, from_left_sem, from_right_sem = sems
    pairs, pair, core = line.pairs, line.pair, line.core
    out_ref[...] = parts_ref[pair * 2 + core].astype(single) + twin_ref[pair].astype(single)

    @pl.when(line.has_left)
    def _():
        remote(send_ref.at[pair], left_ref.at[pair], send_right.at[pair], from_left_sem.at[pair], line.right).wait_recv()
        out_ref[...] += left_ref[pair].astype(single)

    @pl.when(line.has_right)
    def _():
        remote(send_ref.at[pair], right_ref.at[pair], send_left.at[pair], from_right_sem.at[pair], line.left).wait_recv()
        out_ref[...] += right_ref[pair].astype(single)

    for slot in range(pairs):
        remote(parts_ref.at[slot], twin_ref.at[slot], send_twin.at[slot], receive_twin.at[slot], line.twin).wait_send()
        pl.when(slot > pair)(lambda slot=slot: remote(
            send_ref.at[slot], left_ref.at[slot], send_right.at[slot], from_left_sem.at[slot], line.right).wait_send())
        pl.when(slot < pair)(lambda slot=slot: remote(
            send_ref.at[slot], right_ref.at[slot], send_left.at[slot], from_right_sem.at[slot], line.left).wait_send())


def gather_sems(ctx):
    return [pltpu.SemaphoreType.DMA((ctx // 2,))] * 5 + [pltpu.SemaphoreType.DMA]


def scatter_scratch(ctx, shape, dtype):
    return [pltpu.VMEM((ctx // 2,) + shape, dtype)] * 4 + [pltpu.SemaphoreType.DMA((ctx // 2,))] * 6


def pair_sems(count):
    return [pltpu.SemaphoreType.DMA((count,))] * 2 + [pltpu.SemaphoreType.DMA]


class ExchangeCtx:
    reach = "ctx"

    def __init__(self, dp, ctx, parts):
        self.count, self.parts = ctx, parts
        self.axis = len(parts.shape) - 3
        shape = parts.shape if not self.axis else (ctx, parts.shape[0]) + parts.shape[2:]
        self.result = jax.ShapeDtypeStruct(shape, parts.dtype)
        self.scratch = pair_sems(ctx)

    def copies(self, source, target, send, receive, local):
        place = lax.axis_index("ctx")

        def part(index):
            return source.at[:, index] if self.axis else source.at[index]

        out = [pltpu.make_async_copy(part(place), target.at[place], local)]
        for step in range(1, self.count):
            other = (place + step) % self.count
            out.append(
                remote(
                    part(other), target.at[place], send.at[step], receive.at[step], {"ctx": other}
                )
            )
        return out


class ExchangeDp:
    reach = "dp"
    whole = False

    def __init__(self, dp, ctx, parts):
        self.count, self.parts = dp, parts
        shape = (dp,) + parts.shape if self.whole else parts.shape
        self.result = jax.ShapeDtypeStruct(shape, parts.dtype)
        self.scratch = pair_sems(dp)

    def copies(self, source, target, send, receive, local):
        row = lax.axis_index("dp")

        def part(index):
            return source if self.whole else source.at[index]

        out = [pltpu.make_async_copy(part(row), target.at[row], local)]
        for step in range(1, self.count):
            other = (row + step) % self.count
            out.append(
                remote(part(other), target.at[row], send.at[step], receive.at[step], {"dp": other})
            )
        return out


class GatherDp(ExchangeDp):
    whole = True


class ExchangeAll:
    reach = "all"
    whole = False

    def __init__(self, dp, ctx, parts):
        self.dp, self.ctx, self.parts = dp, ctx, parts
        shape = (dp, ctx) + parts.shape if self.whole else parts.shape
        self.result = jax.ShapeDtypeStruct(shape, parts.dtype)
        self.scratch = pair_sems(dp * ctx)

    def copies(self, source, target, send, receive, local):
        row, place = lax.axis_index("dp"), lax.axis_index("ctx")

        def part(index):
            return source if self.whole else source.at[index[0], index[1]]

        out = [pltpu.make_async_copy(part((row, place)), target.at[row, place], local)]
        for index, other in enumerate(everyone(self.dp, self.ctx)):
            out.append(
                remote(
                    part(other), target.at[row, place], send.at[index], receive.at[index],
                    {"dp": other[0], "ctx": other[1]},
                )
            )
        return out


class GatherAll(ExchangeAll):
    whole = True


class GatherLine:
    reach = "ctx"

    def __init__(self, dp, ctx, parts):
        self.parts = parts
        self.result = jax.ShapeDtypeStruct((ctx,) + parts.shape, parts.dtype)
        self.scratch = gather_sems(ctx)

    def run(self, line, source, target, *sems):
        gather_line(line, source, target, sems)


class ScatterLine:
    reach = "ctx"

    def __init__(self, dp, ctx, parts):
        self.parts = parts
        self.result = jax.ShapeDtypeStruct(parts.shape[1:], single)
        self.scratch = scatter_scratch(ctx, parts.shape[1:], parts.dtype)

    def run(self, line, source, target, *scratch):
        scatter_line(line, source, *scratch[:4], scratch[4:])
        scatter_total(line, source, *scratch[:4], scratch[4:], target)


class LatentLine:
    reach = "ctx"

    def __init__(self, dp, ctx, parts):
        shape = parts.shape[1:]
        self.parts = parts
        self.result = [
            jax.ShapeDtypeStruct(shape, single), jax.ShapeDtypeStruct(parts.shape, bfloat)
        ]
        self.scratch = [pltpu.VMEM(shape, bfloat)] + scatter_scratch(ctx, shape, bfloat) + gather_sems(ctx)

    def finish_own(self, extra, sums_ref, own_ref):
        gain_ref, table_ref = extra
        for span in (QUERY_SPAN, LATENT_SPAN):
            normed, _ = normalize(sums_ref[:, span])
            own_ref[:, span] = (normed * gain_ref[:, span]).astype(bfloat)
        own_ref[:, ROPE_SPAN] = turn(sums_ref[:, ROPE_SPAN], table_ref, 1.0).astype(bfloat)

    def run(self, line, extra, source, sums_ref, all_ref, own_ref, *scratch):
        scatter_line(line, source, *scratch[:4], scratch[4:10])
        scatter_total(line, source, *scratch[:4], scratch[4:10], sums_ref)
        self.finish_own(extra, sums_ref, own_ref)
        gather_line(line, own_ref, all_ref, scratch[10:])


class LatentBackLine(LatentLine):
    def finish_own(self, extra, sums_ref, own_ref):
        gain_ref, table_ref, latents_ref = extra
        for span in (QUERY_SPAN, LATENT_SPAN):
            normed, factor = normalize(latents_ref[:, span])
            scaled = sums_ref[:, span] * gain_ref[:, span]
            own_ref[:, span] = norm_back(scaled, normed, factor).astype(bfloat)
        own_ref[:, ROPE_SPAN] = turn(sums_ref[:, ROPE_SPAN], table_ref, -1.0).astype(bfloat)


QUERY_SPAN = slice(0, QRANK)
LATENT_SPAN = slice(QRANK, QRANK + KVRANK)
ROPE_SPAN = slice(QRANK + KVRANK, LATENT)


def turn(values, table_ref, sign):
    return (
        values * table_ref[0]
        + sign * pltpu.roll(values, LANES - ROPE // 2, 1) * table_ref[1]
        + sign * pltpu.roll(values, ROPE // 2, 1) * table_ref[2]
    )


def everyone(dp, ctx):
    row, place = lax.axis_index("dp"), lax.axis_index("ctx")
    steps = [(a, b) for a in range(dp) for b in range(ctx) if a or b]
    return [((row + a) % dp, (place + b) % ctx) for a, b in steps]


def greet(dp, ctx, reach):
    row, place = lax.axis_index("dp"), lax.axis_index("ctx")
    if "all" in reach:
        targets = [{"dp": a, "ctx": b} for a, b in everyone(dp, ctx)]
    else:
        targets = []
        if "ctx" in reach:
            targets += [{"ctx": (place + step) % ctx} for step in range(1, ctx)]
        if "dp" in reach:
            targets += [{"dp": (row + step) % dp} for step in range(1, dp)]
    barrier = pltpu.get_barrier_semaphore()
    for target in targets:
        pl.semaphore_signal(barrier, inc=1, device_id=target, device_id_type=MESH)
    pl.semaphore_wait(barrier, len(targets))


def transfer_kernel(dp, ctx, line_piece, direct, extras, *refs):
    refs = list(refs)

    def take(count):
        taken = refs[:count]
        del refs[:count]
        return taken

    line_count = 1 if line_piece else 0
    sources = take(line_count + len(direct))
    extra = take(extras)
    results = [take(len(piece.result)) if isinstance(piece.result, list) else take(1)
               for piece in ([line_piece] if line_piece else []) + direct]
    greet(dp, ctx, [piece.reach for piece in direct] + (["ctx"] if line_piece else []))
    line_scratch = take(len(line_piece.scratch)) if line_piece else []
    copies = []
    for piece, source, result in zip(direct, sources[line_count:], results[line_count:]):
        copies += piece.copies(source, result[0], *take(len(piece.scratch)))
    for copy in copies:
        copy.start()
    if line_piece:
        before = (extra,) if extras else ()
        line_piece.run(Line(ctx), *before, sources[0], *results[0], *line_scratch)
    for copy in copies:
        copy.wait()


def transfer(dp, ctx, collective_id, name, line=None, direct=(), extra=()):
    line_piece = line[0](dp, ctx, line[1]) if line else None
    pieces = [item[0](dp, ctx, item[1]) for item in direct]
    everything = ([line_piece] if line else []) + pieces
    vmem, anywhere = pl.BlockSpec(memory_space=pltpu.VMEM), pl.BlockSpec(memory_space=pl.ANY)
    shapes, out_specs, in_specs, moved = [], [], [], 0
    for piece in everything:
        held = isinstance(piece, (ScatterLine, LatentLine))
        in_specs.append(vmem if held else anywhere)
        results = piece.result if isinstance(piece.result, list) else [piece.result]
        shapes += results
        out_specs += [vmem if held and index == 0 else anywhere for index in range(len(results))]
        moved += piece.parts.size * 2
    out = pl.pallas_call(
        functools.partial(transfer_kernel, dp, ctx, line_piece, pieces, len(extra)),
        out_shape=shapes,
        in_specs=in_specs + [vmem] * len(extra),
        out_specs=out_specs,
        scratch_shapes=[item for piece in everything for item in piece.scratch],
        compiler_params=comm_params(collective_id, 40 if line and line[0] is not GatherLine else 8),
        cost_estimate=link_cost(150 << 20),
        name=name,
    )(*[piece.parts for piece in everything], *extra)
    return out


def rows_of(ref):
    block = ref[...]
    return block.reshape(block.shape[0] * block.shape[2], block.shape[3])


def store_rows(ref, lanes, values):
    ref[:, :, :, lanes] = values.reshape(ref.shape[0], 1, ref.shape[2], values.shape[-1])


def head_lanes(head):
    return pl.ds(head * LANES, LANES)


def valid_pairs(total, length):
    row = lax.broadcasted_iota(jnp.int32, (total, total), 0)
    col = lax.broadcasted_iota(jnp.int32, (total, total), 1)
    return (col <= row) & (col < length)


def attend_kernel(
    heads, length_ref, latent_ref, query_up_ref, latent_up_ref, table_ref,
    query_ref, kv_ref, attn_ref, total_ref,
):
    latent = rows_of(latent_ref)
    total = latent.shape[0]
    query_normed = latent[:, :QRANK]
    latent_normed = latent[:, QRANK : QRANK + KVRANK]
    rope = latent[:, QRANK + KVRANK :]
    allowed = valid_pairs(total, length_ref[pl.program_id(0)])
    lane = lax.broadcasted_iota(jnp.int32, (total, LANES), 1)
    cosine, sine_low, sine_high = table_ref[0], table_ref[1], table_ref[2]
    totals = jnp.zeros((total, LANES), single)
    for head in range(heads):
        full = dot(query_normed, query_up_ref[:, head_lanes(head)])
        query = (
            full * cosine
            + pltpu.roll(full, LANES - ROPE // 2, 1) * sine_low
            + pltpu.roll(full, ROPE // 2, 1) * sine_high
        ).astype(bfloat)
        kv = dot(latent_normed, latent_up_ref[:, head_lanes(head)]).astype(bfloat)
        key = jnp.where(lane < NOPE, kv, rope)
        store_rows(query_ref, head_lanes(head), query)
        store_rows(kv_ref, head_lanes(head), kv)
        scores = dot(query, key, 1, 1) * score_scale
        masked = jnp.where(allowed, scores, neg_large)
        top = jnp.max(masked, axis=-1, keepdims=True)
        exponent = jnp.exp(masked - top)
        weight = jnp.sum(exponent, axis=-1, keepdims=True)
        totals = jnp.where(lane == head, top + jnp.log(weight), totals)
        probs = (exponent * (1.0 / weight)).astype(bfloat)
        out = dot(probs, kv).T[NOPE:]
        attn_ref[head * VDIM : (head + 1) * VDIM] = out.astype(bfloat)
    store_rows(total_ref, pl.ds(0, LANES), totals)


def attend_back_kernel(
    heads, length_ref, query_ref, kv_ref, rope_ref, total_ref, grad_attn_ref, table_ref,
    grad_query_ref, grad_kv_ref, grad_rope_ref,
):
    rope = rows_of(rope_ref)
    total = rope.shape[0]
    totals = rows_of(total_ref)
    allowed = valid_pairs(total, length_ref[pl.program_id(0)])
    lane = lax.broadcasted_iota(jnp.int32, (total, LANES), 1)
    cosine, sine_low, sine_high = table_ref[0], table_ref[1], table_ref[2]
    grad_rope = jnp.zeros((total, LANES), single)
    queries, kvs, grads = rows_of(query_ref), rows_of(kv_ref), rows_of(grad_attn_ref)
    for head in range(heads):
        span = slice(head * LANES, (head + 1) * LANES)
        query, kv, grad_attn = queries[:, span], kvs[:, span], grads[:, span]
        key = jnp.where(lane < NOPE, kv, rope)
        scores = dot(query, key, 1, 1) * score_scale
        probs = jnp.where(allowed, jnp.exp(scores - totals[:, head : head + 1]), 0.0)
        grad_probs = dot(grad_attn, kv, 1, 1)
        delta = jnp.sum(probs * grad_probs, axis=-1, keepdims=True)
        grad_scores = (probs * (grad_probs - delta)).astype(bfloat)
        grad_query = (dot(grad_scores, key) * score_scale).astype(bfloat).astype(single)
        grad_full = (
            grad_query * cosine
            - pltpu.roll(grad_query, LANES - ROPE // 2, 1) * sine_low
            - pltpu.roll(grad_query, ROPE // 2, 1) * sine_high
        )
        store_rows(grad_query_ref, head_lanes(head), grad_full.astype(bfloat))
        grad_key = dot(grad_scores, query, 0, 0) * score_scale
        grad_value = dot(probs.astype(bfloat), grad_attn, 0, 0)
        store_rows(grad_kv_ref, head_lanes(head), jnp.where(lane < NOPE, grad_key, grad_value))
        grad_rope = grad_rope + jnp.where(lane < NOPE, 0.0, grad_key)
    store_rows(grad_rope_ref, pl.ds(0, LANES), grad_rope)


def slot_spec(ctx, span, width, block=0):
    return pl.BlockSpec((ctx, 1, span, width), lambda b: (0, b, 0, block))


def whole_spec(shape):
    return pl.BlockSpec(shape, lambda b: (0,) * len(shape))


def attend(lengths, latent, query_up, latent_up, table, heads):
    ctx, batch, span, _ = latent.shape
    wide = heads * LANES
    shapes = [
        ((ctx, batch, span, wide), bfloat),
        ((ctx, batch, span, wide), bfloat),
        ((heads * VDIM, batch * ctx * span), bfloat),
        ((ctx, batch, span, LANES), single),
    ]
    return pl.pallas_call(
        functools.partial(attend_kernel, heads),
        grid=(batch,),
        out_shape=[jax.ShapeDtypeStruct(*item) for item in shapes],
        in_specs=[
            pl.BlockSpec(memory_space=pltpu.SMEM),
            slot_spec(ctx, span, LATENT),
            whole_spec(query_up.shape),
            whole_spec(latent_up.shape),
            whole_spec(table.shape),
        ],
        out_specs=[
            slot_spec(ctx, span, wide),
            slot_spec(ctx, span, wide),
            pl.BlockSpec((heads * VDIM, ctx * span), lambda b: (0, b)),
            slot_spec(ctx, span, LANES),
        ],
        compiler_params=pltpu.CompilerParams(vmem_limit_bytes=56 << 20),
        name="attend",
    )(lengths, latent, query_up, latent_up, table)


def attend_back(lengths, query, kv, latent, totals, grad_attn, table, heads):
    ctx, batch, span, _ = latent.shape
    wide = heads * LANES
    shapes = [
        ((ctx, batch, span, wide), bfloat),
        ((ctx, batch, span, wide), single),
        ((ctx, batch, span, LANES), single),
    ]
    return pl.pallas_call(
        functools.partial(attend_back_kernel, heads),
        grid=(batch,),
        out_shape=[jax.ShapeDtypeStruct(*item) for item in shapes],
        in_specs=[
            pl.BlockSpec(memory_space=pltpu.SMEM),
            slot_spec(ctx, span, wide),
            slot_spec(ctx, span, wide),
            slot_spec(ctx, span, LANES, (QRANK + KVRANK) // LANES),
            slot_spec(ctx, span, LANES),
            slot_spec(ctx, span, wide),
            whole_spec(table.shape),
        ],
        out_specs=[slot_spec(ctx, span, item[0][-1]) for item in shapes],
        compiler_params=pltpu.CompilerParams(vmem_limit_bytes=56 << 20),
        name="attend_back",
    )(lengths, query, kv, latent, totals, grad_attn, table)


def angles_at(positions):
    freqs = 10000.0 ** (-(2.0 * jnp.arange(ROPE // 2, dtype=single)) / ROPE)
    angles = positions.astype(single)[:, None] * freqs[None, :]
    return (jnp.cos(angles), jnp.sin(angles))


def head_table(positions):
    total = positions.shape[0]
    cosine, sine = angles_at(positions)
    ones, none = jnp.ones((total, NOPE), single), jnp.zeros((total, NOPE), single)
    tail = jnp.zeros((total, LANES - NOPE - ROPE), single)
    zero = jnp.zeros_like(sine)
    return jnp.stack(
        [
            jnp.concatenate([ones, cosine, cosine, tail], axis=-1),
            jnp.concatenate([none, -sine, zero, tail], axis=-1),
            jnp.concatenate([none, zero, sine, tail], axis=-1),
        ]
    )


def pad_rope(values):
    return jnp.pad(values, ((0, 0), (NOPE, LANES - NOPE - ROPE)))


def on_device(
    dp,
    ctx,
    tokens,
    lengths,
    cotangent,
    input_gain,
    query_gain,
    latent_gain,
    post_gain,
    query_down,
    query_up,
    latent_down,
    latent_up,
    out_proj,
    gate_proj,
    up_proj,
    down_proj,
):
    batch, span, _ = tokens.shape
    own = batch * span
    group = ctx * own
    heads = -(-HEADS // ctx)
    spare = heads * ctx - HEADS
    d_rows, q_rows, l_rows, f_rows = (
        query_down.shape[0], query_up.shape[0], latent_up.shape[0], down_proj.shape[0],
    )
    d_part, f_part = dp * d_rows, dp * f_rows
    place = lax.axis_index("ctx")

    def slices(values):
        return values.reshape(own, dp, ctx, d_rows).transpose(2, 0, 1, 3).reshape(ctx, own, d_part)

    def unslices(values):
        return values.reshape(ctx, own, dp, d_rows).transpose(1, 2, 0, 3).reshape(own, D)

    def columns(values):
        split = values.reshape(d_rows, dp, ctx, f_rows).transpose(2, 0, 1, 3)
        return split.reshape(ctx, d_rows, f_part)

    def from_columns(values):
        split = values.reshape(ctx, d_rows, dp, f_rows).transpose(1, 2, 0, 3)
        return split.reshape(d_rows, FF).astype(single)

    def row_sums(values):
        return jnp.sum(values.astype(single), axis=0)

    wide = heads * LANES
    up_rows = q_rows + l_rows
    run = functools.partial(transfer, dp, ctx)

    flat = tokens.reshape(own, D)
    inputs = flat.astype(single)
    normed_first, factor_first = normalize(inputs)
    gains = jnp.concatenate([input_gain, query_gain, latent_gain, post_gain]).astype(single)
    tile = 8 * LANES
    small = jnp.concatenate(
        [jnp.pad(gains, (0, tile - gains.shape[0])), jnp.pad(factor_first[:, 0], (0, tile - own))]
    )
    down_own = jnp.concatenate(
        [query_down, latent_down[:, :KVRANK], pad_rope(latent_down[:, KVRANK:])], axis=1
    )
    up_query = query_up.reshape(q_rows, HEADS, NOPE + ROPE)
    up_query = jnp.pad(up_query, ((0, 0), (0, spare), (0, LANES - NOPE - ROPE)))
    up_latent = jnp.pad(latent_up.reshape(l_rows, HEADS, NOPE + VDIM), ((0, 0), (0, spare), (0, 0)))
    ups = jnp.concatenate([up_query, up_latent], axis=0)
    ups = ups.reshape(up_rows, ctx, wide).transpose(1, 0, 2)
    token_slices, ups, down_rows, smalls = run(
        1, "open",
        direct=[
            (ExchangeCtx, slices(flat)), (ExchangeCtx, ups), (GatherDp, down_own),
            (GatherAll, small.reshape(16, LANES)),
        ],
    )
    gate_proj, up_proj, out_proj, smalls = lax.optimization_barrier(
        (gate_proj, up_proj, out_proj, smalls)
    )
    down_rows = down_rows.reshape(d_part, LATENT)
    smalls = smalls.reshape(dp, ctx, 2 * tile)
    factor_all = smalls[lax.axis_index("dp"), :, tile : tile + own].reshape(group, 1)
    cuts = (d_rows, d_rows + q_rows, d_rows + up_rows, d_rows + up_rows + d_rows)
    gain_in = lax.dynamic_index_in_dim(smalls[:, :, : cuts[0]], place, 1, keepdims=False)
    gain_in = gain_in.reshape(1, d_part)
    gain_query = smalls[:, :, cuts[0] : cuts[1]].reshape(1, QRANK)
    gain_latent = smalls[:, :, cuts[1] : cuts[2]].reshape(1, KVRANK)
    gain_post = smalls[:, :, cuts[2] : cuts[3]].reshape(1, D)
    gain_down = jnp.concatenate([gain_query, gain_latent, jnp.zeros((1, LANES), single)], axis=1)

    out_padded = jnp.pad(out_proj, ((0, 0), (0, spare * VDIM)))
    out_rows = gather_dp(out_padded)
    down = gather_dp(down_proj)
    grad_out = cotangent.reshape(own, D).astype(single)
    grad_branch = gather_xla((branch_scale * grad_out).astype(bfloat))

    normed_slices = token_slices.reshape(group, d_part).astype(single) * factor_all
    normed_in = (normed_slices * gain_in).astype(bfloat)
    own_table = head_table(place * span + jnp.arange(own, dtype=jnp.int32) % span)
    parts = dot(normed_in, down_rows).astype(bfloat).reshape(ctx, own, LATENT)
    out_heads = out_padded.reshape(d_rows, ctx, heads * VDIM).transpose(1, 0, 2)
    latents, latent_all, ups, gate, up, out_heads = run(
        2, "latent_sum", (LatentLine, parts),
        [
            (GatherDp, ups.reshape(ctx * up_rows, wide)), (ExchangeCtx, columns(gate_proj)),
            (ExchangeCtx, columns(up_proj)), (ExchangeCtx, out_heads),
        ],
        (gain_down, own_table),
    )
    ups = ups.reshape(dp * ctx, up_rows, wide)
    query_ups = ups[:, :q_rows].reshape(QRANK, wide)
    latent_ups = ups[:, q_rows:].reshape(KVRANK, wide)

    table = head_table(jnp.arange(ctx * span, dtype=jnp.int32))
    latent_slots = latent_all.reshape(ctx, batch, span, LATENT)
    latent_all = latent_all.reshape(group, LATENT)
    query, kv, attn, totals = attend(lengths, latent_slots, query_ups, latent_ups, table, heads)
    attn_all, gate = run(
        3, "attn_gather", (GatherLine, attn), [(GatherDp, gate.reshape(ctx * d_rows, f_part))]
    )
    attn_all = attn_all.reshape(ctx * heads * VDIM, group)
    gate = gate.reshape(D, f_part)
    branch = dot(attn_all, out_rows, 0, 1).astype(bfloat).reshape(batch, ctx, span, d_part)
    branch, out_heads = run(
        4, "branch_exchange",
        direct=[(ExchangeCtx, branch), (GatherDp, out_heads.reshape(ctx * d_rows, heads * VDIM))],
    )
    out_heads = jnp.pad(out_heads.reshape(D, heads, VDIM), ((0, 0), (0, 0), (NOPE, 0)))
    out_heads = out_heads.reshape(D, wide)
    middle = inputs + branch_scale * unslices(branch.reshape(ctx, own, d_part)).astype(single)
    normed_post, factor_post = normalize(middle)
    normed_mid, up = run(
        5, "mid_gather", (GatherLine, (normed_post * gain_post).astype(bfloat)),
        [(GatherDp, up.reshape(ctx * d_rows, f_part))],
    )
    normed_mid = normed_mid.reshape(group, D)
    up = up.reshape(D, f_part)

    gate_act = dot(normed_mid, gate)
    up_act = dot(normed_mid, up)
    sigma = jax.nn.sigmoid(gate_act)
    hidden = (gate_act * sigma * up_act).astype(bfloat)
    branch_out = scatter_xla(dot(hidden, down).astype(bfloat)).astype(single)
    layer_out = (middle + branch_scale * branch_out).astype(bfloat)
    grad_hidden = dot(grad_branch, down, 1, 1)
    grad_gate = (grad_hidden * up_act * (sigma * (1.0 + gate_act * (1.0 - sigma)))).astype(bfloat)
    grad_up = (grad_hidden * (gate_act * sigma)).astype(bfloat)
    grad_normed_mid = dot(grad_gate, gate, 1, 1) + dot(grad_up, up, 1, 1)
    rows = (dp, ctx * d_rows, f_part)
    grad_normed_mid, grad_gate_proj = run(
        6, "mid_scatter", (ScatterLine, grad_normed_mid.astype(bfloat).reshape(ctx, own, D)),
        [(ExchangeDp, dot(normed_mid, grad_gate, 0, 0).astype(bfloat).reshape(rows))],
    )
    grad_middle = grad_out + norm_back(grad_normed_mid * gain_post, normed_post, factor_post)
    grad_attn_branch, grad_up_proj = run(
        7, "branch_gather", (GatherLine, (branch_scale * grad_middle).astype(bfloat)),
        [(ExchangeDp, dot(normed_mid, grad_up, 0, 0).astype(bfloat).reshape(rows))],
    )
    grad_attn_branch = grad_attn_branch.reshape(group, D)

    grad_attn = dot(grad_attn_branch, out_heads).astype(bfloat)
    grad_query, grad_kv, grad_rope = attend_back(
        lengths, query, kv, latent_slots, totals,
        grad_attn.reshape(ctx, batch, span, wide), table, heads,
    )
    grad_query = grad_query.reshape(group, wide)
    grad_kv = grad_kv.reshape(group, wide)
    grad_latents = jnp.concatenate(
        [
            dot(grad_query, query_ups, 1, 1),
            dot(grad_kv, latent_ups.astype(single), 1, 1, highest),
            grad_rope.reshape(group, LANES),
        ],
        axis=-1,
    ).astype(bfloat)
    grad_query_ups = dot(latent_all[:, :QRANK], grad_query, 0, 0)
    grad_latent_ups = dot(
        latent_all[:, QRANK : QRANK + KVRANK].astype(single), grad_kv, 0, 0, highest
    )
    grad_ups = jnp.concatenate(
        [
            grad_query_ups.reshape(dp * ctx, q_rows, wide),
            grad_latent_ups.reshape(dp * ctx, l_rows, wide),
        ],
        axis=1,
    ).astype(bfloat)
    grad_down_proj = dot(hidden, grad_branch, 0, 0).astype(bfloat).reshape(dp, f_rows, D)
    columns_shape = (ctx, d_rows, f_part)
    grad_latents, grad_down, grad_ups, grad_down_proj, grad_gate_proj, grad_up_proj = run(
        8, "latent_sum_back", (LatentBackLine, grad_latents.reshape(ctx, own, LATENT)),
        [
            (ExchangeDp, grad_ups.reshape(dp, ctx * up_rows, wide)),
            (ExchangeDp, grad_down_proj),
            (ExchangeCtx, row_sums(grad_gate_proj).astype(bfloat).reshape(columns_shape)),
            (ExchangeCtx, row_sums(grad_up_proj).astype(bfloat).reshape(columns_shape)),
        ],
        (gain_down, own_table, latents),
    )
    grad_down = grad_down.reshape(group, LATENT)
    grad_normed_in = dot(grad_down, down_rows, 1, 1)
    grad_scaled = (grad_normed_in * gain_in).astype(bfloat).reshape(ctx, own, d_part)
    grad_rows = dot(normed_in, grad_down, 0, 0)
    last = jnp.sum(grad_normed_in * normed_slices, axis=0)[:, None]
    grad_rows = jnp.concatenate([grad_rows[:, : LATENT - 1], last], axis=1)
    normed_query, _ = normalize(latents[:, :QRANK])
    normed_latent, _ = normalize(latents[:, QRANK : QRANK + KVRANK])
    grad_query_normed = grad_latents[:, :QRANK]
    grad_latent_normed = grad_latents[:, QRANK : QRANK + KVRANK]
    gain_sums = jnp.concatenate(
        [
            jnp.sum(grad_normed_mid * normed_post, axis=0).reshape(dp, ctx, d_rows),
            jnp.sum(grad_query_normed * normed_query, axis=0).reshape(dp, ctx, q_rows),
            jnp.sum(grad_latent_normed * normed_latent, axis=0).reshape(dp, ctx, l_rows),
        ],
        axis=2,
    )
    gain_sums = jnp.pad(gain_sums, ((0, 0), (0, 0), (0, tile - gain_sums.shape[2])))
    row = lax.broadcasted_iota(jnp.int32, (D, d_part), 0)
    col = lax.broadcasted_iota(jnp.int32, (D, d_part), 1)
    chosen = (row == (col // d_rows) * (ctx * d_rows) + place * d_rows + col % d_rows).astype(bfloat)
    branch_slices = dot(grad_attn_branch, chosen).astype(bfloat).reshape(ctx, batch, span, d_part)
    branch_slices = branch_slices.transpose(1, 0, 2, 3).reshape(group, d_part)
    grad_out_proj = dot(branch_slices, attn_all[: HEADS * VDIM], 0, 1).astype(bfloat)
    grad_scaled, grad_rows, grad_out_proj, grad_ups, gain_sums = run(
        9, "close",
        direct=[
            (ExchangeCtx, grad_scaled), (ExchangeDp, grad_rows.reshape(dp, d_rows, LATENT)),
            (ExchangeDp, grad_out_proj.reshape(dp, d_rows, HEADS * VDIM)),
            (ExchangeCtx, row_sums(grad_ups).astype(bfloat).reshape(ctx, up_rows, wide)),
            (ExchangeAll, gain_sums.reshape(dp, ctx, 8, LANES)),
        ],
    )
    input_grad = grad_middle + norm_back(
        unslices(grad_scaled).astype(single), normed_first, factor_first
    )
    grad_rows = jnp.sum(grad_rows, axis=0)
    gain_sums = jnp.sum(gain_sums.reshape(dp * ctx, tile), axis=0)
    grad_ups = grad_ups.transpose(1, 0, 2).reshape(up_rows, ctx * heads, LANES)
    grad_ups = grad_ups[:, :HEADS].astype(single)
    grad_query_up = grad_ups[:q_rows, :, : NOPE + ROPE].reshape(q_rows, HEADS * (NOPE + ROPE))
    grad_latent_up = grad_ups[q_rows:].reshape(l_rows, HEADS * (NOPE + VDIM))
    rope_start = QRANK + KVRANK + NOPE
    return (
        layer_out.reshape(batch, span, D),
        input_grad.reshape(batch, span, D),
        grad_rows[:, LATENT - 1],
        gain_sums[d_rows : d_rows + q_rows],
        gain_sums[d_rows + q_rows : d_rows + up_rows],
        gain_sums[:d_rows],
        grad_rows[:, :QRANK],
        grad_query_up,
        jnp.concatenate(
            [grad_rows[:, QRANK : QRANK + KVRANK], grad_rows[:, rope_start : rope_start + ROPE]], axis=1
        ),
        grad_latent_up,
        row_sums(grad_out_proj),
        from_columns(grad_gate_proj),
        from_columns(grad_up_proj),
        row_sums(grad_down_proj),
    )


def solution(mesh):
    both = ("dp", "ctx")
    tokens, vector, matrix = P("dp", "ctx", None), P(both), P(both, None)
    return jax.shard_map(
        functools.partial(on_device, mesh.shape["dp"], mesh.shape["ctx"]),
        mesh=mesh,
        in_specs=(tokens, P("dp"), tokens) + (vector,) * 4 + (matrix,) * 8,
        out_specs=(tokens, tokens) + (vector,) * 4 + (matrix,) * 8,
        check_vma=False,
    )
```

time: 1210 us -> 922 us (0.76)
  Pallas kernels: 26.4 us -> 595 us
  waiting for transfers between devices: 550 us -> 0.77 us
  blocking collectives: 284 us -> 0 us
  starting transfers between devices: 33 us -> 0.38 us
  local copies, waits for them, and re-layouts: 128 us -> 150 us
    pallas_call x0 -> x9, Pallas kernels: none -> 568 us  [transfer(): pl.pallas_call(functools.partial(transfer_kernel, dp, ctx, line_piece, pi...]
    all_to_all x5 -> x0, blocking collectives: 182 us -> none  [exchange_ctx(): return lax.all_to_all(values, 'ctx', 0, 0, tiled=True)]
    all_gather x6 -> x1, waiting for transfers between devices: 172 us -> 0.01 us  [gather_xla(): return lax.all_gather(values, 'ctx', axis=0, tiled=True)]
    reduce_scatter x8 -> x1, waiting for transfers between devices: 140 us -> 0.01 us  [scatter_xla(): return lax.psum_scatter(values, 'ctx', scatter_dimension=0, tiled=True)]
    unnamed x24 -> x4, waiting for transfers between devices: 107 us -> 0.74 us
    all_gather x6 -> x2, waiting for transfers between devices: 98 us -> 0.02 us  [gather_dp(): return lax.all_gather(values, 'dp', axis=0, tiled=True)]
    unnamed x2 -> x0, blocking collectives: 79.9 us -> none
    all_to_all x5 -> x0, waiting for transfers between devices: 32.8 us -> none  [exchange_ctx(): return lax.all_to_all(values, 'ctx', 0, 0, tiled=True)]
  transfers between devices with their start and end apart: 27 -> 4, of which waited for: 18 -> 0; matrix products, arithmetic and copies ran while one was open for 19% -> 25% of each run, Pallas kernels for 1% -> 61%
where the time goes in v2:
time: 922 us; the launch traced here: 914 us
  Pallas kernels  595 us (65%)
  local copies, waits for them, and re-layouts  150 us (16%)
  matrix products  117 us (13%)
  other arithmetic  35.8 us (4%)
  between operations  15.5 us (2%)
    pallas_call x9, Pallas kernels, transfer(): pl.pallas_call(functools.partial(transfer_kernel, dp, ctx, line_piece, pi...  568 us
    dot_general x20, matrix products, dot(): lax.dot_general(left, right, (((left_dim,), (right_dim,)), ((), ())), pre...  117 us
    unnamed x183, local copies, waits for them, and re-layouts  27.3 us
    convert_element_type x6, local copies, waits for them, and re-layouts, from_columns(): return split.reshape(d_rows, FF).astype(single)  24.3 us
  transfers between devices with their start and end apart: 4, of which 0 were waited for; matrix products, arithmetic and copies ran while one was open for 25% of the time, Pallas kernels for 61%

profile of v2, /device:TPU:9, one launch (start us, length us, event | category | flops | bytes accessed | tf_op | source)
XLA Modules:
  0.0 914.1 jit_solution(18440979988528802056)
XLA Ops:
  12.9 37.0 %open.1 = (bf16[8,128,320]{2,1,0:T(8,128)(2,1)S(1)}, bf16[8,32,640]{2,1,0:T(8,128)(2,1)S(1)}, bf16[4,80,1152]{2,1,0:T(8,128)(2,1)S(1)}, f32[4,8,16,128]{3,2,1,0:T(8,128)S(1)}) custom-call(bf16[8,128,320]{2,1,0:T(8,128)(2,1)S(1)} %copy.75.refs_0_, bf16[8,32,640]{2,1,0:T(8,128)(2,1)S(1)} %maximum_bitcast_fusion.refs_1_, bf16[80,1152]{1,0:T(8,128)(2,1)S(1)} %fusion.24.refs_2_, ...), custom_call_target="tpu_custom_call" | custom-call | bytes 157286400 | tf_op jit(solution)/shard_map/open/pallas_call | solution.py:441
  63.5 5.8 reshape.386
  78.5 137.7 %latent_sum.1 = (f32[128,1152]{1,0:T(8,128)S(1)}, bf16[8,128,1152]{2,1,0:T(8,128)(2,1)S(1)}, bf16[4,256,640]{2,1,0:T(8,128)(2,1)S(1)}, bf16[8,80,800]{2,1,0:T(8,...) custom-call(bf16[8,128,1152]{2,1,0:T(8,128)(2,1)S(1)} %bitcast.224, ...), custom_call_target="tpu_custom_call" | custom-call | bytes 157286400 | tf_op jit(solution)/shard_map/latent_sum/pallas_call | solution.py:441
  231.3 13.0 %attend.1 = (bf16[8,2,64,640]{3,2,1,0:T(8,128)(2,1)}, bf16[8,2,64,640]{3,2,1,0:T(8,128)(2,1)}, bf16[320,1024]{1,0:T(8,128)(2,1)}, f32[8,2,64,128]{3,2,1,0:T(8,128)}) custom-call(s32[2]{0:T(128)} %length_ref.3, bf16[8,2,64,1152]{3,2,1,0:T(8,128)(2,1)} %bitcast.211, bf16[768,640]{1,0:T(8,128)(2,1)} %bitcast.265, ...), custom_call_target="tpu_custom_call" | custom-call | tf_op jit(solution)/shard_map/attend/pallas_call | solution.py:561
  245.4 57.7 %attn_gather.1 = (bf16[8,320,1024]{2,1,0:T(8,128)(2,1)S(1)}, bf16[4,640,800]{2,1,0:T(8,128)(2,1)S(1)}) custom-call(bf16[320,1024]{1,0:T(8,128)(2,1)S(1)} %copy-done.27, bf16[640,800]{1,0:T(8,128)(2,1)S(1)} %bitcast.232), custom_call_target="tpu_custom_call" | custom-call | bytes 157286400 | tf_op jit(solution)/shard_map/attn_gather/pallas_call | solution.py:441
  314.3 25.7 %branch_exchange.1 = (bf16[8,2,64,320]{3,2,1,0:T(8,128)(2,1)S(1)}, bf16[4,640,320]{2,1,0:T(8,128)(2,1)S(1)}) custom-call(bf16[2,8,64,320]{3,2,1,0:T(8,128)(2,1)S(1)} %bitcast.221, bf16[640,320]{1,0:T(8,128)(2,1)S(1)} %bitcast.233), custom_call_target="tpu_custom_call" | custom-call | bytes 157286400 | tf_op jit(solution)/shard_map/branch_exchange/pallas_call | solution.py:441
  368.7 54.5 %mid_gather.1 = (bf16[8,128,2560]{2,1,0:T(8,128)(2,1)S(1)}, bf16[4,640,800]{2,1,0:T(8,128)(2,1)S(1)}) custom-call(bf16[128,2560]{1,0:T(8,128)(2,1)S(1)} %multiply_convert_fusion.6.refs_0_, bf16[640,800]{1,0:T(8,128)(2,1)S(1)} %bitcast.231), custom_call_target="tpu_custom_call" | custom-call | bytes 157286400 | tf_op jit(solution)/shard_map/mid_gather/pallas_call | solution.py:441
  423.3 12.0 %fusion.47 = f32[1024,800]{0,1:T(8,128)} fusion(bf16[1024,2560]{1,0:T(8,128)(2,1)S(1)} %bitcast.239, bf16[2560,800]{1,0:T(8,128)(2,1)} %bitcast.243), kind=kOutput, calls=%fused_computation.138 | convolution fusion | flops 4194304000 | bytes 12615680 | tf_op jit(solution)/shard_map/dot_general | solution.py:33
  435.2 6.4 fusion.48
  441.7 11.3 %multiply_convert_fusion = (bf16[1024,800]{0,1:T(8,128)(2,1)S(1)}, bf16[1024,800]{0,1:T(8,128)(2,1)S(1)}, bf16[1024,800]{0,1:T(8,128)(2,1)S(1)}) fusion(f32[1024,800]{0,1:T(8,128)} %fusion.47, f32[1024,800]{0,1:T(8,128)} %fusion.48, bf16[1024,2560]{1,0:T(8,128)(2,1)} %all-gather.8.cloned.1.call-done, bf16[800,2560]{1,0:T(8,128)(2,1)} %all-gather.6.cloned.1.call-done), kind=kOutput, calls=%fused_computation.11 | convolution fusion | flops 4206592000 | bytes 20807680 | tf_op jit(solution)/shard_map/dot_general | solution.py:33
  453.0 11.1 %fusion.49 = f32[1024,2560]{1,0:T(8,128)} fusion(bf16[1024,800]{0,1:T(8,128)(2,1)S(1)} %get-tuple-element.101, bf16[2560,800]{1,0:T(8,128)(2,1)} %bitcast.244), kind=kOutput, calls=%fused_computation.140 | convolution fusion | flops 4194304000 | bytes 16220160 | tf_op jit(solution)/shard_map/dot_general | solution.py:33
  464.2 5.9 convolution_convert_fusion.2
  470.1 7.6 convolution_convert_fusion
  477.7 8.4 convolution_convert_fusion.1
  486.1 7.2 copy.85
  493.3 7.3 copy.86
  500.7 11.8 %add_convert_fusion = bf16[1024,2560]{1,0:T(8,128)(2,1)} fusion(f32[1024,2560]{1,0:T(8,128)} %fusion.49, bf16[1024,800]{0,1:T(8,128)(2,1)S(1)} %get-tuple-element.100, bf16[2560,800]{1,0:T(8,128)(2,1)} %bitcast.246), kind=kOutput, calls=%fused_computation | convolution fusion | flops 4199546880 | bytes 21463040 | tf_op jit(solution)/shard_map/dot_general | solution.py:33
  512.5 66.2 %mid_scatter.1 = (f32[128,2560]{1,0:T(8,128)S(1)}, bf16[4,640,800]{2,1,0:T(8,128)(2,1)S(1)}) custom-call(bf16[8,128,2560]{2,1,0:T(8,128)(2,1)} %bitcast.259, bf16[4,640,800]{2,1,0:T(8,128)(2,1)S(1)} %bitcast.216), custom_call_target="tpu_custom_call" | custom-call | bytes 157286400 | tf_op jit(solution)/shard_map/mid_scatter/pallas_call | solution.py:441
  582.8 55.6 %branch_gather.1 = (bf16[8,128,2560]{2,1,0:T(8,128)(2,1)S(1)}, bf16[4,640,800]{2,1,0:T(8,128)(2,1)S(1)}) custom-call(bf16[128,2560]{1,0:T(8,128)(2,1)S(1)} %multiply_convert_fusion.5.refs_0_, bf16[4,640,800]{2,1,0:T(8,128)(2,1)S(1)} %bitcast.213), custom_call_target="tpu_custom_call" | custom-call | bytes 157286400 | tf_op jit(solution)/shard_map/branch_gather/pallas_call | solution.py:441
  640.5 5.3 convolution_convert_fusion.7
  645.8 13.6 %attend_back.1 = (bf16[8,2,64,640]{3,2,1,0:T(8,128)(2,1)}, f32[8,2,64,640]{3,2,1,0:T(8,128)}, f32[8,2,64,128]{3,2,1,0:T(8,128)}) custom-call(s32[2]{0:T(128)} %length_ref.3, bf16[8,2,64,640]{3,2,1,0:T(8,128)(2,1)} %get-tuple-element.76.query_ref, bf16[8,2,64,640]{3,2,1,0:T(8,128)(2,1)} %get-tuple-element.77.kv_ref, bf16[8,2,64,1152]{3,2,1,0:T(8,128)(2,1)} %bitcast.212, ...), custom_call_target="tpu_custom_call" | custom-call | tf_op jit(solution)/shard_map/attend_back/pallas_call | solution.py:591
  680.8 6.0 convolution_convert_fusion.3
  686.8 87.7 %latent_sum_back.1 = (f32[128,1152]{1,0:T(8,128)S(1)}, bf16[8,128,1152]{2,1,0:T(8,128)(2,1)S(1)}, bf16[4,256,640]{2,1,0:T(8,128)(2,1)S(1)}, bf16[4,200,2560]{2,1...) custom-call(bf16[8,128,1152]{2,1,0:T(8,128)(2,1)S(1)} %pad_maximum_fusion.refs_0_, ...), custom_call_target="tpu_custom_call" | custom-call | bytes 157286400 | tf_op jit(solution)/shard_map/latent_sum_back/pallas_call | solution.py:441
  801.9 46.1 %close.1 = (bf16[8,128,320]{2,1,0:T(8,128)(2,1)S(1)}, f32[4,80,1152]{2,1,0:T(8,128)S(1)}, bf16[4,80,2560]{2,1,0:T(8,128)(2,1)S(1)}, bf16[8,32,640]{2,1,0:T(8,128)(2,1)S(1)}, f32[4,8,8,128]{3,2,1,0:T(8,128)S(1)}) custom-call(bf16[8,128,320]{2,1,0:T(8,128)(2,1)S(1)} %bitcast.222, f32[4,80,1152]{2,1,0:T(8,128)S(1)} %pad_maximum_fusion.1.refs_1_, ...), custom_call_target="tpu_custom_call" | custom-call | bytes 157286400 | tf_op jit(solution)/shard_map/close/pallas_call | solution.py:441
  (345 shorter events, 197.7 us)
Async XLA Ops:
  7.2 300.8 %all-gather.4.cloned.1.call-start = ((), (), s32[]{:S(2)}) async-start(), calls=%async_computation.1 | async-start | bytes 2048000 | tf_op jit(solution)/shard_map/all_gather | solution.py:52
  12.7 39.6 %copy-start.52 = (bf16[2,64,2560]{2,1,0:T(8,128)(2,1)S(1)}, bf16[2,64,2560]{2,1,0:T(8,128)(2,1)}, u32[]{:S(2)}) copy-start(bf16[2,64,2560]{2,1,0:T(8,128)(2,1)} %param.17) | copy-start | bytes 1966084
  51.6 390.1 %all-gather.6.cloned.1.call-start = ((), (), s32[]{:S(2)}) async-start(), calls=%async_computation.2 | async-start | bytes 5120000 | tf_op jit(solution)/shard_map/all_gather | solution.py:52
  52.3 389.3 %all-gather.8.cloned.1.call-start = ((), (), s32[]{:S(2)}) async-start(), calls=%async_computation.4 | async-start | bytes 5898240 | tf_op jit(solution)/shard_map/all_gather | solution.py:60
  53.4 849.7 %reduce-scatter.2.cloned.1.call-start = ((), (), s32[]{:S(2)}) async-start(), calls=%async_computation.3 | async-start | bytes 5898240 | tf_op jit(solution)/shard_map/reduce_scatter | solution.py:64
  231.3 13.0 %copy-start.24 = (bf16[8,80,800]{2,1,0:T(8,128)(2,1)S(1)}, bf16[8,80,800]{2,1,0:T(8,128)(2,1)}, u32[]{:S(2)}) copy-start(bf16[8,80,800]{2,1,0:T(8,128)(2,1)} %copy-done.23) | copy-start | bytes 3072004
  244.3 63.4 %copy-start.7 = (f32[128,1152]{1,0:T(8,128)S(1)}, f32[128,1152]{1,0:T(8,128)}, u32[]{:S(2)}) copy-start(f32[128,1152]{1,0:T(8,128)} %copy-done.6) | copy-start | bytes 1769476
  423.2 12.0 %copy-start.35 = (bf16[8,128,2560]{2,1,0:T(8,128)(2,1)}, bf16[8,128,2560]{2,1,0:T(8,128)(2,1)S(1)}, u32[]{:S(2)}) copy-start(bf16[8,128,2560]{2,1,0:T(8,128)(2,1)S(1)} %get-tuple-element.72) | copy-start | bytes 15728644
  423.2 12.0 %copy-start.38 = (bf16[4,640,800]{2,1,0:T(8,128)(2,1)}, bf16[4,640,800]{2,1,0:T(8,128)(2,1)S(1)}, u32[]{:S(2)}) copy-start(bf16[4,640,800]{2,1,0:T(8,128)(2,1)S(1)} %get-tuple-element.74) | copy-start | bytes 12288004
  453.0 17.1 %copy-start.85 = (bf16[1024,800]{0,1:T(8,128)(2,1)}, bf16[1024,800]{0,1:T(8,128)(2,1)S(1)}, u32[]{:S(2)}) copy-start(bf16[1024,800]{0,1:T(8,128)(2,1)S(1)} %get-tuple-element.102) | copy-start | bytes 4915204
  453.0 11.2 %copy-start.36 = (bf16[8,128,2560]{2,1,0:T(8,128)(2,1)S(1)}, bf16[8,128,2560]{2,1,0:T(8,128)(2,1)}, u32[]{:S(2)}) copy-start(bf16[8,128,2560]{2,1,0:T(8,128)(2,1)} %copy-done.35) | copy-start | bytes 15728644
  464.2 5.9 copy-start.83
  493.3 19.2 %slice-start = ((s8[4587520]{0:T(1024)(128)(4,1)}), s8[393216]{0:T(1024)(128)(4,1)S(1)}, s32[]{:S(2)}) async-start(s8[4587520]{0:T(1024)(128)(4,1)} %bitcast.214), calls=%async_computation.5 | async-start | bytes 786432
  500.7 11.8 %slice-start.1 = ((s8[4587520]{0:T(1024)(128)(4,1)}), s8[4194304]{0:T(1024)(128)(4,1)S(1)}, s32[]{:S(2)}) async-start(s8[4587520]{0:T(1024)(128)(4,1)} %bitcast.214), calls=%async_computation.6 | async-start | bytes 8388608
  512.5 66.2 %copy-start.43 = (f32[128,2560]{1,0:T(8,128)S(1)}, f32[128,2560]{1,0:T(8,128)}, u32[]{:S(2)}) copy-start(f32[128,2560]{1,0:T(8,128)} %copy.83) | copy-start | bytes 3932164
  512.5 66.2 %copy-start.47 = (bf16[2,64,2560]{2,1,0:T(8,128)(2,1)S(1)}, bf16[2,64,2560]{2,1,0:T(8,128)(2,1)}, u32[]{:S(2)}) copy-start(bf16[2,64,2560]{2,1,0:T(8,128)(2,1)} %param.15) | copy-start | bytes 1966084
  578.7 59.7 %copy-start.4 = (bf16[4,640,800]{2,1,0:T(8,128)(2,1)}, bf16[4,640,800]{2,1,0:T(8,128)(2,1)S(1)}, u32[]{:S(2)}) copy-start(bf16[4,640,800]{2,1,0:T(8,128)(2,1)S(1)} %get-tuple-element.84) | copy-start | bytes 12288004
  582.8 57.7 %copy-start.56 = (bf16[2560,5,128]{0,2,1:T(8,128)(2,1)S(1)}, bf16[2560,5,128]{0,2,1:T(8,128)(2,1)}, u32[]{:S(2)}) copy-start(bf16[2560,5,128]{0,2,1:T(8,128)(2,1)} %pad.29) | copy-start | bytes 9830404
  638.4 7.4 copy-start.34
  680.8 6.0 copy-start.2
  680.8 6.0 copy-start.12
  686.8 87.8 %copy-start.41 = (bf16[4,80,1152]{2,1,0:T(8,128)(2,1)S(1)}, bf16[4,80,1152]{2,1,0:T(8,128)(2,1)}, u32[]{:S(2)}) copy-start(bf16[4,80,1152]{2,1,0:T(8,128)(2,1)} %copy-done.39) | copy-start | bytes 2211844
  686.8 87.8 %copy-start.62 = (f32[1024,320]{0,1:T(8,128)S(1)}, f32[1024,320]{0,1:T(8,128)}, u32[]{:S(2)}) copy-start(f32[1024,320]{0,1:T(8,128)} %copy.92) | copy-start | bytes 3932164
  686.8 87.8 %copy-start.70 = (f32[320]{0:T(512)S(1)}, f32[320]{0:T(512)}, u32[]{:S(2)}) copy-start(f32[320]{0:T(512)} %mul.277) | copy-start | bytes 3844
  (74 other events, 166.5 us)
Sparse Core Ops, SparseCore 0:
  51.7 32.1 all-gather.3
  85.7 59.2 all-gather.5
  146.6 63.5 all-gather.7
  477.8 54.8 reduce-scatter.1

commit v3 on v2

v3 whole, which is shorter than its diff:
```python
import functools

import jax
import jax.numpy as jnp
from jax import lax
from jax.experimental import pallas as pl
from jax.experimental.pallas import tpu as pltpu
from jax.sharding import PartitionSpec as P

D = 2560
FF = 6400
HEADS = 40
QRANK = 768
KVRANK = 256
NOPE = 64
ROPE = 32
VDIM = 64

LANES = 128
LATENT = QRANK + KVRANK + LANES

epsilon = 1e-05
branch_scale = 1.4 / 62**0.5
score_scale = 1.0 / (NOPE + ROPE) ** 0.5
neg_large = -1e30
bfloat = jnp.bfloat16
MESH = pl.DeviceIdType.MESH
single = jnp.float32
highest = lax.Precision.HIGHEST


def dot(left, right, left_dim=1, right_dim=0, precision=None):
    return lax.dot_general(
        left,
        right,
        (((left_dim,), (right_dim,)), ((), ())),
        precision=precision,
        preferred_element_type=single,
    )


def normalize(values):
    factor = lax.rsqrt(jnp.mean(values * values, axis=-1, keepdims=True) + epsilon)
    return (values * factor, factor)


def norm_back(grad_scaled, normed, factor):
    return factor * (grad_scaled - normed * jnp.mean(grad_scaled * normed, axis=-1, keepdims=True))


def gather_dp(values):
    return lax.all_gather(values, "dp", axis=0, tiled=True)


def scatter_dp(values):
    return lax.psum_scatter(values, "dp", scatter_dimension=0, tiled=True)


def gather_xla(values):
    return lax.all_gather(values, "ctx", axis=0, tiled=True)


def scatter_xla(values):
    return lax.psum_scatter(values, "ctx", scatter_dimension=0, tiled=True)


def exchange_xla(values):
    return lax.all_to_all(values, "ctx", 0, 0, tiled=True)


class Line:
    def __init__(self, ctx):
        self.pairs = ctx // 2
        self.place = lax.axis_index("ctx")
        self.pair, self.core = self.place // 2, self.place % 2
        self.has_left, self.has_right = self.pair > 0, self.pair < self.pairs - 1
        self.left = {"ctx": jnp.maximum(self.place - 2, 0)}
        self.right = {"ctx": jnp.minimum(self.place + 2, ctx - 1)}
        self.twin = {"ctx": self.place + 1 - 2 * self.core}


def remote(source, target, send, receive, device):
    return pltpu.make_async_remote_copy(
        src_ref=source, dst_ref=target, send_sem=send, recv_sem=receive,
        device_id=device, device_id_type=MESH,
    )


def nothing():
    pass


def gather_line(line, own_ref, all_ref, sems, idle=nothing):
    send_left, send_right, send_twin, receive, receive_twin, local = sems
    pairs, pair, core = line.pairs, line.pair, line.core

    def to_side(source, slot, sem, device):
        return remote(source, all_ref.at[slot * 2 + core], sem.at[slot], receive.at[slot], device)

    def to_twin(source, slot):
        return remote(source, all_ref.at[slot * 2 + core], send_twin.at[slot], receive_twin.at[slot], line.twin)

    pl.when(line.has_right)(lambda: to_side(own_ref, pair, send_right, line.right).start())
    pl.when(line.has_left)(lambda: to_side(own_ref, pair, send_left, line.left).start())
    to_twin(own_ref, pair).start()
    keep = pltpu.make_async_copy(own_ref, all_ref.at[line.place], local)
    keep.start()
    for step in range(1, pairs):
        idle()

        def from_left(slot=pair - step):
            block = all_ref.at[slot * 2 + core]
            to_side(block, slot, send_left, line.left).wait_recv()
            pl.when(line.has_right)(lambda: to_side(block, slot, send_right, line.right).start())
            to_twin(block, slot).start()

        def from_right(slot=pair + step):
            block = all_ref.at[slot * 2 + core]
            to_side(block, slot, send_right, line.right).wait_recv()
            pl.when(line.has_left)(lambda: to_side(block, slot, send_left, line.left).start())
            to_twin(block, slot).start()

        pl.when(pair - step >= 0)(from_left)
        pl.when(pair + step < pairs)(from_right)
    keep.wait()
    for slot in range(pairs):
        to_twin(own_ref, slot).wait()
        pl.when((slot <= pair) & line.has_right)(
            lambda slot=slot: to_side(own_ref, slot, send_right, line.right).wait_send())
        pl.when((slot >= pair) & line.has_left)(
            lambda slot=slot: to_side(own_ref, slot, send_left, line.left).wait_send())


def comm_params(collective_id, mebibytes):
    return pltpu.CompilerParams(
        collective_id=collective_id, has_side_effects=True, vmem_limit_bytes=mebibytes << 20
    )


def link_cost(size):
    return pl.CostEstimate(flops=0, transcendentals=0, bytes_accessed=size)


def scatter_line(line, parts_ref, twin_ref, landed_ref, sems, idle=nothing, make=None):
    send_twin, receive_twin, send_left, send_right, from_left, from_right = sems
    pairs, pair = line.pairs, line.pair
    to_twin, to_right, to_left = travels(line, parts_ref, twin_ref, landed_ref, sems)

    def both_cores(slot):
        return parts_ref[slot * 2 + line.core].astype(single) + twin_ref[slot].astype(single)

    def prepare(order):
        ahead = (pair + pairs - 1 - order) % pairs
        slot = jnp.where(pair < pairs // 2, ahead, (pair + 1 + order) % pairs)
        if make:
            make(slot)
        to_twin(slot).start()

    todo = list(range(pairs))
    for _ in range(2 if make else pairs):
        prepare(todo.pop(0))
    for step in range(pairs - 1, 0, -1):
        idle()

        def pass_on(slot, arrives, travel):
            to_twin(slot).wait_recv()

            @pl.when(arrives)
            def _():
                travel(slot).wait_recv()
                total = both_cores(slot) + landed_ref[slot].astype(single)
                twin_ref[slot] = total.astype(twin_ref.dtype)

            @pl.when(jnp.logical_not(arrives))
            def _():
                twin_ref[slot] = both_cores(slot).astype(twin_ref.dtype)

            travel(slot).start()

        pl.when(pair + step < pairs)(lambda slot=pair + step: pass_on(slot, line.has_left, to_right))
        pl.when(pair - step >= 0)(lambda slot=pair - step: pass_on(slot, line.has_right, to_left))
        if todo:
            prepare(todo.pop(0))
    to_twin(pair).wait_recv()


def travels(line, parts_ref, twin_ref, landed_ref, sems):
    send_twin, receive_twin, send_left, send_right, from_left, from_right = sems
    pairs = line.pairs

    def to_twin(slot):
        source = parts_ref.at[slot * 2 + 1 - line.core]
        return remote(source, twin_ref.at[slot], send_twin.at[slot], receive_twin.at[slot], line.twin)

    def to_right(slot):
        return remote(
            twin_ref.at[slot], landed_ref.at[slot], send_right.at[slot], from_left.at[slot], line.right
        )

    def to_left(slot):
        goal = jnp.where(slot == line.pair - 1, pairs, slot)
        return remote(
            twin_ref.at[slot], landed_ref.at[goal], send_left.at[slot], from_right.at[slot], line.left
        )

    return (to_twin, to_right, to_left)


def scatter_total(line, parts_ref, twin_ref, landed_ref, sems, out_ref):
    pairs, pair = line.pairs, line.pair
    to_twin, to_right, to_left = travels(line, parts_ref, twin_ref, landed_ref, sems)
    out_ref[...] = parts_ref[pair * 2 + line.core].astype(single) + twin_ref[pair].astype(single)

    @pl.when(line.has_left)
    def _():
        to_right(pair).wait_recv()
        out_ref[...] += landed_ref[pair].astype(single)

    @pl.when(line.has_right)
    def _():
        to_left(pair).wait_recv()
        out_ref[...] += landed_ref[pairs].astype(single)

    for slot in range(pairs):
        to_twin(slot).wait_send()
        pl.when(slot > pair)(lambda slot=slot: to_right(slot).wait_send())
        pl.when(slot < pair)(lambda slot=slot: to_left(slot).wait_send())


def gather_sems(ctx):
    return [pltpu.SemaphoreType.DMA((ctx // 2,))] * 5 + [pltpu.SemaphoreType.DMA]


def scatter_scratch(ctx, shape, dtype):
    pairs = ctx // 2
    slots = [pltpu.VMEM((count,) + shape, dtype) for count in (pairs, pairs + 1)]
    return slots + [pltpu.SemaphoreType.DMA((pairs,))] * 6


def pair_sems(count):
    return [pltpu.SemaphoreType.DMA((count,))] * 2 + [pltpu.SemaphoreType.DMA]


class ExchangeCtx:
    reach = "ctx"

    def __init__(self, dp, ctx, parts):
        self.count, self.parts = ctx, parts
        self.axis = len(parts.shape) - 3
        shape = parts.shape if not self.axis else (ctx, parts.shape[0]) + parts.shape[2:]
        self.result = jax.ShapeDtypeStruct(shape, parts.dtype)
        self.scratch = pair_sems(ctx)

    def copies(self, source, target, send, receive, local):
        place = lax.axis_index("ctx")

        def part(index):
            return source.at[:, index] if self.axis else source.at[index]

        out = [pltpu.make_async_copy(part(place), target.at[place], local)]
        for step in range(1, self.count):
            other = (place + step) % self.count
            out.append(
                remote(
                    part(other), target.at[place], send.at[step], receive.at[step], {"ctx": other}
                )
            )
        return out


class ExchangeDp:
    reach = "dp"
    whole = False

    def __init__(self, dp, ctx, parts):
        self.count, self.parts = dp, parts
        shape = (dp,) + parts.shape if self.whole else parts.shape
        self.result = jax.ShapeDtypeStruct(shape, parts.dtype)
        self.scratch = pair_sems(dp)

    def copies(self, source, target, send, receive, local):
        row = lax.axis_index("dp")

        def part(index):
            return source if self.whole else source.at[index]

        out = [pltpu.make_async_copy(part(row), target.at[row], local)]
        for step in range(1, self.count):
            other = (row + step) % self.count
            out.append(
                remote(part(other), target.at[row], send.at[step], receive.at[step], {"dp": other})
            )
        return out


class GatherDp(ExchangeDp):
    whole = True


class ExchangeAll:
    reach = "all"
    whole = False

    def __init__(self, dp, ctx, parts):
        self.dp, self.ctx, self.parts = dp, ctx, parts
        shape = (dp, ctx) + parts.shape if self.whole else parts.shape
        self.result = jax.ShapeDtypeStruct(shape, parts.dtype)
        self.scratch = pair_sems(dp * ctx)

    def copies(self, source, target, send, receive, local):
        row, place = lax.axis_index("dp"), lax.axis_index("ctx")

        def part(index):
            return source if self.whole else source.at[index[0], index[1]]

        out = [pltpu.make_async_copy(part((row, place)), target.at[row, place], local)]
        for index, other in enumerate(everyone(self.dp, self.ctx)):
            out.append(
                remote(
                    part(other), target.at[row, place], send.at[index], receive.at[index],
                    {"dp": other[0], "ctx": other[1]},
                )
            )
        return out


class GatherAll(ExchangeAll):
    whole = True


class GatherLine:
    reach = "ctx"
    held = False
    extra_held = True

    def __init__(self, dp, ctx, parts):
        self.parts = parts
        self.result = [jax.ShapeDtypeStruct((ctx,) + parts.shape, parts.dtype)]
        self.in_vmem = [False]
        self.scratch = gather_sems(ctx)

    def run(self, line, extra, source, results, sems):
        gather_line(line, source, results[0], sems)


class LatentLine:
    reach = "ctx"
    held = True

    def __init__(self, dp, ctx, parts):
        shape = parts.shape[1:]
        self.parts = parts
        self.result = [
            jax.ShapeDtypeStruct(shape, single), jax.ShapeDtypeStruct(parts.shape, bfloat)
        ]
        self.in_vmem = [True, False]
        self.scratch = [pltpu.VMEM(shape, bfloat)] + scatter_scratch(ctx, shape, bfloat) + gather_sems(ctx)

    def finish_own(self, extra, sums_ref, own_ref):
        gain_ref, table_ref = extra
        for span in (QUERY_SPAN, LATENT_SPAN):
            normed, _ = normalize(sums_ref[:, span])
            own_ref[:, span] = (normed * gain_ref[:, span]).astype(bfloat)
        own_ref[:, ROPE_SPAN] = turn(sums_ref[:, ROPE_SPAN], table_ref, 1.0).astype(bfloat)

    def run(self, line, extra, source, results, scratch):
        sums_ref, all_ref = results
        own_ref = scratch[0]
        scatter_line(line, source, *scratch[1:3], scratch[3:9])
        scatter_total(line, source, *scratch[1:3], scratch[3:9], sums_ref)
        self.finish_own(extra, sums_ref, own_ref)
        gather_line(line, own_ref, all_ref, scratch[9:])


class ForwardLine(LatentLine):
    reach = "both"

    def __init__(self, dp, ctx, parts, heads, batch, matrices, ups, out_own, out_heads):
        super().__init__(dp, ctx, parts)
        own = parts.shape[1]
        rows, width = matrices[0].shape
        group, wide = ctx * own, heads * LANES
        self.dp, self.ctx, self.heads, self.batch = dp, ctx, heads, batch
        self.cut = (ctx, rows, width // ctx)
        self.pieces = {
            "gate": ExchangeCtx(dp, ctx, jax.ShapeDtypeStruct(self.cut, bfloat)),
            "up": ExchangeCtx(dp, ctx, jax.ShapeDtypeStruct(self.cut, bfloat)),
            "heads": ExchangeCtx(dp, ctx, out_heads),
            "queries": GatherDp(dp, ctx, ups[0]),
            "latents": GatherDp(dp, ctx, ups[1]),
            "rows": GatherDp(dp, ctx, out_own),
            "gates": GatherDp(dp, ctx, jax.ShapeDtypeStruct(self.cut, bfloat)),
        }
        self.result += [
            jax.ShapeDtypeStruct((ctx, own, wide), bfloat),
            jax.ShapeDtypeStruct((ctx, own, wide), bfloat),
            jax.ShapeDtypeStruct((ctx, own, LANES), single),
            jax.ShapeDtypeStruct((ctx, heads * VDIM, group), bfloat),
        ]
        self.result += [
            self.pieces[name].result for name in ("queries", "latents", "rows", "gates", "up", "heads")
        ]
        self.in_vmem = [True, True, True, True, True, False, True, True] + [False] * 4
        self.base = len(self.scratch)
        self.scratch = self.scratch + [
            pltpu.VMEM((2,) + self.cut, bfloat), pltpu.VMEM(self.cut, bfloat),
            pltpu.VMEM((heads * VDIM, group), bfloat),
        ]
        for piece in self.pieces.values():
            self.scratch = self.scratch + piece.scratch
        self.scratch = self.scratch + gather_sems(ctx)

    def run(self, line, extra, source, results, scratch):
        gain_ref, table_ref, length_ref, slot_table_ref = extra[:4]
        matrices, ups, out_own_ref, out_heads_ref = extra[4:6], extra[6:8], extra[8], extra[9]
        sums_ref, all_ref, query_ref, kv_ref, total_ref, attn_all_ref = results[:6]
        query_ups_ref, latent_ups_ref, rows_ref, gates_ref, up_ref, heads_ref = results[6:]
        cut_ref, gate_ref, attn_ref = scratch[self.base : self.base + 3]
        later = list(scratch[self.base + 3 :])
        ends = {
            "gate": (cut_ref.at[0], gate_ref), "up": (cut_ref.at[1], up_ref),
            "heads": (out_heads_ref, heads_ref), "queries": (ups[0], query_ups_ref),
            "latents": (ups[1], latent_ups_ref), "rows": (out_own_ref, rows_ref),
            "gates": (gate_ref, gates_ref),
        }
        copies = {}
        for name, piece in self.pieces.items():
            copies[name] = piece.copies(*ends[name], *later[: len(piece.scratch)])
            del later[: len(piece.scratch)]

        def start(*names):
            for name in names:
                for copy in copies[name]:
                    copy.start()

        def wait(*names):
            for name in names:
                for copy in copies[name]:
                    copy.wait()

        todo = ["gate", "up"]

        def idle():
            while todo:
                name = todo.pop(0)
                index = 1 - len(todo)
                regroup(matrices[index], cut_ref.at[index], self.dp, self.ctx, True)
                start(name)

        start("queries", "latents", "rows")
        scatter_line(line, source, *scratch[1:3], scratch[3:9], idle)
        scatter_total(line, source, *scratch[1:3], scratch[3:9], sums_ref)
        self.finish_own((gain_ref, table_ref), sums_ref, scratch[0])
        gather_line(line, scratch[0], all_ref, scratch[9 : self.base])
        wait("queries", "latents")
        start("heads")

        def slot(index, carry):
            attend_slot(
                self.heads, index, self.batch, length_ref, all_ref, query_ups_ref, latent_ups_ref,
                slot_table_ref, query_ref, kv_ref, attn_ref, total_ref,
            )
            return carry

        lax.fori_loop(0, self.batch, slot, 0)
        wait("gate")
        start("gates")
        gather_line(line, attn_ref, attn_all_ref, later)
        wait("up", "heads", "rows", "gates")


class BackwardLine(LatentLine):
    reach = "both"

    def __init__(self, dp, ctx, branch, heads, batch, columns):
        own = branch.shape[1]
        parts = jax.ShapeDtypeStruct((ctx, own, LATENT), bfloat)
        super().__init__(dp, ctx, parts)
        self.parts = branch
        self.dp, self.ctx, self.heads, self.batch = dp, ctx, heads, batch
        rows, wide = D // (dp * ctx), heads * LANES
        self.ups = [
            ExchangeDp(dp, ctx, jax.ShapeDtypeStruct((dp, rank // dp, wide), bfloat))
            for rank in (QRANK, KVRANK)
        ]
        self.result += [jax.ShapeDtypeStruct((dp, rows, columns), bfloat)]
        self.result += [piece.result for piece in self.ups]
        self.in_vmem += [True, False, False]
        self.base = len(self.scratch)
        total = ctx * own // batch
        self.scratch = self.scratch + [
            pltpu.VMEM((ctx * own, rows), bfloat), pltpu.VMEM(parts.shape, bfloat),
        ]
        self.scratch = self.scratch + [pltpu.VMEM((total, wide), bfloat)] * 3
        self.scratch = self.scratch + [pltpu.VMEM((rank, wide), single) for rank in (QRANK, KVRANK)]
        self.scratch = self.scratch + [pltpu.VMEM(piece.parts.shape, bfloat) for piece in self.ups]
        for piece in self.ups:
            self.scratch = self.scratch + piece.scratch

    def run(self, line, extra, source, results, scratch):
        branch_ref, attn_ref = source, extra[3]
        parts_ref = scratch[self.base + 1]
        work_refs = scratch[self.base + 2 : self.base + 5]
        sum_refs = scratch[self.base + 5 : self.base + 7]
        send_refs = scratch[self.base + 7 : self.base + 9]
        sems = scratch[self.base + 9 :]
        for ref in sum_refs:
            ref[...] = jnp.zeros_like(ref)

        def slot(index, carry):
            attend_back_slot(
                self.heads, index, self.batch, extra[4], extra[5], extra[6], extra[7], extra[8],
                branch_ref, *extra[9:13], parts_ref, *work_refs, *sum_refs,
            )
            return carry

        lax.fori_loop(0, self.batch, slot, 0)
        copies = []
        for index, piece in enumerate(self.ups):
            send_refs[index][...] = sum_refs[index][...].astype(bfloat).reshape(piece.parts.shape)
            copies += piece.copies(
                send_refs[index], results[3 + index], *sems[3 * index : 3 * index + 3]
            )
        for copy in copies:
            copy.start()
        out_ref, slice_ref = results[2], scratch[self.base]
        rows = D // (self.dp * self.ctx)
        height = D // self.dp
        own = branch_ref.shape[1]
        span = own // self.batch

        def work(index):
            row = lax.broadcasted_iota(jnp.int32, (height, rows), 0)
            col = lax.broadcasted_iota(jnp.int32, (height, rows), 1)
            chosen = (row == line.place * rows + col).astype(single).astype(bfloat)
            block = branch_ref[:, :, index * height : (index + 1) * height]
            picked = dot(block.reshape(self.ctx * own, height), chosen).astype(bfloat)
            for place in range(self.ctx):
                for slot in range(self.batch):
                    start = (place * self.batch + slot) * span
                    goal = (slot * self.ctx + place) * span
                    slice_ref[goal : goal + span] = picked[start : start + span]
            columns = out_ref.shape[2]
            out_ref[index] = dot(slice_ref[...].T, attn_ref[:columns], 1, 1).astype(bfloat)

        todo = list(range(self.dp))

        def idle():
            if todo:
                work(todo.pop(0))

        sums_ref, all_ref = results[:2]
        own_ref = scratch[0]
        scatter_line(line, parts_ref, *scratch[1:3], scratch[3:9], idle)
        scatter_total(line, parts_ref, *scratch[1:3], scratch[3:9], sums_ref)
        self.finish_own(extra[:3], sums_ref, own_ref)
        gather_line(line, own_ref, all_ref, scratch[9 : self.base], idle)
        while todo:
            idle()
        for copy in copies:
            copy.wait()

    def finish_own(self, extra, sums_ref, own_ref):
        gain_ref, table_ref, latents_ref = extra
        for span in (QUERY_SPAN, LATENT_SPAN):
            normed, factor = normalize(latents_ref[:, span])
            scaled = sums_ref[:, span] * gain_ref[:, span]
            own_ref[:, span] = norm_back(scaled, normed, factor).astype(bfloat)
        own_ref[:, ROPE_SPAN] = turn(sums_ref[:, ROPE_SPAN], table_ref, -1.0).astype(bfloat)


class MiddleLine:
    reach = "ctx"
    held = False

    def __init__(self, dp, ctx, parts):
        self.dp, self.ctx, self.parts = dp, ctx, parts
        own, cut = parts.shape[0] * parts.shape[2], parts.shape[3]
        self.result = [
            jax.ShapeDtypeStruct((own, D), single), jax.ShapeDtypeStruct((ctx, own, D), bfloat)
        ]
        self.in_vmem = [True, False]
        self.scratch = (
            [pltpu.VMEM((ctx, parts.shape[0], parts.shape[2], cut), bfloat), pltpu.VMEM((own, D), bfloat)]
            + pair_sems(ctx) + gather_sems(ctx)
        )

    def run(self, line, extra, source, results, scratch):
        tokens_ref, gain_ref = extra
        middle_ref, all_ref = results
        landed_ref, own_ref = scratch[:2]
        copies = ExchangeCtx(self.dp, self.ctx, self.parts).copies(source, landed_ref, *scratch[2:5])
        for copy in copies:
            copy.start()
        for copy in copies:
            copy.wait()
        ungroup(landed_ref, middle_ref, self.dp, self.ctx)

        def chunk(rows):
            middle = tokens_ref[rows].astype(single) + branch_scale * middle_ref[rows]
            middle_ref[rows] = middle
            normed, _ = normalize(middle)
            own_ref[rows] = (normed * gain_ref[...]).astype(bfloat)

        by_chunks(own_ref.shape[0], chunk)
        gather_line(line, own_ref, all_ref, scratch[5:])


class MiddleBackLine:
    reach = "both"
    held = True

    def __init__(self, dp, ctx, parts, shape, f_part, fused):
        self.dp, self.ctx, self.parts, self.fused = dp, ctx, parts, fused
        own = shape[0]
        self.cut = (dp, D // dp, f_part)
        self.f_part = f_part
        self.result = [
            jax.ShapeDtypeStruct(shape, single),
            jax.ShapeDtypeStruct((1, D), single),
            jax.ShapeDtypeStruct((ctx, own, D), bfloat),
            jax.ShapeDtypeStruct((f_part, D), bfloat),
            jax.ShapeDtypeStruct(self.cut, bfloat),
            jax.ShapeDtypeStruct(self.cut, bfloat),
        ]
        self.in_vmem = [True, True, False, True, False, False]
        self.scratch = (
            [pltpu.VMEM(shape, bfloat), pltpu.VMEM((2,) + self.cut, bfloat)]
            + scatter_scratch(ctx, shape, bfloat) + gather_sems(ctx)
            + [pltpu.SemaphoreType.DMA((dp,))] * 4
            + ([pltpu.VMEM((ctx,) + shape, bfloat)] if fused else [])
        )

    def run(self, line, extra, source, results, scratch):
        middle_ref, cotangent_ref, gain_ref, normed_mid_ref, grads, hidden_ref, branch_ref = (
            extra[0], extra[1], extra[2], extra[3], extra[4:6], extra[6], extra[7],
        )
        grad_middle_ref, gain_sum_ref, all_ref, down_ref = results[:4]
        landed = results[4:]
        own_ref, cut_ref = scratch[:2]
        travel, sems = scratch[2:4], scratch[4:10]
        pushes = scratch[16:20]
        row = lax.axis_index("dp")
        height = D // self.dp

        def push(index, target):
            return remote(
                cut_ref.at[index, target], landed[index].at[row],
                pushes[2 * index].at[target], pushes[2 * index + 1].at[row], {"dp": target},
            )

        def keep(index):
            return pltpu.make_async_copy(
                cut_ref.at[index, row], landed[index].at[row], pushes[2 * index].at[row]
            )

        def rows_work(target):
            left = normed_mid_ref[:, target * height : (target + 1) * height].T
            for index in range(2):
                cut_ref[index, target] = dot(left, grads[index][...]).astype(bfloat)

        def send_rows():
            for index in range(2):
                for step in range(1, self.dp):
                    push(index, (row + step) % self.dp).start()
                keep(index).start()

        def down_work(part):
            width = D // 4
            span = slice(part * width, (part + 1) * width)
            down_ref[:, span] = dot(hidden_ref[...].T, branch_ref[:, span]).astype(bfloat)

        todo = [functools.partial(rows_work, target) for target in range(self.dp)]
        todo += [send_rows] + [functools.partial(down_work, part) for part in range(4)]

        def idle(count=2):
            for _ in range(min(count, len(todo))):
                todo.pop(0)()

        parts_ref = scratch[20] if self.fused else source

        def make(slot):
            pair_rows = 2 * own_ref.shape[0]
            rows = pl.ds(pl.multiple_of(slot * pair_rows, pair_rows), pair_rows)
            total = dot(grads[0][rows], source[...], 1, 1) + dot(grads[1][rows], extra[8][...], 1, 1)
            parts_ref[pl.ds(slot * 2, 2)] = total.astype(bfloat).reshape((2,) + own_ref.shape)

        scatter_line(line, parts_ref, *travel, sems, idle, make if self.fused else None)
        scatter_total(line, parts_ref, *travel, sems, grad_middle_ref)
        gain_sum_ref[...] = jnp.zeros_like(gain_sum_ref)

        def chunk(rows):
            normed, factor = normalize(middle_ref[rows])
            gradient = grad_middle_ref[rows]
            gain_sum_ref[...] += jnp.sum(gradient * normed, axis=0, keepdims=True)
            back = cotangent_ref[rows].astype(single) + norm_back(gradient * gain_ref[...], normed, factor)
            grad_middle_ref[rows] = back
            own_ref[rows] = (branch_scale * back).astype(bfloat)

        by_chunks(own_ref.shape[0], chunk)
        gather_line(line, own_ref, all_ref, scratch[10:16], lambda: idle(2))
        idle(len(todo))
        for index in range(2):
            for other in range(self.dp):
                @pl.when(row != other)
                def _():
                    push(index, other).wait_send()
                    remote(
                        cut_ref.at[index, other], landed[index].at[other],
                        pushes[2 * index].at[other], pushes[2 * index + 1].at[other], {"dp": other},
                    ).wait_recv()
            keep(index).wait()


class CloseLine:
    reach = "ctx"
    held = False

    def __init__(self, dp, ctx, parts):
        self.dp, self.ctx, self.parts = dp, ctx, parts
        own = parts.shape[1]
        self.result = [jax.ShapeDtypeStruct((own, D), single)]
        self.in_vmem = [True]
        self.scratch = [pltpu.VMEM(parts.shape, bfloat)] + pair_sems(ctx)

    def lay_out(self, rows, width):
        self.result += [jax.ShapeDtypeStruct((rows, width), single)] * 2
        self.in_vmem += [True] * 2
        return self

    def run(self, line, extra, source, results, scratch):
        tokens_ref, grad_middle_ref = extra[:2]
        out_ref, landed_ref = results[0], scratch[0]
        copies = ExchangeCtx(self.dp, self.ctx, self.parts).copies(source, landed_ref, *scratch[1:4])
        for copy in copies:
            copy.start()
        for index in range(2):
            regroup(extra[2 + index], results[1 + index], self.dp, self.ctx, False)
        for copy in copies:
            copy.wait()
        ungroup(landed_ref, out_ref, self.dp, self.ctx)

        def chunk(rows):
            normed, factor = normalize(tokens_ref[rows].astype(single))
            out_ref[rows] = grad_middle_ref[rows] + norm_back(out_ref[rows], normed, factor)

        by_chunks(out_ref.shape[0], chunk)


def by_chunks(total, work):
    def step(index, carry):
        work(pl.ds(pl.multiple_of(index * 16, 16), 16))
        return carry

    lax.fori_loop(0, total // 16, step, 0)


def regroup(source, target, dp, ctx, forward):
    whole, parts = (source, target) if forward else (target, source)
    width = whole.shape[1] // (dp * ctx)
    for place in range(ctx):
        for row in range(dp):
            start = (row * ctx + place) * width
            wide, narrow = slice(start, start + width), slice(row * width, (row + 1) * width)
            if forward:
                target[place, :, narrow] = source[:, wide]
            else:
                target[:, wide] = source[place, :, narrow].astype(single)


def ungroup(landed_ref, out_ref, dp, ctx):
    width = D // (dp * ctx)
    for place in range(ctx):
        block = landed_ref[place]
        block = block.reshape(out_ref.shape[0], dp * width).astype(single)
        for row in range(dp):
            start = (row * ctx + place) * width
            out_ref[:, start : start + width] = block[:, row * width : (row + 1) * width]


QUERY_SPAN = slice(0, QRANK)
LATENT_SPAN = slice(QRANK, QRANK + KVRANK)
ROPE_SPAN = slice(QRANK + KVRANK, LATENT)


def turn(values, table_ref, sign):
    return (
        values * table_ref[0]
        + sign * pltpu.roll(values, LANES - ROPE // 2, 1) * table_ref[1]
        + sign * pltpu.roll(values, ROPE // 2, 1) * table_ref[2]
    )


def everyone(dp, ctx):
    row, place = lax.axis_index("dp"), lax.axis_index("ctx")
    steps = [(a, b) for a in range(dp) for b in range(ctx) if a or b]
    return [((row + a) % dp, (place + b) % ctx) for a, b in steps]


def greet(dp, ctx, reach):
    row, place = lax.axis_index("dp"), lax.axis_index("ctx")
    if "all" in reach:
        targets = [{"dp": a, "ctx": b} for a, b in everyone(dp, ctx)]
    else:
        targets = []
        if "ctx" in reach:
            targets += [{"ctx": (place + step) % ctx} for step in range(1, ctx)]
        if "dp" in reach:
            targets += [{"dp": (row + step) % dp} for step in range(1, dp)]
    barrier = pltpu.get_barrier_semaphore()
    for target in targets:
        pl.semaphore_signal(barrier, inc=1, device_id=target, device_id_type=MESH)
    pl.semaphore_wait(barrier, len(targets))


def transfer_kernel(dp, ctx, line_piece, direct, extras, *refs):
    refs = list(refs)

    def take(count):
        taken = refs[:count]
        del refs[:count]
        return taken

    line_source = take(1) if line_piece else []
    sources = take(len(direct))
    extra = take(extras)
    line_results = take(len(line_piece.result)) if line_piece else []
    results = take(len(direct))
    line_scratch = take(len(line_piece.scratch)) if line_piece else []
    greet(dp, ctx, [piece.reach for piece in direct] + line_reach(line_piece))
    copies = []
    for piece, source, result in zip(direct, sources, results):
        copies += piece.copies(source, result, *take(len(piece.scratch)))
    for copy in copies:
        copy.start()
    if line_piece:
        line_piece.run(Line(ctx), extra, line_source[0], line_results, line_scratch)
    for copy in copies:
        copy.wait()


def line_reach(line_piece):
    if line_piece is None:
        return []
    return ["ctx", "dp"] if line_piece.reach == "both" else ["ctx"]


def transfer(dp, ctx, collective_id, name, line=None, direct=(), extra=(), mebibytes=8):
    pieces = [item[0](dp, ctx, item[1]) for item in direct]
    vmem, anywhere = pl.BlockSpec(memory_space=pltpu.VMEM), pl.BlockSpec(memory_space=pl.ANY)
    operands, in_specs, shapes, out_specs, scratch = [], [], [], [], []
    if line:
        operands.append(line.parts)
        in_specs.append(vmem if line.held else anywhere)
        shapes += line.result
        out_specs += [vmem if held else anywhere for held in line.in_vmem]
        scratch += line.scratch
    for piece in pieces:
        operands.append(piece.parts)
        in_specs.append(anywhere)
        shapes.append(piece.result)
        out_specs.append(anywhere)
        scratch += piece.scratch
    return pl.pallas_call(
        functools.partial(transfer_kernel, dp, ctx, line, pieces, len(extra)),
        out_shape=shapes,
        in_specs=in_specs + [
            pl.BlockSpec(memory_space=pltpu.SMEM) if item.dtype == jnp.int32 else vmem for item in extra
        ],
        out_specs=out_specs,
        scratch_shapes=scratch,
        compiler_params=comm_params(collective_id, mebibytes),
        cost_estimate=link_cost(150 << 20),
        name=name,
    )(*operands, *extra)


def valid_pairs(total, length):
    row = lax.broadcasted_iota(jnp.int32, (total, total), 0)
    col = lax.broadcasted_iota(jnp.int32, (total, total), 1)
    return (col <= row) & (col < length)


def slot_rows(ref, index, batch):
    span = ref.shape[1] // batch
    block = ref[:, pl.ds(pl.multiple_of(index * span, span), span), :]
    return block.reshape(ref.shape[0] * span, ref.shape[2])


def store_slot(ref, index, batch, lanes, values):
    span = ref.shape[1] // batch
    rows = pl.ds(pl.multiple_of(index * span, span), span)
    ref[:, rows, lanes] = values.reshape(ref.shape[0], span, values.shape[-1])


def attend_slot(
    heads, index, batch, length_ref, latent_ref, query_up_ref, latent_up_ref, table_ref,
    query_ref, kv_ref, attn_ref, total_ref,
):
    wide = heads * LANES
    latent = slot_rows(latent_ref, index, batch)
    total = latent.shape[0]
    query_normed, latent_normed, rope = latent[:, QUERY_SPAN], latent[:, LATENT_SPAN], latent[:, ROPE_SPAN]
    allowed = valid_pairs(total, length_ref[index])
    lane = lax.broadcasted_iota(jnp.int32, (total, LANES), 1)
    totals = jnp.zeros((total, LANES), single)
    query_up = query_up_ref[...].reshape(QRANK, wide)
    latent_up = latent_up_ref[...].reshape(KVRANK, wide)
    columns = pl.ds(pl.multiple_of(index * total, LANES), total)
    for head in range(heads):
        span = slice(head * LANES, (head + 1) * LANES)
        query = turn(dot(query_normed, query_up[:, span]), table_ref, 1.0).astype(bfloat)
        kv = dot(latent_normed, latent_up[:, span]).astype(bfloat)
        key = jnp.where(lane < NOPE, kv, rope)
        store_slot(query_ref, index, batch, span, query)
        store_slot(kv_ref, index, batch, span, kv)
        scores = dot(query, key, 1, 1) * score_scale
        masked = jnp.where(allowed, scores, neg_large)
        top = jnp.max(masked, axis=-1, keepdims=True)
        exponent = jnp.exp(masked - top)
        weight = jnp.sum(exponent, axis=-1, keepdims=True)
        totals = jnp.where(lane == head, top + jnp.log(weight), totals)
        probs = (exponent * (1.0 / weight)).astype(bfloat)
        out = dot(probs, kv).T[NOPE:]
        attn_ref[head * VDIM : (head + 1) * VDIM, columns] = out.astype(bfloat)
    store_slot(total_ref, index, batch, slice(0, LANES), totals)


def attend_back_slot(
    heads, index, batch, length_ref, query_ref, kv_ref, latent_ref, total_ref, branch_ref,
    out_heads_ref, query_up_ref, latent_up_ref, table_ref, parts_ref,
    grad_query_ref, grad_high_ref, grad_low_ref, query_sum_ref, latent_sum_ref,
):
    wide = heads * LANES
    latent = slot_rows(latent_ref, index, batch)
    rope = latent[:, ROPE_SPAN]
    total = rope.shape[0]
    totals = slot_rows(total_ref, index, batch)
    allowed = valid_pairs(total, length_ref[index])
    lane = lax.broadcasted_iota(jnp.int32, (total, LANES), 1)
    grad_rope = jnp.zeros((total, LANES), single)
    queries, kvs = slot_rows(query_ref, index, batch), slot_rows(kv_ref, index, batch)
    grads = dot(slot_rows(branch_ref, index, batch), out_heads_ref[...].reshape(D, heads * VDIM))
    grads = grads.astype(bfloat)
    blank = jnp.zeros((total, NOPE), bfloat)
    for head in range(heads):
        span = slice(head * LANES, (head + 1) * LANES)
        query, kv = queries[:, span], kvs[:, span]
        grad_attn = jnp.concatenate([blank, grads[:, head * VDIM : (head + 1) * VDIM]], axis=1)
        key = jnp.where(lane < NOPE, kv, rope)
        scores = dot(query, key, 1, 1) * score_scale
        probs = jnp.where(allowed, jnp.exp(scores - totals[:, head : head + 1]), 0.0)
        grad_probs = dot(grad_attn, kv, 1, 1)
        delta = jnp.sum(probs * grad_probs, axis=-1, keepdims=True)
        grad_scores = (probs * (grad_probs - delta)).astype(bfloat)
        grad_query = (dot(grad_scores, key) * score_scale).astype(bfloat).astype(single)
        grad_query_ref[:, span] = turn(grad_query, table_ref, -1.0).astype(bfloat)
        grad_key = dot(grad_scores, query, 0, 0) * score_scale
        grad_value = dot(probs.astype(bfloat), grad_attn, 0, 0)
        grad_kv = jnp.where(lane < NOPE, grad_key, grad_value)
        high = grad_kv.astype(bfloat)
        grad_high_ref[:, span] = high
        grad_low_ref[:, span] = (grad_kv - high.astype(single)).astype(bfloat)
        grad_rope = grad_rope + jnp.where(lane < NOPE, 0.0, grad_key)
    grad_query, high, low = grad_query_ref[...], grad_high_ref[...], grad_low_ref[...]
    query_up = query_up_ref[...].reshape(QRANK, wide)
    latent_up = latent_up_ref[...].reshape(KVRANK, wide)
    grad_latent = dot(high, latent_up, 1, 1) + dot(low, latent_up, 1, 1)
    for span, values in (
        (QUERY_SPAN, dot(grad_query, query_up, 1, 1)), (LATENT_SPAN, grad_latent), (ROPE_SPAN, grad_rope),
    ):
        store_slot(parts_ref, index, batch, span, values.astype(bfloat))
    latent_normed = latent[:, LATENT_SPAN]
    query_sum_ref[...] += dot(latent[:, QUERY_SPAN], grad_query, 0, 0)
    latent_sum_ref[...] += dot(latent_normed, high, 0, 0) + dot(latent_normed, low, 0, 0)


def angles_at(positions):
    freqs = 10000.0 ** (-(2.0 * jnp.arange(ROPE // 2, dtype=single)) / ROPE)
    angles = positions.astype(single)[:, None] * freqs[None, :]
    return (jnp.cos(angles), jnp.sin(angles))


def head_table(positions):
    total = positions.shape[0]
    cosine, sine = angles_at(positions)
    ones, none = jnp.ones((total, NOPE), single), jnp.zeros((total, NOPE), single)
    tail = jnp.zeros((total, LANES - NOPE - ROPE), single)
    zero = jnp.zeros_like(sine)
    return jnp.stack(
        [
            jnp.concatenate([ones, cosine, cosine, tail], axis=-1),
            jnp.concatenate([none, -sine, zero, tail], axis=-1),
            jnp.concatenate([none, zero, sine, tail], axis=-1),
        ]
    )


def pad_rope(values):
    return jnp.pad(values, ((0, 0), (NOPE, LANES - NOPE - ROPE)))


def on_device(
    dp,
    ctx,
    tokens,
    lengths,
    cotangent,
    input_gain,
    query_gain,
    latent_gain,
    post_gain,
    query_down,
    query_up,
    latent_down,
    latent_up,
    out_proj,
    gate_proj,
    up_proj,
    down_proj,
):
    batch, span, _ = tokens.shape
    own = batch * span
    group = ctx * own
    heads = -(-HEADS // ctx)
    spare = heads * ctx - HEADS
    d_rows, q_rows, l_rows, f_rows = (
        query_down.shape[0], query_up.shape[0], latent_up.shape[0], down_proj.shape[0],
    )
    d_part, f_part = dp * d_rows, dp * f_rows
    place = lax.axis_index("ctx")

    def slices(values):
        return values.reshape(own, dp, ctx, d_rows).transpose(2, 0, 1, 3).reshape(ctx, own, d_part)

    def row_sums(values):
        return jnp.sum(values.astype(single), axis=0)

    wide = heads * LANES
    up_rows = q_rows + l_rows
    run = functools.partial(transfer, dp, ctx)

    grad_out = cotangent.reshape(own, D).astype(single)
    grad_branch = gather_xla((branch_scale * grad_out).astype(bfloat))

    flat = tokens.reshape(own, D)
    inputs = flat.astype(single)
    normed_first, factor_first = normalize(inputs)
    gains = jnp.concatenate([input_gain, query_gain, latent_gain, post_gain]).astype(single)
    tile = 8 * LANES
    small = jnp.concatenate(
        [jnp.pad(gains, (0, tile - gains.shape[0])), jnp.pad(factor_first[:, 0], (0, tile - own))]
    )
    down_own = jnp.concatenate(
        [query_down, latent_down[:, :KVRANK], pad_rope(latent_down[:, KVRANK:])], axis=1
    )
    up_query = query_up.reshape(q_rows, HEADS, NOPE + ROPE)
    up_query = jnp.pad(up_query, ((0, 0), (0, spare), (0, LANES - NOPE - ROPE)))
    up_latent = jnp.pad(latent_up.reshape(l_rows, HEADS, NOPE + VDIM), ((0, 0), (0, spare), (0, 0)))
    up_query = up_query.reshape(q_rows, ctx, wide).transpose(1, 0, 2)
    up_latent = up_latent.reshape(l_rows, ctx, wide).transpose(1, 0, 2)
    token_slices, up_query, up_latent, down_rows, smalls = run(
        1, "open", None,
        [
            (ExchangeCtx, slices(flat)), (ExchangeCtx, up_query), (ExchangeCtx, up_latent),
            (GatherDp, down_own),
            (GatherAll, small.reshape(16, LANES)),
        ],
    )
    smalls, down_proj = lax.optimization_barrier((smalls, down_proj))
    down_rows = down_rows.reshape(d_part, LATENT)
    smalls = smalls.reshape(dp, ctx, 2 * tile)
    factor_all = smalls[lax.axis_index("dp"), :, tile : tile + own].reshape(group, 1)
    cuts = (d_rows, d_rows + q_rows, d_rows + up_rows, d_rows + up_rows + d_rows)
    gain_in = lax.dynamic_index_in_dim(smalls[:, :, : cuts[0]], place, 1, keepdims=False)
    gain_in = gain_in.reshape(1, d_part)
    gain_query = smalls[:, :, cuts[0] : cuts[1]].reshape(1, QRANK)
    gain_latent = smalls[:, :, cuts[1] : cuts[2]].reshape(1, KVRANK)
    gain_post = smalls[:, :, cuts[2] : cuts[3]].reshape(1, D)
    gain_down = jnp.concatenate([gain_query, gain_latent, jnp.zeros((1, LANES), single)], axis=1)

    out_padded = jnp.pad(out_proj, ((0, 0), (0, spare * VDIM)))
    down = gather_dp(down_proj)

    normed_slices = token_slices.reshape(group, d_part).astype(single) * factor_all
    normed_in = (normed_slices * gain_in).astype(bfloat)
    own_table = head_table(place * span + jnp.arange(own, dtype=jnp.int32) % span)
    parts = dot(normed_in, down_rows).astype(bfloat).reshape(ctx, own, LATENT)
    out_heads = out_padded.reshape(d_rows, ctx, heads * VDIM).transpose(1, 0, 2)
    ups = (up_query.reshape(ctx * q_rows, wide), up_latent.reshape(ctx * l_rows, wide))
    table = head_table(jnp.arange(ctx * span, dtype=jnp.int32))
    outs = run(
        2, "forward",
        ForwardLine(dp, ctx, parts, heads, batch, (gate_proj, up_proj), ups, out_padded, out_heads),
        (),
        (gain_down, own_table, lengths, table, gate_proj, up_proj) + ups + (out_padded, out_heads),
        56,
    )
    latents, latent_all, query, kv, totals, attn_all = outs[:6]
    query_ups, latent_ups, out_rows, gate, up, out_heads = outs[6:]
    attn_all = attn_all.reshape(ctx * heads * VDIM, group)
    gate = gate.reshape(D, f_part)
    branch = dot(attn_all, out_rows.reshape(d_part, ctx * heads * VDIM), 0, 1).astype(bfloat).reshape(batch, ctx, span, d_part)
    middle, normed_mid, out_heads, up = run(
        4, "middle", MiddleLine(dp, ctx, branch),
        [
            (GatherDp, out_heads.reshape(ctx * d_rows, heads * VDIM)),
            (GatherDp, up.reshape(ctx * d_rows, f_part)),
        ],
        (flat, gain_post), 24,
    )
    normed_mid = normed_mid.reshape(group, D)
    up = up.reshape(D, f_part)

    gate_act = dot(normed_mid, gate)
    up_act = dot(normed_mid, up)
    sigma = jax.nn.sigmoid(gate_act)
    hidden = (gate_act * sigma * up_act).astype(bfloat)
    grad_hidden = dot(grad_branch, down, 1, 1)
    grad_gate = (grad_hidden * up_act * (sigma * (1.0 + gate_act * (1.0 - sigma)))).astype(bfloat)
    grad_up = (grad_hidden * (gate_act * sigma)).astype(bfloat)
    fused = group <= 1024
    if fused:
        parts, last = gate, (up,)
    else:
        parts = dot(grad_gate, gate, 1, 1) + dot(grad_up, up, 1, 1)
        parts, last = parts.astype(bfloat).reshape(ctx, own, D), ()
    grad_middle, post_sum, grad_attn_branch, grad_down_proj, grad_gate_proj, grad_up_proj = run(
        5, "middle_back",
        MiddleBackLine(dp, ctx, parts, (own, D), f_part, fused),
        (),
        (
            middle, cotangent.reshape(own, D), gain_post, normed_mid, grad_gate, grad_up, hidden,
            grad_branch,
        ) + last,
        60,
    )
    columns_shape = (ctx, d_rows, f_part)
    grad_gate_proj = row_sums(grad_gate_proj).astype(bfloat).reshape(columns_shape)
    grad_up_proj = row_sums(grad_up_proj).astype(bfloat).reshape(columns_shape)
    branch_out = dot(hidden, down).astype(bfloat)
    branch_out, grad_attn_branch = lax.optimization_barrier((branch_out, grad_attn_branch))
    branch_out = scatter_xla(branch_out).astype(single)
    layer_out = (middle + branch_scale * branch_out).astype(bfloat)

    outs = run(
        8, "backward", BackwardLine(dp, ctx, grad_attn_branch, heads, batch, HEADS * VDIM),
        [
            (ExchangeDp, grad_down_proj.reshape(dp, f_rows, D)), (ExchangeCtx, grad_gate_proj),
            (ExchangeCtx, grad_up_proj),
        ],
        (
            gain_down, own_table, latents, attn_all, lengths, query, kv, latent_all, totals, out_heads,
            query_ups, latent_ups, table,
        ),
        62,
    )
    grad_latents, grad_down, grad_out_proj, grad_query_ups, grad_latent_ups = outs[:5]
    grad_down_proj, grad_gate_proj, grad_up_proj = outs[5:]
    grad_down = grad_down.reshape(group, LATENT)
    grad_normed_in = dot(grad_down, down_rows, 1, 1)
    grad_scaled = (grad_normed_in * gain_in).astype(bfloat).reshape(ctx, own, d_part)
    grad_rows = dot(normed_in, grad_down, 0, 0)
    last = jnp.sum(grad_normed_in * normed_slices, axis=0)[:, None]
    grad_rows = jnp.concatenate([grad_rows[:, : LATENT - 1], last], axis=1)
    normed_query, _ = normalize(latents[:, :QRANK])
    normed_latent, _ = normalize(latents[:, QRANK : QRANK + KVRANK])
    grad_query_normed = grad_latents[:, :QRANK]
    grad_latent_normed = grad_latents[:, QRANK : QRANK + KVRANK]
    gain_sums = jnp.concatenate(
        [
            post_sum.reshape(dp, ctx, d_rows),
            jnp.sum(grad_query_normed * normed_query, axis=0).reshape(dp, ctx, q_rows),
            jnp.sum(grad_latent_normed * normed_latent, axis=0).reshape(dp, ctx, l_rows),
        ],
        axis=2,
    )
    gain_sums = jnp.pad(gain_sums, ((0, 0), (0, 0), (0, tile - gain_sums.shape[2])))
    outs = run(
        9, "close", CloseLine(dp, ctx, grad_scaled).lay_out(d_rows, FF),
        [
            (ExchangeDp, grad_rows.reshape(dp, d_rows, LATENT)),
            (ExchangeDp, grad_out_proj),
            (ExchangeCtx, row_sums(grad_query_ups).astype(bfloat).reshape(ctx, q_rows, wide)),
            (ExchangeCtx, row_sums(grad_latent_ups).astype(bfloat).reshape(ctx, l_rows, wide)),
            (ExchangeAll, gain_sums.reshape(dp, ctx, 8, LANES)),
        ],
        (flat, grad_middle, grad_gate_proj, grad_up_proj),
        32,
    )
    input_grad, grad_gate_proj, grad_up_proj, grad_rows, grad_out_proj = outs[:5]
    grad_query_ups, grad_latent_ups, gain_sums = outs[5:]
    grad_rows = jnp.sum(grad_rows, axis=0)
    gain_sums = jnp.sum(gain_sums.reshape(dp * ctx, tile), axis=0)

    def by_heads(values, rows):
        return values.transpose(1, 0, 2).reshape(rows, ctx * heads, LANES)[:, :HEADS].astype(single)

    grad_query_up = by_heads(grad_query_ups, q_rows)[:, :, : NOPE + ROPE]
    grad_query_up = grad_query_up.reshape(q_rows, HEADS * (NOPE + ROPE))
    grad_latent_up = by_heads(grad_latent_ups, l_rows).reshape(l_rows, HEADS * (NOPE + VDIM))
    rope_start = QRANK + KVRANK + NOPE
    return (
        layer_out.reshape(batch, span, D),
        input_grad.reshape(batch, span, D),
        grad_rows[:, LATENT - 1],
        gain_sums[d_rows : d_rows + q_rows],
        gain_sums[d_rows + q_rows : d_rows + up_rows],
        gain_sums[:d_rows],
        grad_rows[:, :QRANK],
        grad_query_up,
        jnp.concatenate(
            [grad_rows[:, QRANK : QRANK + KVRANK], grad_rows[:, rope_start : rope_start + ROPE]], axis=1
        ),
        grad_latent_up,
        row_sums(grad_out_proj),
        grad_gate_proj,
        grad_up_proj,
        row_sums(grad_down_proj),
    )


def solution(mesh):
    both = ("dp", "ctx")
    tokens, vector, matrix = P("dp", "ctx", None), P(both), P(both, None)
    return jax.shard_map(
        functools.partial(on_device, mesh.shape["dp"], mesh.shape["ctx"]),
        mesh=mesh,
        in_specs=(tokens, P("dp"), tokens) + (vector,) * 4 + (matrix,) * 8,
        out_specs=(tokens, tokens) + (vector,) * 4 + (matrix,) * 8,
        check_vma=False,
    )
```

time: 922 us -> 776 us (0.84)
  local copies, waits for them, and re-layouts: 150 us -> 33.3 us
  matrix products: 117 us -> 50.5 us
  Pallas kernels: 595 us -> 637 us
    dot_general x20 -> x8, matrix products: 117 us -> 50.5 us  [dot(): lax.dot_general(left, right, (((left_dim,), (right_dim,)), ((), ())), pre...]
    convert_element_type x16 -> x3, local copies, waits for them, and re-layouts: 52.5 us -> 1.65 us  [the longest x1 1.44 us: on_device(): dot(attn_all, out_rows.reshape(d_part, ctx * heads * VDIM), 0, 1)]
    pallas_call x11 -> x6, Pallas kernels: 595 us -> 637 us  [transfer(): pl.pallas_call(functools.partial(transfer_kernel, dp, ctx, line, pieces,...]
    reshape x10 -> x5, local copies, waits for them, and re-layouts: 22.5 us -> 1.29 us  [the longest x1 0.91 us: on_device(): grad_query_up = grad_query_up.reshape(q_rows, HEADS * (NOPE + ROPE))]
    mul x6 -> x0, local copies, waits for them, and re-layouts: 16.6 us -> none  [the longest x5 16.5 us: on_device(): branch_scale * unslices(branch.reshape(ctx, own, d_part)).astype(single)]
    unnamed x183 -> x92, local copies, waits for them, and re-layouts: 27.3 us -> 17.8 us
  transfers between devices with their start and end apart: 4 -> 3, of which waited for: 0 -> 0; matrix products, arithmetic and copies ran while one was open for 25% -> 9% of each run, Pallas kernels for 61% -> 59%
where the time goes in v3:
time: 776 us; the launch traced here: 766 us
  Pallas kernels  637 us (82%)
  matrix products  50.5 us (7%)
  local copies, waits for them, and re-layouts  33.3 us (4%)
  other arithmetic  30.3 us (4%)
  between operations  14.7 us (2%)
    pallas_call x6, Pallas kernels, transfer(): pl.pallas_call(functools.partial(transfer_kernel, dp, ctx, line, pieces,...  637 us
    dot_general x8, matrix products, dot(): lax.dot_general(left, right, (((left_dim,), (right_dim,)), ((), ())), pre...  50.5 us
    unnamed x92, local copies, waits for them, and re-layouts  17.8 us
    reduce_sum x6, other arithmetic, row_sums(): return jnp.sum(values.astype(single), axis=0)  15.7 us
  transfers between devices with their start and end apart: 3, of which 0 were waited for; matrix products, arithmetic and copies ran while one was open for 9% of the time, Pallas kernels for 59%

profile of v3, /device:TPU:9, one launch (start us, length us, event | category | flops | bytes accessed | tf_op | source)
XLA Modules:
  0.0 765.5 jit_solution(18389993293968159320)
XLA Ops:
  7.2 2.4 reshape_reshape.3
  13.4 37.1 %open.1 = (bf16[8,128,320]{2,1,0:T(8,128)(2,1)S(1)}, bf16[8,24,640]{2,1,0:T(8,128)(2,1)S(1)}, bf16[8,8,640]{2,1,0:T(8,128)(2,1)S(1)}, bf16[4,80,1152]{2,1,0:T(8,128)(2,1)S(1)}, f32[4,8,16,128]{3,2,1,0:T(8,128)S(1)}) custom-call(bf16[8,128,320]{2,1,0:T(8,128)(2,1)S(1)} %copy.60.refs_0_, bf16[8,24,640]{2,1,0:T(8,128)(2,1)S(1)} %bitcast.107, ...), custom_call_target="tpu_custom_call" | custom-call | bytes 157286400 | tf_op jit(solution)/shard_map/open/pallas_call | solution.py:864
  59.5 2.9 convolution_convert_fusion.1
  62.4 196.3 %forward.1 = (f32[128,1152]{1,0:T(8,128)}, bf16[8,128,1152]{2,1,0:T(8,128)(2,1)}, bf16[8,128,640]{2,1,0:T(8,128)(2,1)}, bf16[8,128,640]{2,1,0:T(8,128)(2,1)}, f3...) custom-call(bf16[8,128,1152]{2,1,0:T(8,128)(2,1)} %bitcast.131, ...), custom_call_target="tpu_custom_call" | custom-call | bytes 157286400 | tf_op jit(solution)/shard_map/forward/pallas_call | solution.py:864
  258.7 5.8 convolution_convert_fusion.2
  264.5 1.4 copy.64
  267.3 81.4 %middle.1 = (f32[128,2560]{1,0:T(8,128)S(1)}, bf16[8,128,2560]{2,1,0:T(8,128)(2,1)S(1)}, bf16[4,640,320]{2,1,0:T(8,128)(2,1)S(1)}, bf16[4,640,800]{2,1,0:T(8,128)(2,1)S(1)}) custom-call(bf16[2,8,64,320]{3,2,1,0:T(8,128)(2,1)S(1)} %bitcast.104, bf16[640,320]{1,0:T(8,128)(2,1)S(1)} %bitcast.109, bf16[640,800]{1,0:T(8,128)(2,1)S(1)} %bitcast.106, ...), custom_call_target="tpu_custom_call" | custom-call | bytes 157286400 | tf_op jit(solution)/shard_map/middle/pallas_call | solution.py:864
  348.8 7.4 fusion.19
  356.2 7.4 fusion.18
  363.6 12.8 %multiply_convert_fusion = (bf16[1024,800]{1,0:T(8,128)(2,1)}, bf16[1024,800]{1,0:T(8,128)(2,1)}, bf16[1024,800]{1,0:T(8,128)(2,1)S(1)}) fusion(f32[1024,800]{1,0:T(8,128)} %fusion.18, f32[1024,800]{1,0:T(8,128)} %fusion.19, bf16[1024,2560]{1,0:T(8,128)(2,1)} %all-gather.5.cloned.1.call-done.refs_8_, bf16[800,2560]{1,0:T(8,128)(2,1)} %all-gather.3.cloned.1.call-done), kind=kOutput, calls=%fused_computation.3 | convolution fusion | flops 4206592000 | bytes 20807680 | tf_op jit(solution)/shard_map/dot_general | solution.py:33
  377.6 7.5 convolution_convert_fusion
  385.2 145.2 %middle_back.1 = (f32[128,2560]{1,0:T(8,128)}, f32[1,2560]{1,0:T(1,128)}, bf16[8,128,2560]{2,1,0:T(8,128)(2,1)}, bf16[800,2560]{1,0:T(8,128)(2,1)}, bf16[4,640,8...) custom-call(bf16[2560,800]{1,0:T(8,128)(2,1)} %bitcast.120, f32[128,2560]{1,0:T(8,128)} %copy-done.1, ...), custom_call_target="tpu_custom_call" | custom-call | bytes 157286400 | tf_op jit(solution)/shard_map/middle_back/pallas_call | solution.py:864
  532.0 4.3 reduce_sum.141
  536.3 4.4 reduce_sum.142
  540.7 130.3 %backward.1 = (f32[128,1152]{1,0:T(8,128)}, bf16[8,128,1152]{2,1,0:T(8,128)(2,1)}, bf16[4,80,2560]{2,1,0:T(8,128)(2,1)}, bf16[4,192,640]{2,1,0:T(8,128)(2,1)}, b...) custom-call(bf16[8,128,2560]{2,1,0:T(8,128)(2,1)} %get-tuple-element, ...), custom_call_target="tpu_custom_call" | custom-call | bytes 157286400 | tf_op jit(solution)/shard_map/backward/pallas_call | solution.py:864
  673.6 3.9 multiply_reduce_fusion
  677.7 1.5 copy.76
  679.3 1.4 reduce_sum.144
  680.8 2.9 convolution_bitcast_fusion
  685.5 46.2 %close.1 = (f32[128,2560]{1,0:T(8,128)S(1)}, f32[80,6400]{1,0:T(8,128)S(1)}, f32[80,6400]{1,0:T(8,128)S(1)}, f32[4,80,1152]{2,1,0:T(8,128)S(1)}, bf16[4,80,2560]...) custom-call(bf16[8,128,320]{2,1,0:T(8,128)(2,1)S(1)} %bitcast.102, ...), custom_call_target="tpu_custom_call" | custom-call | bytes 157286400 | tf_op jit(solution)/shard_map/close/pallas_call | solution.py:864
  737.7 1.5 reduce_sum.150
  746.1 4.4 convert_reduce_fusion
  750.5 2.2 add_convert_fusion
  752.7 2.5 copy.95
  (182 shorter events, 37.7 us)
Async XLA Ops:
  7.2 356.4 %all-gather.3.cloned.1.call-start = ((), (), s32[]{:S(2)}) async-start(), calls=%async_computation.1 | async-start | bytes 5120000 | tf_op jit(solution)/shard_map/all_gather | solution.py:52
  7.2 5.1 copy-start.34
  12.4 39.6 %copy-start.30 = (bf16[2,64,2560]{2,1,0:T(8,128)(2,1)S(1)}, bf16[2,64,2560]{2,1,0:T(8,128)(2,1)}, u32[]{:S(2)}) copy-start(bf16[2,64,2560]{2,1,0:T(8,128)(2,1)} %param.17) | copy-start | bytes 1966084
  51.9 7.6 copy-start.24
  51.9 311.7 %all-gather.5.cloned.1.call-start = ((), (), s32[]{:S(2)}) async-start(), calls=%async_computation.2 | async-start | bytes 5898240 | tf_op jit(solution)/shard_map/all_gather | solution.py:60
  53.0 697.5 %reduce-scatter.2.cloned.1.call-start = ((), (), s32[]{:S(2)}) async-start(), calls=%async_computation.3 | async-start | bytes 5898240 | tf_op jit(solution)/shard_map/reduce_scatter | solution.py:64
  258.7 7.3 copy-start
  258.7 7.3 copy-start.19
  266.0 90.1 %copy-start.21 = (f32[1,2560]{1,0:T(1,128)}, f32[1,2560]{1,0:T(1,128)S(1)}, u32[]{:S(2)}) copy-start(f32[1,2560]{1,0:T(1,128)S(1)} %reshape.258.refs_4_.refs_3_) | copy-start | bytes 30724
  267.3 88.9 %slice-start = ((s8[4587520]{0:T(1024)(128)(4,1)}), s8[393216]{0:T(1024)(128)(4,1)S(1)}, s32[]{:S(2)}) async-start(s8[4587520]{0:T(1024)(128)(4,1)} %bitcast.121), calls=%async_computation.4 | async-start | bytes 786432
  348.7 7.4 copy-start.1
  348.7 7.4 copy-start.4
  348.7 7.4 copy-start.9
  348.7 7.4 copy-start.3
  348.8 7.4 slice-start.1
  363.6 14.1 %copy-start.41 = (bf16[800,2560]{1,0:T(8,128)(2,1)S(1)}, bf16[800,2560]{1,0:T(8,128)(2,1)}, u32[]{:S(2)}) copy-start(bf16[800,2560]{1,0:T(8,128)(2,1)} %all-gather.3.cloned.1.call-done) | copy-start | bytes 12288004
  540.7 130.3 %copy-start.27 = (f32[128,1152]{1,0:T(8,128)S(1)}, f32[128,1152]{1,0:T(8,128)}, u32[]{:S(2)}) copy-start(f32[128,1152]{1,0:T(8,128)} %get-tuple-element.82.refs_6_) | copy-start | bytes 1769476
  540.7 132.6 %copy-start.36 = (f32[1,2560]{1,0:T(1,128)S(1)}, f32[1,2560]{1,0:T(1,128)}, u32[]{:S(2)}) copy-start(f32[1,2560]{1,0:T(1,128)} %get-tuple-element.94) | copy-start | bytes 30724
  540.7 132.9 %copy-start.25 = (bf16[4,80,1152]{2,1,0:T(8,128)(2,1)S(1)}, bf16[4,80,1152]{2,1,0:T(8,128)(2,1)}, u32[]{:S(2)}) copy-start(bf16[4,80,1152]{2,1,0:T(8,128)(2,1)} %copy-done.24) | copy-start | bytes 2211844
  677.5 3.2 copy-start.33
  677.5 3.2 copy-start.29
  739.2 5.7 copy-start.11
  746.1 4.4 copy-start.2
  750.4 4.7 copy-start.8
  (25 other events, 44.0 us)
Sparse Core Ops, SparseCore 0:
  52.0 76.5 all-gather.2
  130.8 69.4 all-gather.4
  530.5 114.7 reduce-scatter.1

commit v4 on v3

--- a/solution.py
+++ b/solution.py
@@ -2,6 +2,7 @@
 
 import jax
 import jax.numpy as jnp
+import numpy as np
 from jax import lax
 from jax.experimental import pallas as pl
 from jax.experimental.pallas import tpu as pltpu
@@ -46,14 +47,6 @@
 
 def norm_back(grad_scaled, normed, factor):
     return factor * (grad_scaled - normed * jnp.mean(grad_scaled * normed, axis=-1, keepdims=True))
-
-
-def gather_dp(values):
-    return lax.all_gather(values, "dp", axis=0, tiled=True)
-
-
-def scatter_dp(values):
-    return lax.psum_scatter(values, "dp", scatter_dimension=0, tiled=True)
 
 
 def gather_xla(values):
@@ -90,7 +83,7 @@
     pass
 
 
-def gather_line(line, own_ref, all_ref, sems, idle=nothing):
+def gather_line(line, own_ref, all_ref, sems, idle=nothing, arrived=None):
     send_left, send_right, send_twin, receive, receive_twin, local = sems
     pairs, pair, core = line.pairs, line.pair, line.core
 
@@ -105,6 +98,10 @@
     to_twin(own_ref, pair).start()
     keep = pltpu.make_async_copy(own_ref, all_ref.at[line.place], local)
     keep.start()
+    if arrived:
+        keep.wait()
+        to_twin(own_ref, pair).wait_recv()
+        arrived(pair)
     for step in range(1, pairs):
         idle()
 
@@ -122,13 +119,29 @@
 
         pl.when(pair - step >= 0)(from_left)
         pl.when(pair + step < pairs)(from_right)
-    keep.wait()
+        if arrived:
+            slot = nearest(line, step)
+            to_twin(own_ref, slot).wait_recv()
+            arrived(slot)
+    if not arrived:
+        keep.wait()
     for slot in range(pairs):
-        to_twin(own_ref, slot).wait()
+        if arrived:
+            to_twin(own_ref, slot).wait_send()
+        else:
+            to_twin(own_ref, slot).wait()
         pl.when((slot <= pair) & line.has_right)(
             lambda slot=slot: to_side(own_ref, slot, send_right, line.right).wait_send())
         pl.when((slot >= pair) & line.has_left)(
             lambda slot=slot: to_side(own_ref, slot, send_left, line.left).wait_send())
+
+
+def nearest(line, order):
+    shorter = jnp.minimum(line.pair, line.pairs - 1 - line.pair)
+    distance = (order + 1) // 2
+    both = line.pair + (distance if order % 2 == 0 else -distance)
+    ahead = jnp.where(line.pair < line.pairs - 1 - line.pair, order - shorter, shorter - order)
+    return jnp.where(order <= 2 * shorter, both, line.pair + ahead)
 
 
 def comm_params(collective_id, mebibytes):
@@ -372,25 +385,47 @@
         gather_line(line, own_ref, all_ref, scratch[9:])
 
 
+class OpenLine:
+    reach = "ctx"
+    held = True
+
+    def __init__(self, dp, ctx, parts):
+        self.dp, self.ctx, self.parts = dp, ctx, parts
+        rows, width = parts.shape
+        self.cut = jax.ShapeDtypeStruct((ctx, rows, width // ctx), bfloat)
+        self.result = [self.cut] * 2
+        self.in_vmem = [False] * 2
+        self.scratch = [pltpu.VMEM((2,) + self.cut.shape, bfloat)] + pair_sems(ctx) * 2
+
+    def run(self, line, extra, source, results, scratch):
+        cut_ref, copies = scratch[0], []
+        for index, matrix in enumerate((source, extra[0])):
+            regroup(matrix, cut_ref.at[index], self.dp, self.ctx, True)
+            sems = scratch[1 + 3 * index : 4 + 3 * index]
+            pieces = ExchangeCtx(self.dp, self.ctx, self.cut).copies(cut_ref.at[index], results[index], *sems)
+            for copy in pieces:
+                copy.start()
+            copies += pieces
+        for copy in copies:
+            copy.wait()
+
+
 class ForwardLine(LatentLine):
     reach = "both"
 
-    def __init__(self, dp, ctx, parts, heads, batch, matrices, ups, out_own, out_heads):
+    def __init__(self, dp, ctx, parts, heads, batch, matrices, ups, out_heads):
         super().__init__(dp, ctx, parts)
         own = parts.shape[1]
-        rows, width = matrices[0].shape
         group, wide = ctx * own, heads * LANES
         self.dp, self.ctx, self.heads, self.batch = dp, ctx, heads, batch
-        self.cut = (ctx, rows, width // ctx)
         self.pieces = {
-            "gate": ExchangeCtx(dp, ctx, jax.ShapeDtypeStruct(self.cut, bfloat)),
-            "up": ExchangeCtx(dp, ctx, jax.ShapeDtypeStruct(self.cut, bfloat)),
             "heads": ExchangeCtx(dp, ctx, out_heads),
             "queries": GatherDp(dp, ctx, ups[0]),
             "latents": GatherDp(dp, ctx, ups[1]),
-            "rows": GatherDp(dp, ctx, out_own),
-            "gates": GatherDp(dp, ctx, jax.ShapeDtypeStruct(self.cut, bfloat)),
+            "gates": GatherDp(dp, ctx, matrices[0]),
+            "ups": GatherDp(dp, ctx, matrices[1]),
         }
+        self.elsewhere = (4, 5)
         self.result += [
             jax.ShapeDtypeStruct((ctx, own, wide), bfloat),
             jax.ShapeDtypeStruct((ctx, own, wide), bfloat),
@@ -398,30 +433,26 @@
             jax.ShapeDtypeStruct((ctx, heads * VDIM, group), bfloat),
         ]
         self.result += [
-            self.pieces[name].result for name in ("queries", "latents", "rows", "gates", "up", "heads")
+            self.pieces[name].result for name in ("queries", "latents", "gates", "ups", "heads")
         ]
-        self.in_vmem = [True, True, True, True, True, False, True, True] + [False] * 4
+        self.in_vmem = [True, True, True, True, True, False, True, True] + [False] * 3
         self.base = len(self.scratch)
-        self.scratch = self.scratch + [
-            pltpu.VMEM((2,) + self.cut, bfloat), pltpu.VMEM(self.cut, bfloat),
-            pltpu.VMEM((heads * VDIM, group), bfloat),
-        ]
+        self.scratch = self.scratch + [pltpu.VMEM((heads * VDIM, group), bfloat)]
         for piece in self.pieces.values():
             self.scratch = self.scratch + piece.scratch
         self.scratch = self.scratch + gather_sems(ctx)
 
     def run(self, line, extra, source, results, scratch):
         gain_ref, table_ref, length_ref, slot_table_ref = extra[:4]
-        matrices, ups, out_own_ref, out_heads_ref = extra[4:6], extra[6:8], extra[8], extra[9]
+        matrices, ups, out_heads_ref = extra[4:6], extra[6:8], extra[8]
         sums_ref, all_ref, query_ref, kv_ref, total_ref, attn_all_ref = results[:6]
-        query_ups_ref, latent_ups_ref, rows_ref, gates_ref, up_ref, heads_ref = results[6:]
-        cut_ref, gate_ref, attn_ref = scratch[self.base : self.base + 3]
-        later = list(scratch[self.base + 3 :])
+        query_ups_ref, latent_ups_ref, gates_ref, ups_ref, heads_ref = results[6:]
+        attn_ref = scratch[self.base]
+        later = list(scratch[self.base + 1 :])
         ends = {
-            "gate": (cut_ref.at[0], gate_ref), "up": (cut_ref.at[1], up_ref),
             "heads": (out_heads_ref, heads_ref), "queries": (ups[0], query_ups_ref),
-            "latents": (ups[1], latent_ups_ref), "rows": (out_own_ref, rows_ref),
-            "gates": (gate_ref, gates_ref),
+            "latents": (ups[1], latent_ups_ref),
+            "gates": (matrices[0], gates_ref), "ups": (matrices[1], ups_ref),
         }
         copies = {}
         for name, piece in self.pieces.items():
@@ -438,17 +469,8 @@
                 for copy in copies[name]:
                     copy.wait()
 
-        todo = ["gate", "up"]
-
-        def idle():
-            while todo:
-                name = todo.pop(0)
-                index = 1 - len(todo)
-                regroup(matrices[index], cut_ref.at[index], self.dp, self.ctx, True)
-                start(name)
-
-        start("queries", "latents", "rows")
-        scatter_line(line, source, *scratch[1:3], scratch[3:9], idle)
+        start("queries", "latents", "gates", "ups")
+        scatter_line(line, source, *scratch[1:3], scratch[3:9])
         scatter_total(line, source, *scratch[1:3], scratch[3:9], sums_ref)
         self.finish_own((gain_ref, table_ref), sums_ref, scratch[0])
         gather_line(line, scratch[0], all_ref, scratch[9 : self.base])
@@ -463,10 +485,8 @@
             return carry
 
         lax.fori_loop(0, self.batch, slot, 0)
-        wait("gate")
-        start("gates")
         gather_line(line, attn_ref, attn_all_ref, later)
-        wait("up", "heads", "rows", "gates")
+        wait("heads", "gates", "ups")
 
 
 class BackwardLine(LatentLine):
@@ -483,9 +503,10 @@
             ExchangeDp(dp, ctx, jax.ShapeDtypeStruct((dp, rank // dp, wide), bfloat))
             for rank in (QRANK, KVRANK)
         ]
-        self.result += [jax.ShapeDtypeStruct((dp, rows, columns), bfloat)]
+        self.out = ExchangeDp(dp, ctx, jax.ShapeDtypeStruct((dp, rows, columns), bfloat))
+        self.result += [self.out.result]
         self.result += [piece.result for piece in self.ups]
-        self.in_vmem += [True, False, False]
+        self.in_vmem += [False, False, False]
         self.base = len(self.scratch)
         total = ctx * own // batch
         self.scratch = self.scratch + [
@@ -494,8 +515,9 @@
         self.scratch = self.scratch + [pltpu.VMEM((total, wide), bfloat)] * 3
         self.scratch = self.scratch + [pltpu.VMEM((rank, wide), single) for rank in (QRANK, KVRANK)]
         self.scratch = self.scratch + [pltpu.VMEM(piece.parts.shape, bfloat) for piece in self.ups]
-        for piece in self.ups:
+        for piece in self.ups + [self.out]:
             self.scratch = self.scratch + piece.scratch
+        self.scratch = self.scratch + [pltpu.VMEM(self.out.parts.shape, bfloat)]
 
     def run(self, line, extra, source, results, scratch):
         branch_ref, attn_ref = source, extra[3]
@@ -523,7 +545,8 @@
             )
         for copy in copies:
             copy.start()
-        out_ref, slice_ref = results[2], scratch[self.base]
+        out_ref, slice_ref = scratch[-1], scratch[self.base]
+        out_copies = self.out.copies(out_ref, results[2], *scratch[-4:-1])
         rows = D // (self.dp * self.ctx)
         height = D // self.dp
         own = branch_ref.shape[1]
@@ -548,6 +571,9 @@
         def idle():
             if todo:
                 work(todo.pop(0))
+                if not todo:
+                    for copy in out_copies:
+                        copy.start()
 
         sums_ref, all_ref = results[:2]
         own_ref = scratch[0]
@@ -557,7 +583,7 @@
         gather_line(line, own_ref, all_ref, scratch[9 : self.base], idle)
         while todo:
             idle()
-        for copy in copies:
+        for copy in copies + out_copies:
             copy.wait()
 
     def finish_own(self, extra, sums_ref, own_ref):
@@ -573,24 +599,44 @@
     reach = "ctx"
     held = False
 
-    def __init__(self, dp, ctx, parts):
+    def __init__(self, dp, ctx, parts, f_part):
         self.dp, self.ctx, self.parts = dp, ctx, parts
         own, cut = parts.shape[0] * parts.shape[2], parts.shape[3]
+        group = ctx * own
         self.result = [
-            jax.ShapeDtypeStruct((own, D), single), jax.ShapeDtypeStruct((ctx, own, D), bfloat)
+            jax.ShapeDtypeStruct((own, D), single), jax.ShapeDtypeStruct((ctx, own, D), bfloat),
+            jax.ShapeDtypeStruct((ctx, own, D), bfloat),
         ]
-        self.in_vmem = [True, False]
+        self.result += [jax.ShapeDtypeStruct((group, f_part), bfloat)] * 3
+        self.in_vmem = [True] + [False] * 5
         self.scratch = (
             [pltpu.VMEM((ctx, parts.shape[0], parts.shape[2], cut), bfloat), pltpu.VMEM((own, D), bfloat)]
             + pair_sems(ctx) + gather_sems(ctx)
         )
+        self.base = len(self.scratch)
+        self.scratch = self.scratch + [pltpu.VMEM((ctx, own, D), bfloat)] * 2
+        self.scratch = self.scratch + [pltpu.VMEM((group, f_part), bfloat)] * 3
+        self.scratch = self.scratch + [pltpu.SemaphoreType.DMA((ctx // 2,))] * 5
+        shapes = [(D, f_part), (D, f_part), (f_part, D), (group, D)]
+        self.scratch = self.scratch + [pltpu.VMEM(shape, bfloat) for shape in shapes]
+        self.scratch = self.scratch + [pltpu.SemaphoreType.DMA] * 4
+        self.elsewhere = (2, 3, 4, 5)
 
     def run(self, line, extra, source, results, scratch):
-        tokens_ref, gain_ref = extra
-        middle_ref, all_ref = results
+        tokens_ref, gain_ref = extra[:2]
+        middle_ref = results[0]
         landed_ref, own_ref = scratch[:2]
+        kept = scratch[self.base : self.base + 5]
+        kept_sems = scratch[self.base + 5 : self.base + 10]
+        weights = scratch[self.base + 10 : self.base + 14]
+        all_ref, branch_out_ref, hidden_ref, grad_gate_ref, grad_up_ref = kept
+        gate_ref, up_ref, down_ref, branch_ref = weights
+        loads = [
+            pltpu.make_async_copy(extra[2 + index], ref, scratch[self.base + 14 + index])
+            for index, ref in enumerate(weights)
+        ]
         copies = ExchangeCtx(self.dp, self.ctx, self.parts).copies(source, landed_ref, *scratch[2:5])
-        for copy in copies:
+        for copy in copies + loads:
             copy.start()
         for copy in copies:
             copy.wait()
@@ -603,7 +649,39 @@
             own_ref[rows] = (normed * gain_ref[...]).astype(bfloat)
 
         by_chunks(own_ref.shape[0], chunk)
-        gather_line(line, own_ref, all_ref, scratch[5:])
+        todo = list(loads)
+
+        def out_copies(slot):
+            height = 2 * own_ref.shape[0]
+            for index, (ref, sem) in enumerate(zip(kept, kept_sems)):
+                rows = pl.ds(slot * 2, 2) if index < 2 else pl.ds(slot * height, height)
+                yield pltpu.make_async_copy(ref.at[rows], results[1 + index].at[rows], sem.at[slot])
+
+        def arrived(slot):
+            while todo:
+                todo.pop(0).wait()
+            height = 2 * own_ref.shape[0]
+            rows = pl.ds(pl.multiple_of(slot * height, height), height)
+            normed = all_ref[pl.ds(slot * 2, 2)].reshape(height, D)
+            gate_act = dot(normed, gate_ref[...])
+            up_act = dot(normed, up_ref[...])
+            grad_hidden = dot(branch_ref[rows], down_ref[...], 1, 1)
+            sigma = jax.nn.sigmoid(gate_act)
+            silu = gate_act * sigma
+            hidden = (silu * up_act).astype(bfloat)
+            hidden_ref[rows] = hidden
+            slope = sigma * (1.0 + gate_act * (1.0 - sigma))
+            grad_gate_ref[rows] = (grad_hidden * up_act * slope).astype(bfloat)
+            grad_up_ref[rows] = (grad_hidden * silu).astype(bfloat)
+            out = dot(hidden, down_ref[...]).astype(bfloat)
+            branch_out_ref[pl.ds(slot * 2, 2)] = out.reshape((2,) + own_ref.shape)
+            for copy in out_copies(slot):
+                copy.start()
+
+        gather_line(line, own_ref, all_ref, scratch[5:self.base], arrived=arrived)
+        for slot in range(line.pairs):
+            for copy in out_copies(slot):
+                copy.wait()
 
 
 class MiddleBackLine:
@@ -630,11 +708,21 @@
             + [pltpu.SemaphoreType.DMA((dp,))] * 4
             + ([pltpu.VMEM((ctx,) + shape, bfloat)] if fused else [])
         )
+        self.base = len(self.scratch)
+        group = ctx * own
+        for size in (D, f_part, D):
+            self.scratch = self.scratch + [pltpu.VMEM((group, size), bfloat), pltpu.SemaphoreType.DMA]
+        self.elsewhere = (3, 6, 7)
 
     def run(self, line, extra, source, results, scratch):
-        middle_ref, cotangent_ref, gain_ref, normed_mid_ref, grads, hidden_ref, branch_ref = (
-            extra[0], extra[1], extra[2], extra[3], extra[4:6], extra[6], extra[7],
-        )
+        middle_ref, cotangent_ref, gain_ref, grads = extra[0], extra[1], extra[2], extra[4:6]
+        normed_mid_ref, hidden_ref, branch_ref = scratch[self.base :: 2]
+        loads = [
+            pltpu.make_async_copy(extra[place], scratch[self.base + 2 * index], scratch[self.base + 2 * index + 1])
+            for index, place in enumerate(self.elsewhere)
+        ]
+        for load in loads:
+            load.start()
         grad_middle_ref, gain_sum_ref, all_ref, down_ref = results[:4]
         landed = results[4:]
         own_ref, cut_ref = scratch[:2]
@@ -654,24 +742,40 @@
                 cut_ref.at[index, row], landed[index].at[row], pushes[2 * index].at[row]
             )
 
-        def rows_work(target):
-            left = normed_mid_ref[:, target * height : (target + 1) * height].T
+        def rows_work(step):
+            if step == 1:
+                loads[0].wait()
+            if height % LANES == 0:
+                target = (row + step) % self.dp
+                columns = pl.ds(pl.multiple_of(target * height, LANES), height)
+            else:
+                target = step % self.dp
+                columns = slice(target * height, (target + 1) * height)
+            left = normed_mid_ref[:, columns].T
             for index in range(2):
                 cut_ref[index, target] = dot(left, grads[index][...]).astype(bfloat)
-
-        def send_rows():
+                if height % LANES == 0 and step < self.dp:
+                    push(index, target).start()
+            if step == self.dp:
+                last_rows()
+
+        def last_rows():
             for index in range(2):
                 for step in range(1, self.dp):
-                    push(index, (row + step) % self.dp).start()
+                    if height % LANES:
+                        push(index, (row + step) % self.dp).start()
                 keep(index).start()
 
         def down_work(part):
             width = D // 4
+            if part == 0:
+                loads[1].wait()
+                loads[2].wait()
             span = slice(part * width, (part + 1) * width)
             down_ref[:, span] = dot(hidden_ref[...].T, branch_ref[:, span]).astype(bfloat)
 
-        todo = [functools.partial(rows_work, target) for target in range(self.dp)]
-        todo += [send_rows] + [functools.partial(down_work, part) for part in range(4)]
+        todo = [functools.partial(rows_work, step) for step in range(1, self.dp + 1)]
+        todo += [functools.partial(down_work, part) for part in range(4)]
 
         def idle(count=2):
             for _ in range(min(count, len(todo))):
@@ -865,7 +969,9 @@
         functools.partial(transfer_kernel, dp, ctx, line, pieces, len(extra)),
         out_shape=shapes,
         in_specs=in_specs + [
-            pl.BlockSpec(memory_space=pltpu.SMEM) if item.dtype == jnp.int32 else vmem for item in extra
+            pl.BlockSpec(memory_space=pltpu.SMEM) if item.dtype == jnp.int32
+            else anywhere if index in getattr(line, "elsewhere", ()) else vmem
+            for index, item in enumerate(extra)
         ],
         out_specs=out_specs,
         scratch_shapes=scratch,
@@ -975,25 +1081,17 @@
     latent_sum_ref[...] += dot(latent_normed, high, 0, 0) + dot(latent_normed, low, 0, 0)
 
 
-def angles_at(positions):
-    freqs = 10000.0 ** (-(2.0 * jnp.arange(ROPE // 2, dtype=single)) / ROPE)
-    angles = positions.astype(single)[:, None] * freqs[None, :]
-    return (jnp.cos(angles), jnp.sin(angles))
-
-
-def head_table(positions):
-    total = positions.shape[0]
-    cosine, sine = angles_at(positions)
-    ones, none = jnp.ones((total, NOPE), single), jnp.zeros((total, NOPE), single)
-    tail = jnp.zeros((total, LANES - NOPE - ROPE), single)
-    zero = jnp.zeros_like(sine)
-    return jnp.stack(
-        [
-            jnp.concatenate([ones, cosine, cosine, tail], axis=-1),
-            jnp.concatenate([none, -sine, zero, tail], axis=-1),
-            jnp.concatenate([none, zero, sine, tail], axis=-1),
-        ]
-    )
+def head_table(total):
+    freqs = np.float32(10000.0) ** (-(2.0 * np.arange(ROPE // 2, dtype=np.float32)) / ROPE)
+    angles = np.arange(total, dtype=np.float32)[:, None] * freqs.astype(np.float32)[None, :]
+    cosine, sine = np.cos(angles), np.sin(angles)
+    table = np.zeros((3, total, LANES), np.float32)
+    half, end = NOPE + ROPE // 2, NOPE + ROPE
+    table[0, :, :NOPE] = 1.0
+    table[0, :, NOPE:half] = table[0, :, half:end] = cosine
+    table[1, :, NOPE:half] = -sine
+    table[2, :, half:end] = sine
+    return jnp.asarray(table)
 
 
 def pad_rope(values):
@@ -1041,7 +1139,7 @@
     run = functools.partial(transfer, dp, ctx)
 
     grad_out = cotangent.reshape(own, D).astype(single)
-    grad_branch = gather_xla((branch_scale * grad_out).astype(bfloat))
+    grad_branch = (branch_scale * grad_out).astype(bfloat)
 
     flat = tokens.reshape(own, D)
     inputs = flat.astype(single)
@@ -1059,15 +1157,19 @@
     up_latent = jnp.pad(latent_up.reshape(l_rows, HEADS, NOPE + VDIM), ((0, 0), (0, spare), (0, 0)))
     up_query = up_query.reshape(q_rows, ctx, wide).transpose(1, 0, 2)
     up_latent = up_latent.reshape(l_rows, ctx, wide).transpose(1, 0, 2)
-    token_slices, up_query, up_latent, down_rows, smalls = run(
-        1, "open", None,
+    out_padded = jnp.pad(out_proj, ((0, 0), (0, spare * VDIM)))
+    gate, up, token_slices, up_query, up_latent, down_rows, smalls, out_rows, down = run(
+        1, "open", OpenLine(dp, ctx, gate_proj),
         [
             (ExchangeCtx, slices(flat)), (ExchangeCtx, up_query), (ExchangeCtx, up_latent),
             (GatherDp, down_own),
-            (GatherAll, small.reshape(16, LANES)),
+            (GatherAll, small.reshape(16, LANES)), (GatherDp, out_padded), (GatherDp, down_proj),
         ],
-    )
-    smalls, down_proj = lax.optimization_barrier((smalls, down_proj))
+        (up_proj,), 16,
+    )
+    smalls, grad_branch = lax.optimization_barrier((smalls, grad_branch))
+    grad_branch = gather_xla(grad_branch)
+    down = down.reshape(f_part, D)
     down_rows = down_rows.reshape(d_part, LATENT)
     smalls = smalls.reshape(dp, ctx, 2 * tile)
     factor_all = smalls[lax.axis_index("dp"), :, tile : tile + own].reshape(group, 1)
@@ -1079,46 +1181,32 @@
     gain_post = smalls[:, :, cuts[2] : cuts[3]].reshape(1, D)
     gain_down = jnp.concatenate([gain_query, gain_latent, jnp.zeros((1, LANES), single)], axis=1)
 
-    out_padded = jnp.pad(out_proj, ((0, 0), (0, spare * VDIM)))
-    down = gather_dp(down_proj)
-
     normed_slices = token_slices.reshape(group, d_part).astype(single) * factor_all
     normed_in = (normed_slices * gain_in).astype(bfloat)
-    own_table = head_table(place * span + jnp.arange(own, dtype=jnp.int32) % span)
+    table = head_table(ctx * span)
+    own_table = lax.dynamic_slice_in_dim(table, place * span, span, 1)
+    own_table = jnp.tile(own_table, (1, batch, 1))
     parts = dot(normed_in, down_rows).astype(bfloat).reshape(ctx, own, LATENT)
     out_heads = out_padded.reshape(d_rows, ctx, heads * VDIM).transpose(1, 0, 2)
     ups = (up_query.reshape(ctx * q_rows, wide), up_latent.reshape(ctx * l_rows, wide))
-    table = head_table(jnp.arange(ctx * span, dtype=jnp.int32))
     outs = run(
         2, "forward",
-        ForwardLine(dp, ctx, parts, heads, batch, (gate_proj, up_proj), ups, out_padded, out_heads),
+        ForwardLine(dp, ctx, parts, heads, batch, (gate, up), ups, out_heads),
         (),
-        (gain_down, own_table, lengths, table, gate_proj, up_proj) + ups + (out_padded, out_heads),
+        (gain_down, own_table, lengths, table, gate, up) + ups + (out_heads,),
         56,
     )
     latents, latent_all, query, kv, totals, attn_all = outs[:6]
-    query_ups, latent_ups, out_rows, gate, up, out_heads = outs[6:]
+    query_ups, latent_ups, gate, up, out_heads = outs[6:]
     attn_all = attn_all.reshape(ctx * heads * VDIM, group)
-    gate = gate.reshape(D, f_part)
     branch = dot(attn_all, out_rows.reshape(d_part, ctx * heads * VDIM), 0, 1).astype(bfloat).reshape(batch, ctx, span, d_part)
-    middle, normed_mid, out_heads, up = run(
-        4, "middle", MiddleLine(dp, ctx, branch),
-        [
-            (GatherDp, out_heads.reshape(ctx * d_rows, heads * VDIM)),
-            (GatherDp, up.reshape(ctx * d_rows, f_part)),
-        ],
-        (flat, gain_post), 24,
+    gate, up = gate.reshape(D, f_part), up.reshape(D, f_part)
+    middle, normed_mid, branch_out, hidden, grad_gate, grad_up, out_heads = run(
+        4, "middle", MiddleLine(dp, ctx, branch, f_part),
+        [(GatherDp, out_heads.reshape(ctx * d_rows, heads * VDIM))],
+        (flat, gain_post, gate, up, down, grad_branch), 60,
     )
     normed_mid = normed_mid.reshape(group, D)
-    up = up.reshape(D, f_part)
-
-    gate_act = dot(normed_mid, gate)
-    up_act = dot(normed_mid, up)
-    sigma = jax.nn.sigmoid(gate_act)
-    hidden = (gate_act * sigma * up_act).astype(bfloat)
-    grad_hidden = dot(grad_branch, down, 1, 1)
-    grad_gate = (grad_hidden * up_act * (sigma * (1.0 + gate_act * (1.0 - sigma)))).astype(bfloat)
-    grad_up = (grad_hidden * (gate_act * sigma)).astype(bfloat)
     fused = group <= 1024
     if fused:
         parts, last = gate, (up,)
@@ -1138,10 +1226,6 @@
     columns_shape = (ctx, d_rows, f_part)
     grad_gate_proj = row_sums(grad_gate_proj).astype(bfloat).reshape(columns_shape)
     grad_up_proj = row_sums(grad_up_proj).astype(bfloat).reshape(columns_shape)
-    branch_out = dot(hidden, down).astype(bfloat)
-    branch_out, grad_attn_branch = lax.optimization_barrier((branch_out, grad_attn_branch))
-    branch_out = scatter_xla(branch_out).astype(single)
-    layer_out = (middle + branch_scale * branch_out).astype(bfloat)
 
     outs = run(
         8, "backward", BackwardLine(dp, ctx, grad_attn_branch, heads, batch, HEADS * VDIM),
@@ -1157,6 +1241,9 @@
     )
     grad_latents, grad_down, grad_out_proj, grad_query_ups, grad_latent_ups = outs[:5]
     grad_down_proj, grad_gate_proj, grad_up_proj = outs[5:]
+    branch_out, grad_down = lax.optimization_barrier((branch_out, grad_down))
+    branch_out = scatter_xla(branch_out.reshape(group, D)).astype(single)
+    layer_out = (middle + branch_scale * branch_out).astype(bfloat)
     grad_down = grad_down.reshape(group, LATENT)
     grad_normed_in = dot(grad_down, down_rows, 1, 1)
     grad_scaled = (grad_normed_in * gain_in).astype(bfloat).reshape(ctx, own, d_part)
@@ -1180,7 +1267,6 @@
         9, "close", CloseLine(dp, ctx, grad_scaled).lay_out(d_rows, FF),
         [
             (ExchangeDp, grad_rows.reshape(dp, d_rows, LATENT)),
-            (ExchangeDp, grad_out_proj),
             (ExchangeCtx, row_sums(grad_query_ups).astype(bfloat).reshape(ctx, q_rows, wide)),
             (ExchangeCtx, row_sums(grad_latent_ups).astype(bfloat).reshape(ctx, l_rows, wide)),
             (ExchangeAll, gain_sums.reshape(dp, ctx, 8, LANES)),
@@ -1188,8 +1274,8 @@
         (flat, grad_middle, grad_gate_proj, grad_up_proj),
         32,
     )
-    input_grad, grad_gate_proj, grad_up_proj, grad_rows, grad_out_proj = outs[:5]
-    grad_query_ups, grad_latent_ups, gain_sums = outs[5:]
+    input_grad, grad_gate_proj, grad_up_proj, grad_rows = outs[:4]
+    grad_query_ups, grad_latent_ups, gain_sums = outs[4:]
     grad_rows = jnp.sum(grad_rows, axis=0)
     gain_sums = jnp.sum(gain_sums.reshape(dp * ctx, tile), axis=0)
 

time: 776 us -> 698 us (0.90)
  Pallas kernels: 637 us -> 596 us
  matrix products: 50.5 us -> 14.3 us
    pallas_call x6, Pallas kernels: 637 us -> 596 us  [transfer(): pl.pallas_call(functools.partial(transfer_kernel, dp, ctx, line, pieces,...]
    dot_general x8 -> x4, matrix products: 50.5 us -> 14.3 us  [dot(): lax.dot_general(left, right, (((left_dim,), (right_dim,)), ((), ())), pre...]
    unnamed x92 -> x88, local copies, waits for them, and re-layouts: 17.8 us -> 21.8 us
  transfers between devices with their start and end apart: 3 -> 2, of which waited for: 0 -> 0; matrix products, arithmetic and copies ran while one was open for 9% -> 6% of each run, Pallas kernels for 59% -> 29%
where the time goes in v4:
time: 698 us; the launch traced here: 690 us
  Pallas kernels  596 us (85%)
  local copies, waits for them, and re-layouts  39.1 us (6%)
  other arithmetic  26.4 us (4%)
  between operations  14.8 us (2%)
  matrix products  14.3 us (2%)
    pallas_call x6, Pallas kernels, transfer(): pl.pallas_call(functools.partial(transfer_kernel, dp, ctx, line, pieces,...  596 us
    unnamed x88, local copies, waits for them, and re-layouts  21.8 us
    reduce_sum x6, other arithmetic, row_sums(): return jnp.sum(values.astype(single), axis=0)  17.1 us
    dot_general x4, matrix products, dot(): lax.dot_general(left, right, (((left_dim,), (right_dim,)), ((), ())), pre...  14.3 us
  transfers between devices with their start and end apart: 2, of which 0 were waited for; matrix products, arithmetic and copies ran while one was open for 6% of the time, Pallas kernels for 29%

profile of v4, /device:TPU:9, one launch (start us, length us, event | category | flops | bytes accessed | tf_op | source)
XLA Modules:
  0.0 690.4 jit_solution(1899357504341402344)
XLA Ops:
  7.2 2.4 reshape_reshape.3
  17.5 86.7 %open.1 = (bf16[8,80,800]{2,1,0:T(8,128)(2,1)S(1)}, bf16[8,80,800]{2,1,0:T(8,128)(2,1)S(1)}, bf16[8,128,320]{2,1,0:T(8,128)(2,1)S(1)}, bf16[8,24,640]{2,1,0:T(8,...) custom-call(bf16[80,6400]{1,0:T(8,128)(2,1)S(1)} %copy-done.14, ...), custom_call_target="tpu_custom_call" | custom-call | bytes 157286400 | tf_op jit(solution)/shard_map/open/pallas_call | solution.py:968
  104.2 1.9 copy-done.2
  115.2 2.9 convolution_convert_fusion
  118.7 142.7 %forward.1 = (f32[128,1152]{1,0:T(8,128)}, bf16[8,128,1152]{2,1,0:T(8,128)(2,1)}, bf16[8,128,640]{2,1,0:T(8,128)(2,1)}, bf16[8,128,640]{2,1,0:T(8,128)(2,1)}, f3...) custom-call(bf16[8,128,1152]{2,1,0:T(8,128)(2,1)} %bitcast.110, ...), custom_call_target="tpu_custom_call" | custom-call | bytes 157286400 | tf_op jit(solution)/shard_map/forward/pallas_call | solution.py:968
  261.4 4.3 convolution_convert_fusion.1
  267.6 74.8 %middle.1 = (f32[128,2560]{1,0:T(8,128)}, bf16[8,128,2560]{2,1,0:T(8,128)(2,1)}, bf16[8,128,2560]{2,1,0:T(8,128)(2,1)}, bf16[1024,800]{1,0:T(8,128)(2,1)}, bf16[...) custom-call(bf16[2,8,64,320]{3,2,1,0:T(8,128)(2,1)} %bitcast.106, ...), custom_call_target="tpu_custom_call" | custom-call | bytes 157286400 | tf_op jit(solution)/shard_map/middle/pallas_call | solution.py:968
  342.4 132.4 %middle_back.1 = (f32[128,2560]{1,0:T(8,128)}, f32[1,2560]{1,0:T(1,128)}, bf16[8,128,2560]{2,1,0:T(8,128)(2,1)}, bf16[800,2560]{1,0:T(8,128)(2,1)}, bf16[4,640,8...) custom-call(bf16[2560,800]{1,0:T(8,128)(2,1)} %bitcast.94, f32[128,2560]{1,0:T(8,128)} %get-tuple-element.81.refs_1_, ...), custom_call_target="tpu_custom_call" | custom-call | bytes 157286400 | tf_op jit(solution)/shard_map/middle_back/pallas_call | solution.py:968
  474.8 4.3 reduce_sum.141
  479.2 4.3 reduce_sum.142
  483.5 99.1 %backward.1 = (f32[128,1152]{1,0:T(8,128)}, bf16[8,128,1152]{2,1,0:T(8,128)(2,1)}, bf16[4,80,2560]{2,1,0:T(8,128)(2,1)}, bf16[4,192,640]{2,1,0:T(8,128)(2,1)}, b...) custom-call(bf16[8,128,2560]{2,1,0:T(8,128)(2,1)} %get-tuple-element, ...), custom_call_target="tpu_custom_call" | custom-call | bytes 157286400 | tf_op jit(solution)/shard_map/backward/pallas_call | solution.py:968
  582.7 1.3 copy.42
  584.9 3.9 multiply_reduce_fusion
  589.0 1.5 copy.40
  590.6 1.4 reduce_sum.144
  592.1 3.2 convolution_bitcast_fusion
  597.1 60.0 %close.1 = (f32[128,2560]{1,0:T(8,128)S(1)}, f32[80,6400]{1,0:T(8,128)S(1)}, f32[80,6400]{1,0:T(8,128)S(1)}, f32[4,80,1152]{2,1,0:T(8,128)S(1)}, bf16[8,24,640]{...) custom-call(bf16[8,128,320]{2,1,0:T(8,128)(2,1)S(1)} %bitcast.81, ...), custom_call_target="tpu_custom_call" | custom-call | bytes 157286400 | tf_op jit(solution)/shard_map/close/pallas_call | solution.py:968
  657.2 1.3 copy-done.3
  661.9 1.5 reduce_sum.150
  669.2 2.7 convert_reduce_fusion.1
  671.9 4.3 convert_reduce_fusion
  676.2 2.6 add_convert_fusion
  680.8 1.3 copy.57
  682.1 1.3 copy.58
  (156 shorter events, 33.4 us)
Async XLA Ops:
  7.2 2.5 copy-start
  7.2 260.4 %all-gather.2.cloned.1.call-start = ((), (), s32[]{:S(2)}) async-start(), calls=%async_computation.1 | async-start | bytes 5898240 | tf_op jit(solution)/shard_map/all_gather | solution.py:53
  11.2 1.9 copy-start.38
  11.3 1.9 copy-start.39
  11.3 1.9 copy-start.40
  11.3 1.9 slice-start.1
  11.3 1.9 slice-start.2
  11.7 2.5 copy-start.5
  11.7 2.5 copy-start.14
  104.2 1.9 copy-start.2
  111.5 564.6 %reduce-scatter.2.cloned.1.call-start = ((), (), s32[]{:S(2)}) async-start(), calls=%async_computation.2 | async-start | bytes 5898240 | tf_op jit(solution)/shard_map/reduce_scatter | solution.py:57
  112.2 3.0 copy-start.27
  115.2 2.9 copy-start.29
  118.7 142.7 %copy-start.25 = (bf16[4,80,2560]{2,1,0:T(8,128)(2,1)S(1)}, bf16[4,80,2560]{2,1,0:T(8,128)(2,1)}, u32[]{:S(2)}) copy-start(bf16[4,80,2560]{2,1,0:T(8,128)(2,1)} %copy-done.24) | copy-start | bytes 4915204
  582.7 2.0 copy-start.37
  588.8 3.2 copy-start.35
  588.8 3.2 copy-start.30
  592.1 3.3 copy-start.11
  661.9 2.4 copy-start.19
  663.4 2.6 copy-start.32
  663.5 3.7 copy-start.21
  666.2 2.3 slice-start
  676.2 2.6 copy-start.8
  678.8 2.0 copy-start.4
  (23 other events, 27.0 us)
Sparse Core Ops, SparseCore 0:
  111.7 78.2 all-gather.1
  582.8 89.3 reduce-scatter.1

commit v5 on v4

--- a/solution.py
+++ b/solution.py
@@ -84,6 +84,13 @@
 
 
 def gather_line(line, own_ref, all_ref, sems, idle=nothing, arrived=None):
+    steps = gather_steps(line, own_ref, all_ref, sems, arrived)
+    for step, _ in enumerate(steps):
+        if step < line.pairs - 1:
+            idle()
+
+
+def gather_steps(line, own_ref, all_ref, sems, arrived=None):
     send_left, send_right, send_twin, receive, receive_twin, local = sems
     pairs, pair, core = line.pairs, line.pair, line.core
 
@@ -103,7 +110,7 @@
         to_twin(own_ref, pair).wait_recv()
         arrived(pair)
     for step in range(1, pairs):
-        idle()
+        yield
 
         def from_left(slot=pair - step):
             block = all_ref.at[slot * 2 + core]
@@ -123,6 +130,7 @@
             slot = nearest(line, step)
             to_twin(own_ref, slot).wait_recv()
             arrived(slot)
+    yield
     if not arrived:
         keep.wait()
     for slot in range(pairs):
@@ -154,7 +162,12 @@
     return pl.CostEstimate(flops=0, transcendentals=0, bytes_accessed=size)
 
 
-def scatter_line(line, parts_ref, twin_ref, landed_ref, sems, idle=nothing, make=None):
+def scatter_line(line, parts_ref, twin_ref, landed_ref, sems, idle=nothing):
+    for _ in scatter_steps(line, parts_ref, twin_ref, landed_ref, sems):
+        idle()
+
+
+def scatter_steps(line, parts_ref, twin_ref, landed_ref, sems, make=None, begun=False):
     send_twin, receive_twin, send_left, send_right, from_left, from_right = sems
     pairs, pair = line.pairs, line.pair
     to_twin, to_right, to_left = travels(line, parts_ref, twin_ref, landed_ref, sems)
@@ -169,11 +182,11 @@
             make(slot)
         to_twin(slot).start()
 
-    todo = list(range(pairs))
-    for _ in range(2 if make else pairs):
+    todo = [] if begun else list(range(pairs))
+    for _ in range(2 if make else len(todo)):
         prepare(todo.pop(0))
     for step in range(pairs - 1, 0, -1):
-        idle()
+        yield
 
         def pass_on(slot, arrives, travel):
             to_twin(slot).wait_recv()
@@ -698,55 +711,95 @@
             jax.ShapeDtypeStruct((1, D), single),
             jax.ShapeDtypeStruct((ctx, own, D), bfloat),
             jax.ShapeDtypeStruct((f_part, D), bfloat),
-            jax.ShapeDtypeStruct(self.cut, bfloat),
-            jax.ShapeDtypeStruct(self.cut, bfloat),
+            jax.ShapeDtypeStruct(self.cut[1:], bfloat),
+            jax.ShapeDtypeStruct(self.cut[1:], bfloat),
         ]
         self.in_vmem = [True, True, False, True, False, False]
         self.scratch = (
             [pltpu.VMEM(shape, bfloat), pltpu.VMEM((2,) + self.cut, bfloat)]
-            + scatter_scratch(ctx, shape, bfloat) + gather_sems(ctx)
-            + [pltpu.SemaphoreType.DMA((dp,))] * 4
+            + scatter_scratch(ctx, (own // 2, D), bfloat) + gather_sems(ctx)
+            + [pltpu.SemaphoreType.DMA((2, dp - 1))] * 2 + [pltpu.VMEM((2, dp - 1) + self.cut[1:], bfloat)]
+            + [pltpu.SemaphoreType.DMA]
             + ([pltpu.VMEM((ctx,) + shape, bfloat)] if fused else [])
         )
         self.base = len(self.scratch)
+        self.second = self.base + 6
         group = ctx * own
-        for size in (D, f_part, D):
+        for size in (D, f_part):
             self.scratch = self.scratch + [pltpu.VMEM((group, size), bfloat), pltpu.SemaphoreType.DMA]
+        self.scratch = self.scratch + [
+            pltpu.VMEM((2, group, D // 4), bfloat), pltpu.SemaphoreType.DMA((2,))
+        ]
+        self.scratch = self.scratch + scatter_scratch(ctx, (own // 2, D), bfloat) + gather_sems(ctx)
         self.elsewhere = (3, 6, 7)
 
     def run(self, line, extra, source, results, scratch):
         middle_ref, cotangent_ref, gain_ref, grads = extra[0], extra[1], extra[2], extra[4:6]
-        normed_mid_ref, hidden_ref, branch_ref = scratch[self.base :: 2]
+        normed_mid_ref, hidden_ref, branch_ref = scratch[self.base : self.second : 2]
         loads = [
             pltpu.make_async_copy(extra[place], scratch[self.base + 2 * index], scratch[self.base + 2 * index + 1])
-            for index, place in enumerate(self.elsewhere)
+            for index, place in enumerate(self.elsewhere[:2])
         ]
-        for load in loads:
+
+        def branch_load(part):
+            span = slice(part * (D // 4), (part + 1) * (D // 4))
+            sem = scratch[self.base + 5].at[part % 2]
+            return pltpu.make_async_copy(extra[7].at[:, span], branch_ref.at[part % 2], sem)
+
+        for load in loads + [branch_load(0), branch_load(1)]:
             load.start()
         grad_middle_ref, gain_sum_ref, all_ref, down_ref = results[:4]
         landed = results[4:]
         own_ref, cut_ref = scratch[:2]
-        travel, sems = scratch[2:4], scratch[4:10]
-        pushes = scratch[16:20]
+        send, receive, halves_ref = scratch[16:19]
         row = lax.axis_index("dp")
         height = D // self.dp
 
-        def push(index, target):
+        levels = [list(range(self.dp.bit_length() - 1)), list(range(self.dp.bit_length() - 1))[::-1]]
+
+        def bit(level):
+            return (row // (1 << level)) % 2
+
+        def flipped(step):
+            return sum(((bit(level) + (step >> level)) % 2) * (1 << level) for level in levels[0])
+
+        def target_of(index, phase, part, own):
+            order = levels[index]
+            level = order[phase]
+            total = sum(bit(done) * (1 << done) for done in order[:phase])
+            total += (bit(level) if own else 1 - bit(level)) * (1 << level)
+            return total + sum(((part // (1 << k)) % 2) * (1 << rest) for k, rest in enumerate(order[phase + 1 :]))
+
+        def exchange(index, phase, part):
+            level = levels[index][phase]
+            place = self.dp - (self.dp >> phase) + part
             return remote(
-                cut_ref.at[index, target], landed[index].at[row],
-                pushes[2 * index].at[target], pushes[2 * index + 1].at[row], {"dp": target},
+                cut_ref.at[index, target_of(index, phase, part, False)], halves_ref.at[index, place],
+                send.at[index, place], receive.at[index, place],
+                {"dp": row + (1 - 2 * bit(level)) * (1 << level)},
             )
 
-        def keep(index):
-            return pltpu.make_async_copy(
-                cut_ref.at[index, row], landed[index].at[row], pushes[2 * index].at[row]
-            )
+        def parts_in(phase):
+            return self.dp >> (phase + 1)
+
+        def reduce(index, phase):
+            last = phase == len(levels[index]) - 1
+            for part in range(parts_in(phase)):
+                exchange(index, phase, part).wait_recv()
+                goal = target_of(index, phase, part, True)
+                place = self.dp - (self.dp >> phase) + part
+                total = cut_ref[index, goal].astype(single) + halves_ref[index, place].astype(single)
+                cut_ref[index, goal] = total.astype(bfloat)
+            if not last:
+                for part in range(parts_in(phase + 1)):
+                    exchange(index, phase + 1, part).start()
 
         def rows_work(step):
             if step == 1:
                 loads[0].wait()
-            if height % LANES == 0:
-                target = (row + step) % self.dp
+            aligned = height % LANES == 0
+            if aligned:
+                target = flipped(step % self.dp)
                 columns = pl.ds(pl.multiple_of(target * height, LANES), height)
             else:
                 target = step % self.dp
@@ -754,25 +807,24 @@
             left = normed_mid_ref[:, columns].T
             for index in range(2):
                 cut_ref[index, target] = dot(left, grads[index][...]).astype(bfloat)
-                if height % LANES == 0 and step < self.dp:
-                    push(index, target).start()
-            if step == self.dp:
-                last_rows()
-
-        def last_rows():
-            for index in range(2):
-                for step in range(1, self.dp):
-                    if height % LANES:
-                        push(index, (row + step) % self.dp).start()
-                keep(index).start()
+                level = levels[index][0]
+                if aligned and (step % self.dp >> level) % 2:
+                    rest = enumerate(levels[index][1:])
+                    part = sum(((bit(low) + (step >> low)) % 2) * (1 << k) for k, low in rest)
+                    exchange(index, 0, part).start()
+                elif not aligned and step == self.dp:
+                    for part in range(parts_in(0)):
+                        exchange(index, 0, part).start()
 
         def down_work(part):
             width = D // 4
             if part == 0:
                 loads[1].wait()
-                loads[2].wait()
+            branch_load(part).wait()
             span = slice(part * width, (part + 1) * width)
-            down_ref[:, span] = dot(hidden_ref[...].T, branch_ref[:, span]).astype(bfloat)
+            down_ref[:, span] = dot(hidden_ref[...].T, branch_ref[part % 2]).astype(bfloat)
+            if part < 2:
+                branch_load(part + 2).start()
 
         todo = [functools.partial(rows_work, step) for step in range(1, self.dp + 1)]
         todo += [functools.partial(down_work, part) for part in range(4)]
@@ -789,31 +841,70 @@
             total = dot(grads[0][rows], source[...], 1, 1) + dot(grads[1][rows], extra[8][...], 1, 1)
             parts_ref[pl.ds(slot * 2, 2)] = total.astype(bfloat).reshape((2,) + own_ref.shape)
 
-        scatter_line(line, parts_ref, *travel, sems, idle, make if self.fused else None)
-        scatter_total(line, parts_ref, *travel, sems, grad_middle_ref)
+        half = own_ref.shape[0] // 2
+        spans = [pl.ds(0, half), pl.ds(half, half)]
+        parts = [parts_ref.at[:, span] for span in spans]
+        travel = [scratch[2:10], scratch[self.second : self.second + 8]]
+        gather = [scratch[10:16], scratch[self.second + 8 : self.second + 14]]
+
+        def make_both(slot):
+            if self.fused:
+                make(slot)
+            travels(line, parts[1], *travel[1][:2], travel[1][2:])[0](slot).start()
+
+        sums = [
+            scatter_steps(line, parts[0], *travel[0][:2], travel[0][2:], make_both),
+            scatter_steps(line, parts[1], *travel[1][:2], travel[1][2:], None, True),
+        ]
+        gathers = [
+            gather_steps(line, own_ref.at[span], all_ref.at[:, span], sems)
+            for span, sems in zip(spans, gather)
+        ]
         gain_sum_ref[...] = jnp.zeros_like(gain_sum_ref)
 
-        def chunk(rows):
-            normed, factor = normalize(middle_ref[rows])
-            gradient = grad_middle_ref[rows]
-            gain_sum_ref[...] += jnp.sum(gradient * normed, axis=0, keepdims=True)
-            back = cotangent_ref[rows].astype(single) + norm_back(gradient * gain_ref[...], normed, factor)
-            grad_middle_ref[rows] = back
-            own_ref[rows] = (branch_scale * back).astype(bfloat)
-
-        by_chunks(own_ref.shape[0], chunk)
-        gather_line(line, own_ref, all_ref, scratch[10:16], lambda: idle(2))
+        def finish(index):
+            span = spans[index]
+            scatter_total(line, parts[index], *travel[index][:2], travel[index][2:], grad_middle_ref.at[span])
+
+            def chunk(rows):
+                normed, factor = normalize(middle_ref[rows])
+                gradient = grad_middle_ref[rows]
+                gain_sum_ref[...] += jnp.sum(gradient * normed, axis=0, keepdims=True)
+                back = norm_back(gradient * gain_ref[...], normed, factor)
+                back = cotangent_ref[rows].astype(single) + back
+                grad_middle_ref[rows] = back
+                own_ref[rows] = (branch_scale * back).astype(bfloat)
+
+            by_chunks(half, chunk, index * half)
+
+        for _ in sums[0]:
+            idle()
+        next(sums[1], None)
+        finish(0)
+        next(gathers[0])
+        for _ in range(line.pairs - 1):
+            next(sums[1], None)
+            next(gathers[0])
+            idle(1)
+        finish(1)
+        next(gathers[1])
         idle(len(todo))
+        phases = len(levels[0])
+        for phase in range(phases - 1):
+            for index in range(2):
+                reduce(index, phase)
+            next(gathers[1])
+        for _ in gathers[1]:
+            pass
+        next(gathers[0], None)
         for index in range(2):
-            for other in range(self.dp):
-                @pl.when(row != other)
-                def _():
-                    push(index, other).wait_send()
-                    remote(
-                        cut_ref.at[index, other], landed[index].at[other],
-                        pushes[2 * index].at[other], pushes[2 * index + 1].at[other], {"dp": other},
-                    ).wait_recv()
-            keep(index).wait()
+            reduce(index, phases - 1)
+            out = pltpu.make_async_copy(cut_ref.at[index, row], landed[index], scratch[19])
+            out.start()
+            out.wait()
+            for phase in range(phases):
+                for part in range(parts_in(phase)):
+                    exchange(index, phase, part).wait_send()
 
 
 class CloseLine:
@@ -851,9 +942,9 @@
         by_chunks(out_ref.shape[0], chunk)
 
 
-def by_chunks(total, work):
+def by_chunks(total, work, first=0):
     def step(index, carry):
-        work(pl.ds(pl.multiple_of(index * 16, 16), 16))
+        work(pl.ds(pl.multiple_of(first + index * 16, 16), 16))
         return carry
 
     lax.fori_loop(0, total // 16, step, 0)
@@ -1221,11 +1312,11 @@
             middle, cotangent.reshape(own, D), gain_post, normed_mid, grad_gate, grad_up, hidden,
             grad_branch,
         ) + last,
-        60,
+        62,
     )
     columns_shape = (ctx, d_rows, f_part)
-    grad_gate_proj = row_sums(grad_gate_proj).astype(bfloat).reshape(columns_shape)
-    grad_up_proj = row_sums(grad_up_proj).astype(bfloat).reshape(columns_shape)
+    grad_gate_proj = grad_gate_proj.reshape(columns_shape)
+    grad_up_proj = grad_up_proj.reshape(columns_shape)
 
     outs = run(
         8, "backward", BackwardLine(dp, ctx, grad_attn_branch, heads, batch, HEADS * VDIM),

time: 698 us -> 683 us (0.979)
  Pallas kernels: 596 us -> 583 us
    pallas_call x6, Pallas kernels: 596 us -> 583 us  [transfer(): pl.pallas_call(functools.partial(transfer_kernel, dp, ctx, line, pieces,...]
    reduce_sum x6 -> x4, other arithmetic: 17.1 us -> 8.15 us  [row_sums(): return jnp.sum(values.astype(single), axis=0)]
  transfers between devices with their start and end apart: 2 -> 2, of which waited for: 0 -> 0; matrix products, arithmetic and copies ran while one was open for 6% -> 6% of each run, Pallas kernels for 29% -> 30%
where the time goes in v5:
time: 683 us; the launch traced here: 676 us
  Pallas kernels  583 us (85%)
  local copies, waits for them, and re-layouts  44.6 us (7%)
  other arithmetic  19.5 us (3%)
  between operations  14.8 us (2%)
  matrix products  13.6 us (2%)
    pallas_call x6, Pallas kernels, transfer(): pl.pallas_call(functools.partial(transfer_kernel, dp, ctx, line, pieces,...  583 us
    unnamed x88, local copies, waits for them, and re-layouts  21.9 us
  transfers between devices with their start and end apart: 2, of which 0 were waited for; matrix products, arithmetic and copies ran while one was open for 6% of the time, Pallas kernels for 30%

profile of v5, /device:TPU:9, one launch (start us, length us, event | category | flops | bytes accessed | tf_op | source)
XLA Modules:
  0.0 675.6 jit_solution(1513959981439033236)
XLA Ops:
  7.2 2.4 reshape_reshape.3
  14.4 1.7 copy.51
  20.8 86.7 %open.1 = (bf16[8,80,800]{2,1,0:T(8,128)(2,1)S(1)}, bf16[8,80,800]{2,1,0:T(8,128)(2,1)S(1)}, bf16[8,128,320]{2,1,0:T(8,128)(2,1)S(1)}, bf16[8,24,640]{2,1,0:T(8,...) custom-call(bf16[80,6400]{1,0:T(8,128)(2,1)S(1)} %copy-done.14, ...), custom_call_target="tpu_custom_call" | custom-call | bytes 157286400 | tf_op jit(solution)/shard_map/open/pallas_call | solution.py:1059
  107.5 1.9 copy-done.2
  118.4 2.9 convolution_convert_fusion
  122.0 142.8 %forward.1 = (f32[128,1152]{1,0:T(8,128)}, bf16[8,128,1152]{2,1,0:T(8,128)(2,1)}, bf16[8,128,640]{2,1,0:T(8,128)(2,1)}, bf16[8,128,640]{2,1,0:T(8,128)(2,1)}, f3...) custom-call(bf16[8,128,1152]{2,1,0:T(8,128)(2,1)} %bitcast.108, ...), custom_call_target="tpu_custom_call" | custom-call | bytes 157286400 | tf_op jit(solution)/shard_map/forward/pallas_call | solution.py:1059
  264.9 4.3 convolution_convert_fusion.1
  271.0 74.6 %middle.1 = (f32[128,2560]{1,0:T(8,128)}, bf16[8,128,2560]{2,1,0:T(8,128)(2,1)}, bf16[8,128,2560]{2,1,0:T(8,128)(2,1)}, bf16[1024,800]{1,0:T(8,128)(2,1)}, bf16[...) custom-call(bf16[2,8,64,320]{3,2,1,0:T(8,128)(2,1)} %bitcast.104, ...), custom_call_target="tpu_custom_call" | custom-call | bytes 157286400 | tf_op jit(solution)/shard_map/middle/pallas_call | solution.py:1059
  345.7 122.3 %middle_back.1 = (f32[128,2560]{1,0:T(8,128)}, f32[1,2560]{1,0:T(1,128)}, bf16[8,128,2560]{2,1,0:T(8,128)(2,1)}, bf16[800,2560]{1,0:T(8,128)(2,1)}, bf16[640,800]{1,0:T(8,128)(2,1)}, /*index=5*/bf16[640,800]{1,0:T(8,128)(2,1)}) custom-call(bf16[2560,800]{1,0:T(8,128)(2,1)} %bitcast.94, f32[128,2560]{1,0:T(8,128)} %get-tuple-element.81.refs_1_, ...), custom_call_target="tpu_custom_call" | custom-call | bytes 157286400 | tf_op jit(solution)/shard_map/middle_back/pallas_call | solution.py:1059
  468.0 97.5 %backward.1 = (f32[128,1152]{1,0:T(8,128)}, bf16[8,128,1152]{2,1,0:T(8,128)(2,1)}, bf16[4,80,2560]{2,1,0:T(8,128)(2,1)}, bf16[4,192,640]{2,1,0:T(8,128)(2,1)}, b...) custom-call(bf16[8,128,2560]{2,1,0:T(8,128)(2,1)} %get-tuple-element, ...), custom_call_target="tpu_custom_call" | custom-call | bytes 157286400 | tf_op jit(solution)/shard_map/backward/pallas_call | solution.py:1059
  565.6 1.3 copy.42
  567.2 1.2 multiply_reduce_fusion.2
  569.8 3.6 multiply_reduce_fusion
  573.6 1.6 copy.40
  576.5 2.8 convolution_bitcast_fusion
  581.2 59.0 %close.1 = (f32[128,2560]{1,0:T(8,128)S(1)}, f32[80,6400]{1,0:T(8,128)S(1)}, f32[80,6400]{1,0:T(8,128)S(1)}, f32[4,80,1152]{2,1,0:T(8,128)S(1)}, bf16[8,24,640]{...) custom-call(bf16[8,128,320]{2,1,0:T(8,128)(2,1)S(1)} %bitcast.81, ...), custom_call_target="tpu_custom_call" | custom-call | bytes 157286400 | tf_op jit(solution)/shard_map/close/pallas_call | solution.py:1059
  640.3 1.3 copy-done.3
  645.0 1.5 reduce_sum.124
  652.9 1.6 pad_maximum_fusion.1
  654.4 2.6 convert_reduce_fusion.1
  657.1 4.3 convert_reduce_fusion
  661.4 2.6 add_convert_fusion
  666.0 1.3 copy.57
  667.3 1.3 copy.58
  (153 shorter events, 37.6 us)
Async XLA Ops:
  7.2 2.5 copy-start
  7.2 263.9 %all-gather.2.cloned.1.call-start = ((), (), s32[]{:S(2)}) async-start(), calls=%async_computation.1 | async-start | bytes 5898240 | tf_op jit(solution)/shard_map/all_gather | solution.py:53
  10.9 5.3 copy-start.32
  11.2 5.9 copy-start.38
  11.3 5.9 copy-start.39
  11.3 5.9 copy-start.40
  11.3 5.9 copy-start.41
  11.3 6.0 slice-start
  11.3 6.0 slice-start.1
  11.3 6.0 copy-start.36
  12.4 5.0 copy-start.5
  12.4 5.0 copy-start.14
  12.4 5.0 copy-start.23
  114.8 546.6 %reduce-scatter.2.cloned.1.call-start = ((), (), s32[]{:S(2)}) async-start(), calls=%async_computation.2 | async-start | bytes 5898240 | tf_op jit(solution)/shard_map/reduce_scatter | solution.py:57
  115.4 3.0 copy-start.28
  118.4 2.9 copy-start.30
  122.0 142.8 %copy-start.26 = (bf16[4,80,2560]{2,1,0:T(8,128)(2,1)S(1)}, bf16[4,80,2560]{2,1,0:T(8,128)(2,1)}, u32[]{:S(2)}) copy-start(bf16[4,80,2560]{2,1,0:T(8,128)(2,1)} %copy-done.25) | copy-start | bytes 4915204
  565.6 4.0 copy-start.37
  566.9 2.9 copy-start.33
  573.6 2.9 copy-start.31
  576.5 3.0 copy-start.11
  645.0 3.6 copy-start.20
  647.9 3.6 copy-start.22
  661.4 2.6 copy-start.8
  (22 other events, 26.5 us)
Sparse Core Ops, SparseCore 0:
  114.9 78.2 all-gather.1
  565.7 87.7 reduce-scatter.1

commit v6 on v5

--- a/solution.py
+++ b/solution.py
@@ -908,29 +908,68 @@
 
 
 class CloseLine:
-    reach = "ctx"
-    held = False
-
-    def __init__(self, dp, ctx, parts):
+    reach = "both"
+    held = True
+
+    def __init__(self, dp, ctx, parts, rows, width, arrived):
         self.dp, self.ctx, self.parts = dp, ctx, parts
-        own = parts.shape[1]
+        own, latent = parts.shape[1:]
+        cut = jax.ShapeDtypeStruct((ctx, own, dp * rows), bfloat)
+        self.scaled = ExchangeCtx(dp, ctx, cut)
+        self.sums = [
+            ExchangeDp(dp, ctx, jax.ShapeDtypeStruct(shape, single))
+            for shape in ((dp, rows, latent), (dp, 8, LANES))
+        ]
         self.result = [jax.ShapeDtypeStruct((own, D), single)]
-        self.in_vmem = [True]
-        self.scratch = [pltpu.VMEM(parts.shape, bfloat)] + pair_sems(ctx)
-
-    def lay_out(self, rows, width):
         self.result += [jax.ShapeDtypeStruct((rows, width), single)] * 2
-        self.in_vmem += [True] * 2
-        return self
+        self.result += [jax.ShapeDtypeStruct(item.shape[1:], single) for item in arrived]
+        self.result += [piece.result for piece in self.sums]
+        self.in_vmem = [True] * 5 + [False] * 2
+        self.scratch = [pltpu.VMEM(cut.shape, bfloat)] * 2 + pair_sems(ctx)
+        for piece in self.sums:
+            self.scratch = self.scratch + [pltpu.VMEM(piece.parts.shape, single)] + piece.scratch
+        for item in arrived:
+            self.scratch = self.scratch + [pltpu.VMEM(item.shape, bfloat), pltpu.SemaphoreType.DMA]
+        self.elsewhere = (8, 9)
 
     def run(self, line, extra, source, results, scratch):
         tokens_ref, grad_middle_ref = extra[:2]
-        out_ref, landed_ref = results[0], scratch[0]
-        copies = ExchangeCtx(self.dp, self.ctx, self.parts).copies(source, landed_ref, *scratch[1:4])
+        down_rows_ref, normed_ref, slices_ref, gain_ref = extra[4:8]
+        out_ref, landed_ref, send_ref = results[0], scratch[0], scratch[1]
+        rows_ref, small_ref = scratch[5], scratch[9]
+        loads = [
+            pltpu.make_async_copy(extra[8 + k], scratch[13 + 2 * k], scratch[14 + 2 * k]) for k in range(2)
+        ]
+        for load in loads:
+            load.start()
+        group = self.ctx * source.shape[1]
+        height = rows_ref.shape[1]
+        gradient = source[...].reshape(group, source.shape[2])
+        grad_in = dot(gradient, down_rows_ref[...], 1, 1)
+        send_ref[...] = (grad_in * gain_ref[...]).astype(bfloat).reshape(send_ref.shape)
+        copies = self.scaled.copies(send_ref, landed_ref, *scratch[2:5])
         for copy in copies:
+            copy.start()
+        sums = dot(normed_ref[...].T, gradient)
+        gains = jnp.sum(grad_in * slices_ref[...], axis=0, keepdims=True)
+        small_ref[...] = jnp.zeros_like(small_ref)
+        for row in range(self.dp):
+            span = slice(row * height, (row + 1) * height)
+            rows_ref[row] = sums[span]
+            small_ref[row, 0:1, 0:height] = gains[:, span]
+        later = self.sums[0].copies(rows_ref, results[5], *scratch[6:9])
+        later += self.sums[1].copies(small_ref, results[6], *scratch[10:13])
+        for copy in later:
             copy.start()
         for index in range(2):
             regroup(extra[2 + index], results[1 + index], self.dp, self.ctx, False)
+        for index, load in enumerate(loads):
+            load.wait()
+            parts = scratch[13 + 2 * index]
+            total = parts[0].astype(single)
+            for row in range(1, self.dp):
+                total = total + parts[row].astype(single)
+            results[3 + index][...] = total
         for copy in copies:
             copy.wait()
         ungroup(landed_ref, out_ref, self.dp, self.ctx)
@@ -940,6 +979,8 @@
             out_ref[rows] = grad_middle_ref[rows] + norm_back(out_ref[rows], normed, factor)
 
         by_chunks(out_ref.shape[0], chunk)
+        for copy in later:
+            copy.wait()
 
 
 def by_chunks(total, work, first=0):
@@ -1335,12 +1376,6 @@
     branch_out, grad_down = lax.optimization_barrier((branch_out, grad_down))
     branch_out = scatter_xla(branch_out.reshape(group, D)).astype(single)
     layer_out = (middle + branch_scale * branch_out).astype(bfloat)
-    grad_down = grad_down.reshape(group, LATENT)
-    grad_normed_in = dot(grad_down, down_rows, 1, 1)
-    grad_scaled = (grad_normed_in * gain_in).astype(bfloat).reshape(ctx, own, d_part)
-    grad_rows = dot(normed_in, grad_down, 0, 0)
-    last = jnp.sum(grad_normed_in * normed_slices, axis=0)[:, None]
-    grad_rows = jnp.concatenate([grad_rows[:, : LATENT - 1], last], axis=1)
     normed_query, _ = normalize(latents[:, :QRANK])
     normed_latent, _ = normalize(latents[:, QRANK : QRANK + KVRANK])
     grad_query_normed = grad_latents[:, :QRANK]
@@ -1355,18 +1390,21 @@
     )
     gain_sums = jnp.pad(gain_sums, ((0, 0), (0, 0), (0, tile - gain_sums.shape[2])))
     outs = run(
-        9, "close", CloseLine(dp, ctx, grad_scaled).lay_out(d_rows, FF),
+        9, "close",
+        CloseLine(dp, ctx, grad_down, d_rows, FF, (grad_down_proj, grad_out_proj)),
         [
-            (ExchangeDp, grad_rows.reshape(dp, d_rows, LATENT)),
             (ExchangeCtx, row_sums(grad_query_ups).astype(bfloat).reshape(ctx, q_rows, wide)),
             (ExchangeCtx, row_sums(grad_latent_ups).astype(bfloat).reshape(ctx, l_rows, wide)),
             (ExchangeAll, gain_sums.reshape(dp, ctx, 8, LANES)),
         ],
-        (flat, grad_middle, grad_gate_proj, grad_up_proj),
-        32,
-    )
-    input_grad, grad_gate_proj, grad_up_proj, grad_rows = outs[:4]
-    grad_query_ups, grad_latent_ups, gain_sums = outs[4:]
+        (
+            flat, grad_middle, grad_gate_proj, grad_up_proj, down_rows, normed_in, normed_slices, gain_in,
+            grad_down_proj, grad_out_proj,
+        ),
+        48,
+    )
+    input_grad, grad_gate_proj, grad_up_proj, grad_down_proj, grad_out_proj, grad_rows, in_sums = outs[:7]
+    grad_query_ups, grad_latent_ups, gain_sums = outs[7:]
     grad_rows = jnp.sum(grad_rows, axis=0)
     gain_sums = jnp.sum(gain_sums.reshape(dp * ctx, tile), axis=0)
 
@@ -1380,7 +1418,7 @@
     return (
         layer_out.reshape(batch, span, D),
         input_grad.reshape(batch, span, D),
-        grad_rows[:, LATENT - 1],
+        jnp.sum(in_sums, axis=0)[0, :d_rows],
         gain_sums[d_rows : d_rows + q_rows],
         gain_sums[d_rows + q_rows : d_rows + up_rows],
         gain_sums[:d_rows],
@@ -1390,10 +1428,10 @@
             [grad_rows[:, QRANK : QRANK + KVRANK], grad_rows[:, rope_start : rope_start + ROPE]], axis=1
         ),
         grad_latent_up,
-        row_sums(grad_out_proj),
+        grad_out_proj,
         grad_gate_proj,
         grad_up_proj,
-        row_sums(grad_down_proj),
+        grad_down_proj,
     )
 
 

time: 683 us -> 676 us (0.990)
  waiting for transfers between devices: 0.04 us -> 8.31 us
  other arithmetic: 19.5 us -> 11.7 us
    reduce_scatter x1, waiting for transfers between devices: 0.01 us -> 8.27 us  [scatter_xla(): return lax.psum_scatter(values, 'ctx', scatter_dimension=0, tiled=True)]
    unnamed x88 -> x80, local copies, waits for them, and re-layouts: 21.9 us -> 21.9 us
  transfers between devices with their start and end apart: 2 -> 2, of which waited for: 0 -> 1; matrix products, arithmetic and copies ran while one was open for 6% -> 4% of each run, Pallas kernels for 30% -> 30%
where the time goes in v6:
time: 676 us; the launch traced here: 669 us
  Pallas kernels  586 us (87%)
  local copies, waits for them, and re-layouts  40.4 us (6%)
  between operations  14.7 us (2%)
  other arithmetic  11.7 us (2%)
  waiting for transfers between devices  8.31 us (1%)
  matrix products  7.25 us (1%)
    pallas_call x6, Pallas kernels, transfer(): pl.pallas_call(functools.partial(transfer_kernel, dp, ctx, line, pieces,...  586 us
    unnamed x80, local copies, waits for them, and re-layouts  21.9 us
  transfers between devices with their start and end apart: 2, of which 1 were waited for; matrix products, arithmetic and copies ran while one was open for 4% of the time, Pallas kernels for 30%

profile of v6, /device:TPU:9, one launch (start us, length us, event | category | flops | bytes accessed | tf_op | source)
XLA Modules:
  0.0 668.7 jit_solution(17491193168617722388)
XLA Ops:
  7.2 2.4 reshape_reshape.3
  12.4 1.1 pad.21
  16.7 1.2 copy-done.8
  17.9 1.2 copy-done.9
  19.1 86.7 %open.1 = (bf16[8,80,800]{2,1,0:T(8,128)(2,1)S(1)}, bf16[8,80,800]{2,1,0:T(8,128)(2,1)S(1)}, bf16[8,128,320]{2,1,0:T(8,128)(2,1)S(1)}, bf16[8,24,640]{2,1,0:T(8,...) custom-call(bf16[80,6400]{1,0:T(8,128)(2,1)S(1)} %copy-done.7, ...), custom_call_target="tpu_custom_call" | custom-call | bytes 157286400 | tf_op jit(solution)/shard_map/open/pallas_call | solution.py:1100
  105.8 1.9 copy-done.2
  112.6 1.2 copy-done.19
  118.4 2.9 convolution_convert_fusion
  122.0 139.8 %forward.1 = (f32[128,1152]{1,0:T(8,128)}, bf16[8,128,1152]{2,1,0:T(8,128)(2,1)}, bf16[8,128,640]{2,1,0:T(8,128)(2,1)}, bf16[8,128,640]{2,1,0:T(8,128)(2,1)}, f3...) custom-call(bf16[8,128,1152]{2,1,0:T(8,128)(2,1)} %bitcast.102, ...), custom_call_target="tpu_custom_call" | custom-call | bytes 157286400 | tf_op jit(solution)/shard_map/forward/pallas_call | solution.py:1100
  261.8 4.3 convolution_convert_fusion.1
  266.1 1.2 copy.38
  268.0 76.3 %middle.1 = (f32[128,2560]{1,0:T(8,128)}, bf16[8,128,2560]{2,1,0:T(8,128)(2,1)}, bf16[8,128,2560]{2,1,0:T(8,128)(2,1)}, bf16[1024,800]{1,0:T(8,128)(2,1)}, bf16[...) custom-call(bf16[2,8,64,320]{3,2,1,0:T(8,128)(2,1)} %bitcast.99, ...), custom_call_target="tpu_custom_call" | custom-call | bytes 157286400 | tf_op jit(solution)/shard_map/middle/pallas_call | solution.py:1100
  344.3 120.8 %middle_back.1 = (f32[128,2560]{1,0:T(8,128)}, f32[1,2560]{1,0:T(1,128)}, bf16[8,128,2560]{2,1,0:T(8,128)(2,1)}, bf16[800,2560]{1,0:T(8,128)(2,1)}, bf16[640,800]{1,0:T(8,128)(2,1)}, /*index=5*/bf16[640,800]{1,0:T(8,128)(2,1)}) custom-call(bf16[2560,800]{1,0:T(8,128)(2,1)} %bitcast.90, f32[128,2560]{1,0:T(8,128)} %get-tuple-element.84.refs_1_, ...), custom_call_target="tpu_custom_call" | custom-call | bytes 157286400 | tf_op jit(solution)/shard_map/middle_back/pallas_call | solution.py:1100
  465.1 98.9 %backward.1 = (f32[128,1152]{1,0:T(8,128)}, bf16[8,128,1152]{2,1,0:T(8,128)(2,1)}, bf16[4,80,2560]{2,1,0:T(8,128)(2,1)}, bf16[4,192,640]{2,1,0:T(8,128)(2,1)}, b...) custom-call(bf16[8,128,2560]{2,1,0:T(8,128)(2,1)} %get-tuple-element, ...), custom_call_target="tpu_custom_call" | custom-call | bytes 157286400 | tf_op jit(solution)/shard_map/backward/pallas_call | solution.py:1100
  565.3 1.4 bitcast_multiply_fusion
  567.0 1.1 multiply_reduce_fusion.3
  568.4 1.4 reduce_sum.99
  571.0 63.8 %close.1 = (f32[128,2560]{1,0:T(8,128)}, f32[80,6400]{1,0:T(8,128)}, f32[80,6400]{1,0:T(8,128)}, f32[200,2560]{1,0:T(8,128)}, f32[80,2560]{1,0:T(8,128)S(1)}, /*...) custom-call(bf16[8,128,1152]{2,1,0:T(8,128)(2,1)} %get-tuple-element, ...), custom_call_target="tpu_custom_call" | custom-call | bytes 157286400 | tf_op jit(solution)/shard_map/close/pallas_call | solution.py:1100
  635.8 1.5 reduce_sum.108
  642.8 8.3 %reduce-scatter.2.cloned.1.call-done = bf16[128,2560]{1,0:T(8,128)(2,1)} async-done(((bf16[1024,2560]{1,0:T(8,128)(2,1)}), bf16[128,2560]{1,0:T(8,128)(2,1)}) %reduce-scatter.2.cloned.1.call-update) | async-done | bytes 655376 | tf_op jit(solution)/shard_map/reduce_scatter | solution.py:57
  651.1 2.1 add_convert_fusion
  655.7 1.3 copy.56
  658.0 1.3 copy.57
  660.3 1.3 copy.58
  (140 shorter events, 30.6 us)
Async XLA Ops:
  7.2 2.5 copy-start
  7.2 260.8 %all-gather.2.cloned.1.call-start = ((), (), s32[]{:S(2)}) async-start(), calls=%async_computation.1 | async-start | bytes 5898240 | tf_op jit(solution)/shard_map/all_gather | solution.py:53
  10.9 4.6 copy-start.23
  11.2 5.2 copy-start.33
  11.3 5.2 copy-start.34
  11.3 5.2 copy-start.35
  11.3 5.2 copy-start.36
  11.3 5.3 slice-start
  11.3 5.3 slice-start.1
  11.3 5.3 copy-start.31
  12.4 4.3 copy-start.3
  12.4 4.3 copy-start.7
  12.4 4.3 copy-start.17
  113.8 537.3 %reduce-scatter.2.cloned.1.call-start = ((), (), s32[]{:S(2)}) async-start(), calls=%async_computation.2 | async-start | bytes 5898240 | tf_op jit(solution)/shard_map/reduce_scatter | solution.py:57
  115.4 3.0 copy-start.13
  122.0 139.8 %copy-start.20 = (bf16[4,80,2560]{2,1,0:T(8,128)(2,1)S(1)}, bf16[4,80,2560]{2,1,0:T(8,128)(2,1)}, u32[]{:S(2)}) copy-start(bf16[4,80,2560]{2,1,0:T(8,128)(2,1)} %copy-done.19) | copy-start | bytes 4915204
  565.3 2.9 copy-start.32
  566.8 3.1 copy-start.29
  566.8 3.1 copy-start.1
  566.8 3.2 copy-start.4
  638.1 13.0 %copy-start.21 = (f32[128,2560]{1,0:T(8,128)S(1)}, f32[128,2560]{1,0:T(8,128)}, u32[]{:S(2)}) copy-start(f32[128,2560]{1,0:T(8,128)} %get-tuple-element.84.refs_1_) | copy-start | bytes 3932164
  641.0 12.2 %copy-start.27 = (f32[128,2560]{1,0:T(8,128)S(1)}, f32[128,2560]{1,0:T(8,128)}, u32[]{:S(2)}) copy-start(f32[128,2560]{1,0:T(8,128)} %get-tuple-element.114) | copy-start | bytes 3932164
  653.2 2.5 copy-start.26
  655.7 2.3 copy-start.25
  (17 other events, 20.2 us)
Sparse Core Ops, SparseCore 0:
  113.9 78.1 all-gather.1
  564.2 86.9 reduce-scatter.1
